TPU v7x, 32 devices: a whole 2x2x4 slice. The times are simulated.
32 devices in a mesh: dp: 8 (over y, x, core), tensor: 4 (over z).
Axes of the slice: x: 2, y: 2, z: 4, core: 2. Of those that a mesh axis runs over, the one named last changes fastest.
Arguments:
- activations: bfloat16 [8192, 28672], P('dp', 'tensor'), may hold values from -6 to 6
- out_grads: bfloat16 [8192, 8192], P('dp', 'tensor'), may hold values from -6 to 6
- proj_in: bfloat16 [28672, 64], P('tensor'), may hold values from -0.03125 to 0.03125
- proj_out: bfloat16 [8192, 64], P('tensor'), may hold values from -0.0625 to 0.0625
- validation: bfloat16 [512, 4096], P('tensor', 'dp'), may hold values from -0.09375 to 0.09375
- doc_lengths: int32 [8, 32], P('dp'), may hold values from 0 to 1024, as said below
- owner_rows: int32 [8, 32], P('dp'), may hold values from 0 to 255, as said below
Outputs:
- scores: bfloat16 [256, 512], P('dp', 'tensor')
Inputs may be any that keep to these rules, and one draw needn't show every extreme that they name: `doc_lengths`: in each row the first 1 to 32 entries are positive and sum to 1024, the rest are zero; some row has 32 documents and some row a single document. `owner_rows`: A permutation of 0 to 256 - 1 over all entries; with owner = row // 32, the slots of one row go to 8 distinct owners, exactly 4 slot to each.
All inputs are finite; a program needn't handle non-finite values.
Results may differ from a plain program's by a relative error of at most 0.0098.
Values may be sent and summed in bfloat16 or wider, within the bound.
No kernel may reach another device: no remote copies, remote signals or barrier semaphores. Data moves between devices by JAX's collectives and lax.ppermute only.
A program may use at most 64 MiB of HBM per device.

v0:
```python
import jax
import jax.numpy as jnp
from jax import lax
from jax.sharding import PartitionSpec as P


def rate(sketch, validation):
    summed = lax.dot_general(
        sketch,
        lax.all_gather(validation, "dp", axis=1, tiled=True),
        (((1,), (1,)), ((), ())),
        preferred_element_type=jnp.float32,
    )
    return summed.astype(jnp.bfloat16)


def deliver(payload, out_rows, is_live):
    maxdoc = payload.shape[0]
    devices = lax.axis_size("dp")
    per_owner = max(1, maxdoc // devices)
    owners = out_rows // maxdoc
    out_slot = out_rows % maxdoc
    indices = jnp.arange(maxdoc, dtype=jnp.int32)
    same_owner = owners[None, :] == owners[:, None]
    earlier = indices[None, :] < indices[:, None]
    within = jnp.sum((same_owner & earlier).astype(jnp.int32), axis=1)
    target_pos = owners * per_owner + within
    positions = jnp.arange(devices * per_owner, dtype=jnp.int32)
    select = target_pos[None, :] == positions[:, None]
    packed = jnp.dot(
        select.astype(jnp.bfloat16), payload, preferred_element_type=jnp.float32
    ).astype(jnp.bfloat16)
    labels = (
        jnp.sum(select.astype(jnp.int32) * jnp.where(is_live, out_slot + 1, 0)[None, :], axis=1) - 1
    )
    gathered, got_labels = (
        lax.all_to_all(packed, "dp", split_axis=0, concat_axis=0, tiled=True),
        lax.all_to_all(labels, "dp", split_axis=0, concat_axis=0, tiled=True),
    )
    choose = (got_labels[None, :] == indices[:, None]).astype(jnp.bfloat16)
    return jnp.dot(choose, gathered, preferred_element_type=jnp.float32).astype(jnp.bfloat16)


def make_sketch(left_cols, grad_proj, member, scaling):
    tokens = left_cols.shape[0]
    outer_prod = (left_cols[:, :, None] * grad_proj[:, None, :]).reshape(tokens, -1)
    summed = jnp.dot(
        member, outer_prod, precision=lax.Precision.HIGHEST, preferred_element_type=jnp.float32
    )
    return (summed * scaling[:, None]).astype(jnp.bfloat16)


def shards(activations, out_grads, proj_in, proj_out, validation, doc_lengths, owner_rows):
    act_part = jnp.dot(activations, proj_in, preferred_element_type=jnp.float32)
    grad_part = jnp.dot(out_grads, proj_out, preferred_element_type=jnp.float32)
    act_proj, grad_proj = lax.psum((act_part, grad_part), "tensor")
    lengths = doc_lengths[0]
    out_rows = owner_rows[0]
    tokens = act_proj.shape[0]
    starts = jnp.cumsum(lengths) - lengths
    positions = jnp.arange(tokens, dtype=jnp.int32)
    member = (
        (positions[None, :] >= starts[:, None])
        & (positions[None, :] < starts[:, None] + lengths[:, None])
    ).astype(jnp.float32)
    scaling = 1.0 / jnp.sqrt(jnp.maximum(lengths, 1).astype(jnp.float32))
    sketch = make_sketch(act_proj, grad_proj, member, scaling)
    is_live = lengths > 0
    owned = deliver(sketch, out_rows, is_live)
    result = rate(owned, validation)
    return result


def solution(mesh):
    placed = (
        P("dp", "tensor"),
        P("dp", "tensor"),
        P("tensor", None),
        P("tensor", None),
        P("tensor", "dp"),
        P("dp", None),
        P("dp", None),
    )
    return jax.shard_map(
        shards, mesh=mesh, in_specs=placed, out_specs=P("dp", "tensor"), check_vma=False
    )
```

profile of v0, /device:TPU:0, one launch (start us, length us, event | category | flops | bytes accessed | tf_op | source)
XLA Modules:
  0.0 96.1 jit_solution(880141845566068147)
XLA Ops:
  7.4 0.0 copy-start
  7.4 0.0 all-reduce.3.cloned.1.call-start
  7.4 1.1 %copy-done = bf16[7168,64]{0,1:T(8,128)(2,1)S(1)} copy-done((bf16[7168,64]{0,1:T(8,128)(2,1)S(1)}, bf16[7168,64]{0,1:T(8,128)(2,1)}, u32[]{:S(2)}) %copy-start) | copy-done | bytes 917528
  8.5 10.6 %fusion.16 = f32[1024,64]{0,1:T(8,128)} fusion(bf16[1024,7168]{1,0:T(8,128)(2,1)} %param.7, bf16[7168,64]{0,1:T(8,128)(2,1)S(1)} %copy-done), kind=kOutput, calls=%fused_computation.40 | convolution fusion | flops 939524096 | bytes 15859712 | tf_op jit(solution)/shard_map/dot_general | solution.py:54
  19.1 0.0 copy-done.2
  19.1 0.0 copy-done.1
  19.1 2.1 %fusion.17 = f32[1024,64]{0,1:T(8,128)} fusion(bf16[1024,2048]{1,0:T(8,128)(2,1)S(1)} %copy-done.1, bf16[2048,64]{0,1:T(8,128)(2,1)S(1)} %copy-done.2), kind=kOutput, calls=%fused_computation.41 | convolution fusion | flops 268435456 | bytes 4718592 | tf_op jit(solution)/shard_map/dot_general | solution.py:55
  21.3 0.0 all-reduce.3.cloned.1.call-update
  21.3 0.0 copy-done.4
  21.3 0.2 convert_reduce_fusion
  21.5 0.1 select_reduce_fusion
  21.6 0.7 sub.24
  22.3 5.2 %all-to-all-start = ((s32[8,4,1]{1,2,0:T(1,128)}), s32[8,4,1]{1,2,0:T(1,128)S(1)}, u32[]{:S(2)}, u32[]{:S(2)}) async-start(s32[8,4,1]{1,2,0:T(1,128)} %bitcast.5), calls=%async_computation | async-start | bytes 8192 | tf_op jit(solution)/shard_map/all_to_all | solution.py:38
  27.5 0.2 all-gather.2.cloned.1.call-start
  27.8 0.3 all-gather.2.cloned.1.call-update
  28.1 0.1 copy.15
  28.2 0.1 reduce-window.7
  28.3 0.1 reduce.1
  28.4 34.6 %all-reduce.3.cloned.1.call-done = (f32[1024,64]{0,1:T(8,128)}, f32[1024,64]{0,1:T(8,128)}) async-done(((f32[1024,64]{0,1:T(8,128)}, f32[1024,64]{0,1:T(8,128)}), (f32[1024,64]{0,1:T(8,128)}, f32[1024,64]{0,1:T(8,128)})) %all-reduce.3.cloned.1.call-update) | async-done | bytes 524304 | tf_op jit(solution)/shard_map/psum | solution.py:56
  62.9 3.2 %broadcast_multiply_fusion = f32[1024,64,64]{0,2,1:T(8,128)S(1)} fusion(f32[1024,64]{0,1:T(8,128)} %get-tuple-element.5, f32[1024,64]{0,1:T(8,128)} %get-tuple-element.6), kind=kLoop, calls=%fused_computation | loop fusion | flops 4194304 | bytes 17301504 | tf_op jit(solution)/shard_map/mul | solution.py:46
  66.2 8.5 %fusion = bf16[32,4096]{1,0:T(8,128)(2,1)S(1)} fusion(f32[1024,4096]{0,1:T(8,128)S(1)} %bitcast.36, f32[32]{0:T(128)S(1)} %fusion.14, s32[32]{0:T(128)S(1)} %reduce.1, s32[32]{0:T(128)S(1)} %bitcast_subtract_fusion), kind=kOutput, calls=%fused_computation.2 | convolution fusion | flops 1610973184 | bytes 17039744 | tf_op jit(solution)/shard_map/dot_general | solution.py:47
  74.7 0.2 convolution_convert_fusion.1
  74.9 0.8 all_to_all.13
  75.7 0.0 all-to-all-done
  75.7 3.6 %all-to-all-start.1 = ((bf16[8,4,4096]{2,1,0:T(4,128)(2,1)}), bf16[8,4,4096]{2,1,0:T(4,128)(2,1)S(1)}, u32[]{:S(2)}, u32[]{:S(2)}) async-start(bf16[8,4,4096]{2,1,0:T(4,128)(2,1)} %all_to_all.13), calls=%async_computation.1 | async-start | bytes 524288 | tf_op jit(solution)/shard_map/all_to_all | solution.py:37
  79.3 0.5 broadcast.113
  79.8 0.7 reduce.4
  80.4 0.1 eq.50
  80.5 5.6 %all-to-all-done.1 = bf16[8,4,4096]{2,1,0:T(4,128)(2,1)S(1)} async-done(((bf16[8,4,4096]{2,1,0:T(4,128)(2,1)}), bf16[8,4,4096]{2,1,0:T(4,128)(2,1)S(1)}, u32[]{:S(2)}, u32[]{:S(2)}) %all-to-all-start.1) | async-done | bytes 262176 | tf_op jit(solution)/shard_map/all_to_all | solution.py:37
  86.2 0.1 all_to_all.15
  86.2 0.0 all-gather.2.cloned.1.call-done
  86.3 2.4 %fusion.2 = bf16[32,128]{1,0:T(8,128)(2,1)} fusion(bf16[128,4096]{1,0:T(8,128)(2,1)} %all-gather.2.cloned.1.call-done, bf16[32,4096]{1,0:T(8,128)(2,1)S(1)} %all_to_all.15, s32[32]{0:T(128)S(1)} %eq.50), kind=kOutput, calls=%fused_computation.6 | convolution fusion | flops 42079232 | bytes 1319040 | tf_op jit(solution)/shard_map/dot_general | solution.py:8
  (11 shorter events, 0.1 us)
Async XLA Ops:
  7.4 1.2 %copy-start = (bf16[7168,64]{0,1:T(8,128)(2,1)S(1)}, bf16[7168,64]{0,1:T(8,128)(2,1)}, u32[]{:S(2)}) copy-start(bf16[7168,64]{0,1:T(8,128)(2,1)} %param.9) | copy-start | bytes 2752516
  7.4 11.8 %copy-start.2 = (bf16[2048,64]{0,1:T(8,128)(2,1)S(1)}, bf16[2048,64]{0,1:T(8,128)(2,1)}, u32[]{:S(2)}) copy-start(bf16[2048,64]{0,1:T(8,128)(2,1)} %param.10) | copy-start | bytes 786436
  7.4 13.9 %copy-start.4 = (s32[1,32]{1,0:T(1,128)S(1)}, s32[1,32]{1,0:T(1,128)}, u32[]{:S(2)}) copy-start(s32[1,32]{1,0:T(1,128)} %param.13) | copy-start | bytes 388
  7.4 13.9 %copy-start.3 = (s32[1,32]{1,0:T(1,128)S(1)}, s32[1,32]{1,0:T(1,128)}, u32[]{:S(2)}) copy-start(s32[1,32]{1,0:T(1,128)} %param.12) | copy-start | bytes 388
  7.4 55.6 %all-reduce.3.cloned.1.call-start = ((), (), s32[]{:S(2)}) async-start(), calls=%async_computation.3 | async-start | bytes 1048576 | tf_op jit(solution)/shard_map/psum | solution.py:56
  8.5 10.6 %copy-start.1 = (bf16[1024,2048]{1,0:T(8,128)(2,1)S(1)}, bf16[1024,2048]{1,0:T(8,128)(2,1)}, u32[]{:S(2)}) copy-start(bf16[1024,2048]{1,0:T(8,128)(2,1)} %param.8) | copy-start | bytes 12582916
  22.3 53.4 %all-to-all-start = ((s32[8,4,1]{1,2,0:T(1,128)}), s32[8,4,1]{1,2,0:T(1,128)S(1)}, u32[]{:S(2)}, u32[]{:S(2)}) async-start(s32[8,4,1]{1,2,0:T(1,128)} %bitcast.5), calls=%async_computation | async-start | bytes 8192 | tf_op jit(solution)/shard_map/all_to_all | solution.py:38
  27.5 58.7 %all-gather.2.cloned.1.call-start = ((), (), s32[]{:S(2)}) async-start(), calls=%async_computation.2 | async-start | bytes 1179648 | tf_op jit(solution)/shard_map/all_gather | solution.py:10
  75.7 10.5 %all-to-all-start.1 = ((bf16[8,4,4096]{2,1,0:T(4,128)(2,1)}), bf16[8,4,4096]{2,1,0:T(4,128)(2,1)S(1)}, u32[]{:S(2)}, u32[]{:S(2)}) async-start(bf16[8,4,4096]{2,1,0:T(4,128)(2,1)} %all_to_all.13), calls=%async_computation.1 | async-start | bytes 524288 | tf_op jit(solution)/shard_map/all_to_all | solution.py:37
Sparse Core Ops, SparseCore 0:
  21.4 41.4 all-reduce.2
Sparse Core Ops, SparseCore 1:
  29.9 25.0 all-gather.1
where the time goes:
time: 96.5 us; the launch traced here: 96.1 us
  waiting for transfers between devices  40.6 us (42%)
  matrix products  23.8 us (25%)
  between operations  14.9 us (15%)
  starting transfers between devices  9.03 us (9%)
  other arithmetic  4.39 us (5%)
  local copies, waits for them, and re-layouts  3.39 us (4%)
    psum x1, waiting for transfers between devices, shards(): act_proj, grad_proj = lax.psum((act_part, grad_part), 'tensor')  34.6 us
    dot_general x1, matrix products, shards(): act_part = jnp.dot(activations, proj_in, preferred_element_type=jnp.float32)  10.6 us
    dot_general x1, matrix products, make_sketch(): jnp.dot(member, outer_prod, precision=lax.Precision.HIGHEST, preferred_el...  8.48 us
    all_to_all x1, waiting for transfers between devices, deliver(): lax.all_to_all(packed, 'dp', split_axis=0, concat_axis=0, tiled=True)  5.65 us
    all_to_all x1, starting transfers between devices, deliver(): lax.all_to_all(labels, 'dp', split_axis=0, concat_axis=0, tiled=True)  5.2 us
    all_to_all x1, starting transfers between devices, deliver(): lax.all_to_all(packed, 'dp', split_axis=0, concat_axis=0, tiled=True)  3.58 us
    mul x1, other arithmetic, make_sketch(): left_cols[:, :, None] * grad_proj[:, None, :]  3.22 us
    dot_general x1, matrix products, rate(): lax.dot_general(sketch, lax.all_gather(validation, 'dp', axis=1, tiled=Tr...  2.42 us
  transfers between devices with their start and end apart: 4, of which 2 were waited for; matrix products, arithmetic and copies ran while one was open for 15% of the time, Pallas kernels for 0%

commit v1 on v0

v1 whole, which is shorter than its diff:
```python
import functools

import jax
import jax.numpy as jnp
from jax import lax
from jax.experimental import pallas as pl
from jax.experimental.pallas import tpu as pltpu
from jax.sharding import PartitionSpec as P

BF16, F32 = jnp.bfloat16, jnp.float32
NT = (((1,), (1,)), ((), ()))
VMEM_LIMIT = 48 << 20


def swap(x, axis, k):
    return lax.ppermute(x, axis, [(i, i ^ k) for i in range(lax.axis_size(axis))])


def project_kernel(steps, chunk_ref, act_ref, grad_ref, wa_ref, wg_ref, out_ref, acc_a, acc_g):
    step = pl.program_id(0)

    @pl.when(step == 0)
    def _():
        acc_a[...] = jnp.zeros_like(acc_a)
        acc_g[...] = jnp.zeros_like(acc_g)

    ka, kg = act_ref.shape[1], grad_ref.shape[1]
    wa = wa_ref[:, pl.ds(pl.multiple_of(step * ka, 128), ka)]
    wg = wg_ref[:, pl.ds(pl.multiple_of(step * kg, 128), kg)]
    acc_a[...] += lax.dot_general(act_ref[...], wa, NT, preferred_element_type=F32)
    acc_g[...] += lax.dot_general(grad_ref[...], wg, NT, preferred_element_type=F32)

    @pl.when(step == steps - 1)
    def _():
        out_ref[...] = jnp.concatenate([acc_a[...], acc_g[...]], axis=1).astype(out_ref.dtype)


def project(chunk, activations, out_grads, wa, wg, rows, steps, name):
    ff, d = activations.shape[1], out_grads.shape[1]
    k = wa.shape[0]
    return pl.pallas_call(
        functools.partial(project_kernel, steps),
        out_shape=jax.ShapeDtypeStruct((rows, 2 * k), BF16),
        grid_spec=pltpu.PrefetchScalarGridSpec(
            num_scalar_prefetch=1,
            grid=(steps,),
            in_specs=[
                pl.BlockSpec((rows, ff // steps), lambda i, c: (c[0], i)),
                pl.BlockSpec((rows, d // steps), lambda i, c: (c[0], i)),
                pl.BlockSpec(memory_space=pltpu.VMEM),
                pl.BlockSpec(memory_space=pltpu.VMEM),
            ],
            out_specs=pl.BlockSpec((rows, 2 * k), lambda i, c: (0, 0)),
            scratch_shapes=[pltpu.VMEM((rows, k), F32), pltpu.VMEM((rows, k), F32)],
        ),
        compiler_params=pltpu.CompilerParams(vmem_limit_bytes=VMEM_LIMIT),
        cost_estimate=pl.CostEstimate(
            flops=2 * rows * (ff + d) * k, bytes_accessed=2 * rows * (ff + d), transcendentals=0
        ),
        name=name,
    )(chunk, activations, out_grads, wa, wg)


def score_kernel(n_chunks, n_blocks, group, place_ref, bounds_ref, scale_ref, select_ref, labels_ref, *refs):
    chunks, blocks = refs[:n_chunks], refs[n_chunks : n_chunks + n_blocks]
    out_ref, left, right, member, sketch = refs[n_chunks + n_blocks :]
    rows, k = chunks[0].shape[0], chunks[0].shape[1] // 2
    docs = bounds_ref.shape[1]
    for c, ref in enumerate(chunks):
        turned = ref[...].astype(F32).T.astype(BF16)
        left[:, c * rows : (c + 1) * rows] = turned[:k].astype(F32)
        right[:, c * rows : (c + 1) * rows] = turned[k:]
        at = place_ref[c] * rows + lax.broadcasted_iota(jnp.int32, (rows, docs), 0)
        inside = (at >= bounds_ref[0:1, :]) & (at < bounds_ref[1:2, :])
        member[c * rows : (c + 1) * rows, :] = inside.astype(F32).astype(BF16)
    grads = right[...]
    for i in range(0, k, group):
        outer = jnp.concatenate(
            [left[j : j + 1, :].astype(BF16) * grads for j in range(i, i + group)], axis=0
        )
        summed = jnp.dot(outer, member[...], preferred_element_type=F32)
        sketch[i * k : (i + group) * k, :] = (summed * scale_ref[...]).astype(BF16)
    wide = blocks[0].shape[1]
    local = jnp.zeros((blocks[0].shape[0], docs), F32)
    for b, ref in enumerate(blocks):
        start = pl.multiple_of(place_ref[n_chunks + b] * wide, wide)
        local += jnp.dot(ref[...], sketch[pl.ds(start, wide), :], preferred_element_type=F32)
    packed = lax.dot_general(select_ref[...], local.astype(BF16), NT, preferred_element_type=F32)
    out_ref[...] = (packed + labels_ref[...]).astype(BF16)


def score(place, bounds, scaling, select, labels, chunks, blocks):
    tokens = len(chunks) * chunks[0].shape[0]
    k = chunks[0].shape[1] // 2
    docs = bounds.shape[1]
    group = 8
    vmem = pl.BlockSpec(memory_space=pltpu.VMEM)
    nval = blocks[0].shape[0]
    return pl.pallas_call(
        functools.partial(score_kernel, len(chunks), len(blocks), group),
        out_shape=jax.ShapeDtypeStruct((select.shape[0], nval), BF16),
        in_specs=[pl.BlockSpec(memory_space=pltpu.SMEM)] + [vmem] * (4 + len(chunks) + len(blocks)),
        out_specs=vmem,
        scratch_shapes=[
            pltpu.VMEM((k, tokens), F32),
            pltpu.VMEM((k, tokens), BF16),
            pltpu.VMEM((tokens, docs), BF16),
            pltpu.VMEM((k * k, docs), BF16),
        ],
        compiler_params=pltpu.CompilerParams(vmem_limit_bytes=VMEM_LIMIT),
        cost_estimate=pl.CostEstimate(
            flops=2 * k * k * docs * (tokens + nval), bytes_accessed=2 * k * k * nval, transcendentals=0
        ),
        name="score",
    )(place, bounds, scaling, select, labels, *chunks, *blocks)


def shards(activations, out_grads, proj_in, proj_out, validation, doc_lengths, owner_rows):
    devices, parts = lax.axis_size("dp"), lax.axis_size("tensor")
    me, part = lax.axis_index("dp"), lax.axis_index("tensor")
    tokens, maxdoc = activations.shape[0], doc_lengths.shape[1]
    rows = tokens // parts

    half = [validation] + [swap(validation, "dp", b) for b in range(2, devices, 2)]
    other = swap(jnp.concatenate(half, axis=0), "dp", 1)
    nval = validation.shape[0]
    blocks = []
    for b in range(devices // 2):
        blocks += [half[b], other[b * nval : (b + 1) * nval]]

    wa, wg = proj_in.T, proj_out.T
    got, own = [], None
    for peer in list(range(parts - 1, 0, -1)) + [0]:
        partial = project(
            jnp.array([0], jnp.int32) + (part ^ peer), activations, out_grads, wa, wg, rows, 4, f"project{peer}"
        )
        if peer:
            got.append(swap(partial, "tensor", peer))
        else:
            own = partial
    total = own.astype(F32)
    for piece in got:
        total = total + piece.astype(F32)
    mine = total.astype(BF16)
    chunks = [mine] + [swap(mine, "tensor", peer) for peer in range(1, parts)]

    lengths, out_rows = doc_lengths[0], owner_rows[0]
    indices = jnp.arange(maxdoc, dtype=jnp.int32)
    starts = jnp.sum(jnp.where(indices[:, None] < indices[None, :], lengths[:, None], 0), axis=0)
    bounds = jnp.stack([starts, starts + lengths])
    scaling = (1.0 / jnp.sqrt(jnp.maximum(lengths, 1).astype(F32)))[None, :]

    per_owner = max(1, maxdoc // devices)
    height = -(-2 * per_owner // 8) * 8
    owners, out_slot = out_rows // maxdoc, out_rows % maxdoc
    earlier = (owners[None, :] == owners[:, None]) & (indices[None, :] < indices[:, None])
    target = owners * height + jnp.sum(earlier.astype(jnp.int32), axis=1)
    at = jnp.arange(devices * height, dtype=jnp.int32)
    select = (target[None, :] == at[:, None]).astype(BF16)
    label = jnp.where(lengths > 0, out_slot, -1)
    labels = jnp.sum(jnp.where(target[None, :] + per_owner == at[:, None], label[None, :], 0), axis=1)
    labels = jnp.broadcast_to(labels.astype(F32)[:, None], (devices * height, nval))

    place = jnp.concatenate(
        [part ^ jnp.arange(parts, dtype=jnp.int32), me ^ jnp.arange(devices, dtype=jnp.int32)]
    )
    payload = score(place, bounds, scaling, select, labels, chunks, blocks)
    got_rows = lax.all_to_all(
        payload.reshape(devices, height, nval), "dp", split_axis=0, concat_axis=0, tiled=True
    )
    data = got_rows[:, :per_owner].reshape(devices * per_owner, nval)
    tags = got_rows[:, per_owner : 2 * per_owner, :maxdoc].reshape(devices * per_owner, maxdoc)
    choose = (tags.astype(F32) == indices.astype(F32)[None, :]).astype(BF16)
    return lax.dot_general(
        choose, data, (((0,), (0,)), ((), ())), preferred_element_type=F32
    ).astype(BF16)


def solution(mesh):
    placed = (
        P("dp", "tensor"),
        P("dp", "tensor"),
        P("tensor", None),
        P("tensor", None),
        P("tensor", "dp"),
        P("dp", None),
        P("dp", None),
    )
    return jax.shard_map(
        shards, mesh=mesh, in_specs=placed, out_specs=P("dp", "tensor"), check_vma=False
    )
```

time: 96.5 us -> 59.5 us (0.62)
  waiting for transfers between devices: 40.6 us -> 10.8 us
  matrix products: 23.8 us -> 0.8 us
  Pallas kernels: 0 us -> 20.2 us
  between operations: 14.9 us -> 0.2 us
  starting transfers between devices: 9.03 us -> 17.6 us
  local copies, waits for them, and re-layouts: 3.39 us -> 8.82 us
  other arithmetic: 4.39 us -> 0.58 us
    psum x1 -> x0, waiting for transfers between devices: 34.6 us -> none  [shards(): act_proj, grad_proj = lax.psum((act_part, grad_part), 'tensor')]
    dot_general x5 -> x1, matrix products: 23.8 us -> 0.8 us  [shards(): lax.dot_general(choose, data, (((0,), (0,)), ((), ())), preferred_element...]
    pallas_call x0 -> x5, Pallas kernels: none -> 20.2 us  [the longest x4 16 us: project(): pl.pallas_call(functools.partial(project_kernel, steps), out_shape=jax.Sh...]
    ppermute x0 -> x10, starting transfers between devices: none -> 13.9 us  [swap(): lax.ppermute(x, axis, [(i, i ^ k) for i in range(lax.axis_size(axis))])]
    unnamed x10 -> x20, local copies, waits for them, and re-layouts: 1.15 us -> 8.71 us
    ppermute x0 -> x10, waiting for transfers between devices: none -> 6.02 us  [swap(): lax.ppermute(x, axis, [(i, i ^ k) for i in range(lax.axis_size(axis))])]
    all_to_all x2 -> x1, starting transfers between devices: 8.78 us -> 3.72 us  [shards(): lax.all_to_all(payload.reshape(devices, height, nval), 'dp', split_axis=0...]
    mul x2 -> x0, other arithmetic: 3.23 us -> none  [the longest x1 3.22 us: make_sketch(): left_cols[:, :, None] * grad_proj[:, None, :]]
  transfers between devices with their start and end apart: 4 -> 11, of which waited for: 2 -> 5; matrix products, arithmetic and copies ran while one was open for 15% -> 1% of each run, Pallas kernels for 0% -> 27%
where the time goes in v1:
time: 59.5 us; the launch traced here: 58.9 us
  Pallas kernels  20.2 us (34%)
  starting transfers between devices  17.6 us (30%)
  waiting for transfers between devices  10.8 us (18%)
  local copies, waits for them, and re-layouts  8.82 us (15%)
  matrix products  0.8 us (1%)
    pallas_call x4, Pallas kernels, project(): pl.pallas_call(functools.partial(project_kernel, steps), out_shape=jax.Sh...  16 us
    ppermute x10, starting transfers between devices, swap(): lax.ppermute(x, axis, [(i, i ^ k) for i in range(lax.axis_size(axis))])  13.9 us
    unnamed x20, local copies, waits for them, and re-layouts  8.71 us
    ppermute x10, waiting for transfers between devices, swap(): lax.ppermute(x, axis, [(i, i ^ k) for i in range(lax.axis_size(axis))])  6.02 us
    all_to_all x1, waiting for transfers between devices, shards(): lax.all_to_all(payload.reshape(devices, height, nval), 'dp', split_axis=0...  4.75 us
    pallas_call x1, Pallas kernels, score(): pl.pallas_call(functools.partial(score_kernel, len(chunks), len(blocks),...  4.17 us
    all_to_all x1, starting transfers between devices, shards(): lax.all_to_all(payload.reshape(devices, height, nval), 'dp', split_axis=0...  3.72 us
  transfers between devices with their start and end apart: 11, of which 5 were waited for; matrix products, arithmetic and copies ran while one was open for 1% of the time, Pallas kernels for 27%

profile of v1, /device:TPU:0, one launch (start us, length us, event | category | flops | bytes accessed | tf_op | source)
XLA Modules:
  0.0 58.9 jit_solution(15020499968031727221)
XLA Ops:
  0.0 3.9 %collective-permute-start.8 = (bf16[128,512]{1,0:T(8,128)(2,1)}, bf16[128,512]{1,0:T(8,128)(2,1)S(1)}, u32[]{:S(2)}, u32[]{:S(2)}) collective-permute-start(bf16[128,512]{1,0:T(8,128)(2,1)} %refs_4_.1), channel_id=1, source_target_pairs={{0,24},{4,28},{8,16},{12,20},{16,8},{20,12},{24,0},{28,4},{1,25},{... | collective-permute-start | bytes 393224 | tf_op jit(solution)/shard_map/ppermute | solution.py:16
  3.9 0.5 collective-permute-start.7
  4.4 0.1 collective-permute-start.6
  4.5 2.2 %copy-done = bf16[1024,2048]{1,0:T(8,128)(2,1)S(1)} copy-done((bf16[1024,2048]{1,0:T(8,128)(2,1)S(1)}, bf16[1024,2048]{1,0:T(8,128)(2,1)}, u32[]{:S(2)}) %copy-start) | copy-done | bytes 4194328
  6.7 1.2 %copy-done.3 = bf16[7168,64]{0,1:T(8,128)(2,1)S(1)} copy-done((bf16[7168,64]{0,1:T(8,128)(2,1)S(1)}, bf16[7168,64]{0,1:T(8,128)(2,1)}, u32[]{:S(2)}) %copy-start.3) | copy-done | bytes 917528
  7.9 0.9 %copy-done.5 = bf16[2048,64]{0,1:T(8,128)(2,1)S(1)} copy-done((bf16[2048,64]{0,1:T(8,128)(2,1)S(1)}, bf16[2048,64]{0,1:T(8,128)(2,1)}, u32[]{:S(2)}) %copy-start.5) | copy-done | bytes 262168
  8.8 4.1 %project1.1 = bf16[256,128]{1,0:T(8,128)(2,1)S(1)} custom-call(s32[1]{0:T(128)} %bitcast.13.chunk_ref, bf16[1024,7168]{1,0:T(8,128)(2,1)} %act_ref.7, bf16[1024,2048]{1,0:T(8,128)(2,1)S(1)} %copy-done, bf16[64,7168]{1,0:T(8,128)(2,1)S(1)} %bitcast.35, bf16[64,2048]{1,0:T(8,128)(2,1)S(1)} %bitcast.39), custom_call_target="tpu_custom_call" | custom-call | flops 301989888 | bytes 4718592 | tf_op jit(solution)/shard_map/project1/pallas_call | solution.py:41
  12.9 2.1 %collective-permute-start.2 = (bf16[256,128]{1,0:T(8,128)(2,1)S(1)}, bf16[256,128]{1,0:T(8,128)(2,1)S(1)}, u32[]{:S(2)}, u32[]{:S(2)}) collective-permute-start(bf16[256,128]{1,0:T(8,128)(2,1)S(1)} %project1.1), channel_id=1, source_target_pairs={{0,1},{1,0},{2,3},{3,2},{4,5},{5,4},{6,7},{7,6},{8,9},{9,8},{10,11... | collective-permute-start | bytes 196616 | tf_op jit(solution)/shard_map/ppermute | solution.py:16
  15.0 2.2 %copy-done.1 = bf16[1024,2048]{1,0:T(8,128)(2,1)S(1)} copy-done((bf16[1024,2048]{1,0:T(8,128)(2,1)S(1)}, bf16[1024,2048]{1,0:T(8,128)(2,1)}, u32[]{:S(2)}) %copy-start.1) | copy-done | bytes 4194328
  17.2 4.0 %project2.1 = bf16[256,128]{1,0:T(8,128)(2,1)S(1)} custom-call(s32[1]{0:T(128)} %bitcast.12.chunk_ref, bf16[1024,7168]{1,0:T(8,128)(2,1)} %act_ref.7, bf16[1024,2048]{1,0:T(8,128)(2,1)S(1)} %copy-done.1, bf16[64,7168]{1,0:T(8,128)(2,1)S(1)} %bitcast.36, bf16[64,2048]{1,0:T(8,128)(2,1)S(1)} %bitcast.40), custom_call_target="tpu_custom_call" | custom-call | flops 301989888 | bytes 4718592 | tf_op jit(solution)/shard_map/project2/pallas_call | solution.py:41
  21.2 2.7 %collective-permute-start.1 = (bf16[256,128]{1,0:T(8,128)(2,1)S(1)}, bf16[256,128]{1,0:T(8,128)(2,1)S(1)}, u32[]{:S(2)}, u32[]{:S(2)}) collective-permute-start(bf16[256,128]{1,0:T(8,128)(2,1)S(1)} %project2.1), channel_id=1, source_target_pairs={{0,2},{1,3},{2,0},{3,1},{4,6},{5,7},{6,4},{7,5},{8,10},{9,11},{10,... | collective-permute-start | bytes 196616 | tf_op jit(solution)/shard_map/ppermute | solution.py:16
  23.9 0.1 select_reduce_fusion.1
  24.0 0.2 convert_reduce_fusion
  24.3 2.2 %copy-done.2 = bf16[1024,2048]{1,0:T(8,128)(2,1)S(1)} copy-done((bf16[1024,2048]{1,0:T(8,128)(2,1)S(1)}, bf16[1024,2048]{1,0:T(8,128)(2,1)}, u32[]{:S(2)}) %copy-start.2) | copy-done | bytes 4194328
  26.4 4.0 %project3.1 = bf16[256,128]{1,0:T(8,128)(2,1)S(1)} custom-call(s32[1]{0:T(128)} %bitcast.11.chunk_ref, bf16[1024,7168]{1,0:T(8,128)(2,1)} %act_ref.7, bf16[1024,2048]{1,0:T(8,128)(2,1)S(1)} %copy-done.2, bf16[64,7168]{1,0:T(8,128)(2,1)S(1)} %bitcast.37, bf16[64,2048]{1,0:T(8,128)(2,1)S(1)} %bitcast.41), custom_call_target="tpu_custom_call" | custom-call | flops 301989888 | bytes 4718592 | tf_op jit(solution)/shard_map/project3/pallas_call | solution.py:41
  30.5 0.1 collective-permute-start
  30.6 0.1 collective-permute-start.9
  30.7 0.1 select_reduce_fusion
  30.8 0.1 pad_add_fusion.1.place_ref
  30.9 4.0 %project0.1 = bf16[256,128]{1,0:T(8,128)(2,1)S(1)} custom-call(s32[1]{0:T(128)} %bitcast.8.chunk_ref, bf16[1024,7168]{1,0:T(8,128)(2,1)} %act_ref.7, bf16[1024,2048]{1,0:T(8,128)(2,1)S(1)} %copy-done.2, bf16[64,7168]{1,0:T(8,128)(2,1)S(1)} %bitcast.38, bf16[64,2048]{1,0:T(8,128)(2,1)S(1)} %bitcast.42), custom_call_target="tpu_custom_call" | custom-call | flops 301989888 | bytes 4718592 | tf_op jit(solution)/shard_map/project0/pallas_call | solution.py:41
  34.9 1.7 %collective-permute-done = bf16[256,128]{1,0:T(8,128)(2,1)S(1)} collective-permute-done((bf16[256,128]{1,0:T(8,128)(2,1)S(1)}, bf16[256,128]{1,0:T(8,128)(2,1)S(1)}, u32[]{:S(2)}, u32[]{:S(2)}) %collective-permute-start) | collective-permute-done | bytes 65568 | tf_op jit(solution)/shard_map/ppermute | solution.py:16
  36.6 0.1 collective-permute-start.3
  36.7 2.6 %collective-permute-start.4 = (bf16[256,128]{1,0:T(8,128)(2,1)S(1)}, bf16[256,128]{1,0:T(8,128)(2,1)S(1)}, u32[]{:S(2)}, u32[]{:S(2)}) collective-permute-start(bf16[256,128]{1,0:T(8,128)(2,1)S(1)} %add_convert_fusion.refs_0_), channel_id=1, source_target_pairs={{0,2},{1,3},{2,0},{3,1},{4,6},{5,7},{6,4},{7,5},{8,10},{9,11},{10,... | collective-permute-start | bytes 196616 | tf_op jit(solution)/shard_map/ppermute | solution.py:16
  39.3 1.7 %collective-permute-start.5 = (bf16[256,128]{1,0:T(8,128)(2,1)S(1)}, bf16[256,128]{1,0:T(8,128)(2,1)S(1)}, u32[]{:S(2)}, u32[]{:S(2)}) collective-permute-start(bf16[256,128]{1,0:T(8,128)(2,1)S(1)} %add_convert_fusion.refs_0_), channel_id=1, source_target_pairs={{0,3},{1,2},{2,1},{3,0},{4,7},{5,6},{6,5},{7,4},{8,11},{9,10},{10,... | collective-permute-start | bytes 196616 | tf_op jit(solution)/shard_map/ppermute | solution.py:16
  41.1 0.9 %collective-permute-done.3.refs_1_ = bf16[256,128]{1,0:T(8,128)(2,1)S(1)} collective-permute-done((bf16[256,128]{1,0:T(8,128)(2,1)S(1)}, bf16[256,128]{1,0:T(8,128)(2,1)S(1)}, u32[]{:S(2)}, u32[]{:S(2)}) %collective-permute-start.3) | collective-permute-done | bytes 65568 | tf_op jit(solution)/shard_map/ppermute | solution.py:16
  42.0 2.5 %collective-permute-done.4.refs_2_ = bf16[256,128]{1,0:T(8,128)(2,1)S(1)} collective-permute-done((bf16[256,128]{1,0:T(8,128)(2,1)S(1)}, bf16[256,128]{1,0:T(8,128)(2,1)S(1)}, u32[]{:S(2)}, u32[]{:S(2)}) %collective-permute-start.4) | collective-permute-done | bytes 65568 | tf_op jit(solution)/shard_map/ppermute | solution.py:16
  44.5 0.9 %collective-permute-done.5.refs_3_ = bf16[256,128]{1,0:T(8,128)(2,1)S(1)} collective-permute-done((bf16[256,128]{1,0:T(8,128)(2,1)S(1)}, bf16[256,128]{1,0:T(8,128)(2,1)S(1)}, u32[]{:S(2)}, u32[]{:S(2)}) %collective-permute-start.5) | collective-permute-done | bytes 65568 | tf_op jit(solution)/shard_map/ppermute | solution.py:16
  45.4 0.1 broadcast_in_dim.55.labels_ref
  45.5 4.2 %score.1 = bf16[64,128]{1,0:T(8,128)(2,1)} custom-call(s32[12]{0:T(128)S(1)} %pad_add_fusion.1.place_ref, s32[2,32]{1,0:T(2,128)S(1)} %pad_add_fusion.bounds_ref, f32[1,32]{1,0:T(1,128)S(1)} %convert_rsqrt_fusion.scale_ref, bf16[64,32]{1,0:T(8,128)(2,1)S(1)} %fusion.1.select_ref, f32[64,128]{1,0:T(8,128)S(1)} %broadcast_in_dim.55.labels_ref, ...), custom_call_target="tpu_custom_call" | custom-call | flops 301989888 | bytes 1048576 | tf_op jit(solution)/shard_map/score/pallas_call | solution.py:99
  49.7 3.7 %all-to-all-start = ((bf16[8,8,128]{2,1,0:T(8,128)(2,1)}), bf16[8,8,128]{2,1,0:T(8,128)(2,1)S(1)}, u32[]{:S(2)}, u32[]{:S(2)}) async-start(bf16[8,8,128]{2,1,0:T(8,128)(2,1)} %bitcast.14), calls=%async_computation | async-start | bytes 32768 | tf_op jit(solution)/shard_map/all_to_all | solution.py:168
  53.4 4.7 %all-to-all-done = bf16[8,8,128]{2,1,0:T(8,128)(2,1)S(1)} async-done(((bf16[8,8,128]{2,1,0:T(8,128)(2,1)}), bf16[8,8,128]{2,1,0:T(8,128)(2,1)S(1)}, u32[]{:S(2)}, u32[]{:S(2)}) %all-to-all-start) | async-done | bytes 16416 | tf_op jit(solution)/shard_map/all_to_all | solution.py:168
  58.1 0.8 %fusion = bf16[32,128]{1,0:T(8,128)(2,1)} fusion(bf16[8,8,128]{2,1,0:T(8,128)(2,1)S(1)} %all-to-all-done, f32[32]{0:T(128)S(1)} %iota_convert_fusion), kind=kOutput, calls=%fused_computation.1 | convolution fusion | flops 268288 | bytes 24704 | tf_op jit(solution)/shard_map/dot_general | solution.py:174
  (34 shorter events, 0.2 us)
Async XLA Ops:
  0.0 30.4 %collective-permute-start.8 = (bf16[128,512]{1,0:T(8,128)(2,1)}, bf16[128,512]{1,0:T(8,128)(2,1)S(1)}, u32[]{:S(2)}, u32[]{:S(2)}) collective-permute-start(bf16[128,512]{1,0:T(8,128)(2,1)} %refs_4_.1), channel_id=1, source_target_pairs={{0,24},{4,28},{8,16},{12,20},{16,8},{20,12},{24,0},{28,4},{1,25},{... | collective-permute-start | bytes 393224 | tf_op jit(solution)/shard_map/ppermute | solution.py:16
  3.9 26.6 %collective-permute-start.7 = (bf16[128,512]{1,0:T(8,128)(2,1)}, bf16[128,512]{1,0:T(8,128)(2,1)S(1)}, u32[]{:S(2)}, u32[]{:S(2)}) collective-permute-start(bf16[128,512]{1,0:T(8,128)(2,1)} %refs_4_.1), channel_id=1, source_target_pairs={{0,16},{4,20},{8,24},{12,28},{16,0},{20,4},{24,8},{28,12},{1,17},{... | collective-permute-start | bytes 393224 | tf_op jit(solution)/shard_map/ppermute | solution.py:16
  4.4 26.1 %collective-permute-start.6 = (bf16[128,512]{1,0:T(8,128)(2,1)}, bf16[128,512]{1,0:T(8,128)(2,1)S(1)}, u32[]{:S(2)}, u32[]{:S(2)}) collective-permute-start(bf16[128,512]{1,0:T(8,128)(2,1)} %refs_4_.1), channel_id=1, source_target_pairs={{0,8},{4,12},{8,0},{12,4},{16,24},{20,28},{24,16},{28,20},{1,9},{5... | collective-permute-start | bytes 393224 | tf_op jit(solution)/shard_map/ppermute | solution.py:16
  4.5 2.2 %copy-start = (bf16[1024,2048]{1,0:T(8,128)(2,1)S(1)}, bf16[1024,2048]{1,0:T(8,128)(2,1)}, u32[]{:S(2)}) copy-start(bf16[1024,2048]{1,0:T(8,128)(2,1)} %grad_ref.7) | copy-start | bytes 12582916
  6.7 1.2 %copy-start.3 = (bf16[7168,64]{0,1:T(8,128)(2,1)S(1)}, bf16[7168,64]{0,1:T(8,128)(2,1)}, u32[]{:S(2)}) copy-start(bf16[7168,64]{0,1:T(8,128)(2,1)} %param.13) | copy-start | bytes 2752516
  7.9 0.9 %copy-start.5 = (bf16[2048,64]{0,1:T(8,128)(2,1)S(1)}, bf16[2048,64]{0,1:T(8,128)(2,1)}, u32[]{:S(2)}) copy-start(bf16[2048,64]{0,1:T(8,128)(2,1)} %param.14) | copy-start | bytes 786436
  8.8 6.2 %copy-start.4 = (bf16[7168,64]{0,1:T(8,128)(2,1)S(1)}, bf16[7168,64]{0,1:T(8,128)(2,1)}, u32[]{:S(2)}) copy-start(bf16[7168,64]{0,1:T(8,128)(2,1)} %param.13) | copy-start | bytes 2752516
  8.8 6.2 %copy-start.6 = (bf16[2048,64]{0,1:T(8,128)(2,1)S(1)}, bf16[2048,64]{0,1:T(8,128)(2,1)}, u32[]{:S(2)}) copy-start(bf16[2048,64]{0,1:T(8,128)(2,1)} %param.14) | copy-start | bytes 786436
  12.9 11.0 %copy-start.8 = (s32[1,32]{1,0:T(1,128)S(1)}, s32[1,32]{1,0:T(1,128)}, u32[]{:S(2)}) copy-start(s32[1,32]{1,0:T(1,128)} %param.16) | copy-start | bytes 388
  12.9 11.1 %copy-start.9 = (s32[1,32]{1,0:T(1,128)S(1)}, s32[1,32]{1,0:T(1,128)}, u32[]{:S(2)}) copy-start(s32[1,32]{1,0:T(1,128)} %param.17) | copy-start | bytes 388
  12.9 21.9 %collective-permute-start.2 = (bf16[256,128]{1,0:T(8,128)(2,1)S(1)}, bf16[256,128]{1,0:T(8,128)(2,1)S(1)}, u32[]{:S(2)}, u32[]{:S(2)}) collective-permute-start(bf16[256,128]{1,0:T(8,128)(2,1)S(1)} %project1.1), channel_id=1, source_target_pairs={{0,1},{1,0},{2,3},{3,2},{4,5},{5,4},{6,7},{7,6},{8,9},{9,8},{10,11... | collective-permute-start | bytes 196616 | tf_op jit(solution)/shard_map/ppermute | solution.py:16
  15.0 2.2 %copy-start.1 = (bf16[1024,2048]{1,0:T(8,128)(2,1)S(1)}, bf16[1024,2048]{1,0:T(8,128)(2,1)}, u32[]{:S(2)}) copy-start(bf16[1024,2048]{1,0:T(8,128)(2,1)} %grad_ref.7) | copy-start | bytes 12582916
  17.2 13.3 %copy-start.7 = (bf16[128,512]{1,0:T(8,128)(2,1)S(1)}, bf16[128,512]{1,0:T(8,128)(2,1)}, u32[]{:S(2)}) copy-start(bf16[128,512]{1,0:T(8,128)(2,1)} %refs_4_.1) | copy-start | bytes 393220
  21.2 13.6 %collective-permute-start.1 = (bf16[256,128]{1,0:T(8,128)(2,1)S(1)}, bf16[256,128]{1,0:T(8,128)(2,1)S(1)}, u32[]{:S(2)}, u32[]{:S(2)}) collective-permute-start(bf16[256,128]{1,0:T(8,128)(2,1)S(1)} %project2.1), channel_id=1, source_target_pairs={{0,2},{1,3},{2,0},{3,1},{4,6},{5,7},{6,4},{7,5},{8,10},{9,11},{10,... | collective-permute-start | bytes 196616 | tf_op jit(solution)/shard_map/ppermute | solution.py:16
  24.3 2.2 %copy-start.2 = (bf16[1024,2048]{1,0:T(8,128)(2,1)S(1)}, bf16[1024,2048]{1,0:T(8,128)(2,1)}, u32[]{:S(2)}) copy-start(bf16[1024,2048]{1,0:T(8,128)(2,1)} %grad_ref.7) | copy-start | bytes 12582916
  30.5 6.1 %collective-permute-start = (bf16[256,128]{1,0:T(8,128)(2,1)S(1)}, bf16[256,128]{1,0:T(8,128)(2,1)S(1)}, u32[]{:S(2)}, u32[]{:S(2)}) collective-permute-start(bf16[256,128]{1,0:T(8,128)(2,1)S(1)} %project3.1), channel_id=1, source_target_pairs={{0,3},{1,2},{2,1},{3,0},{4,7},{5,6},{6,5},{7,4},{8,11},{9,10},{10,... | collective-permute-start | bytes 196616 | tf_op jit(solution)/shard_map/ppermute | solution.py:16
  30.6 10.5 %collective-permute-start.9 = (bf16[512,512]{1,0:T(8,128)(2,1)S(1)}, bf16[512,512]{1,0:T(8,128)(2,1)S(1)}, u32[]{:S(2)}, u32[]{:S(2)}) collective-permute-start(bf16[512,512]{1,0:T(8,128)(2,1)S(1)} %pad_maximum_fusion), channel_id=1, source_target_pairs={{0,4},{4,0},{8,12},{12,8},{16,20},{20,16},{24,28},{28,24},{1,5},{5... | collective-permute-start | bytes 1572872 | tf_op jit(solution)/shard_map/ppermute | solution.py:16
  36.6 5.4 %collective-permute-start.3 = (bf16[256,128]{1,0:T(8,128)(2,1)S(1)}, bf16[256,128]{1,0:T(8,128)(2,1)S(1)}, u32[]{:S(2)}, u32[]{:S(2)}) collective-permute-start(bf16[256,128]{1,0:T(8,128)(2,1)S(1)} %add_convert_fusion.refs_0_), channel_id=1, source_target_pairs={{0,1},{1,0},{2,3},{3,2},{4,5},{5,4},{6,7},{7,6},{8,9},{9,8},{10,11... | collective-permute-start | bytes 196616 | tf_op jit(solution)/shard_map/ppermute | solution.py:16
  36.7 7.8 %collective-permute-start.4 = (bf16[256,128]{1,0:T(8,128)(2,1)S(1)}, bf16[256,128]{1,0:T(8,128)(2,1)S(1)}, u32[]{:S(2)}, u32[]{:S(2)}) collective-permute-start(bf16[256,128]{1,0:T(8,128)(2,1)S(1)} %add_convert_fusion.refs_0_), channel_id=1, source_target_pairs={{0,2},{1,3},{2,0},{3,1},{4,6},{5,7},{6,4},{7,5},{8,10},{9,11},{10,... | collective-permute-start | bytes 196616 | tf_op jit(solution)/shard_map/ppermute | solution.py:16
  39.3 6.1 %collective-permute-start.5 = (bf16[256,128]{1,0:T(8,128)(2,1)S(1)}, bf16[256,128]{1,0:T(8,128)(2,1)S(1)}, u32[]{:S(2)}, u32[]{:S(2)}) collective-permute-start(bf16[256,128]{1,0:T(8,128)(2,1)S(1)} %add_convert_fusion.refs_0_), channel_id=1, source_target_pairs={{0,3},{1,2},{2,1},{3,0},{4,7},{5,6},{6,5},{7,4},{8,11},{9,10},{10,... | collective-permute-start | bytes 196616 | tf_op jit(solution)/shard_map/ppermute | solution.py:16
  49.7 8.5 %all-to-all-start = ((bf16[8,8,128]{2,1,0:T(8,128)(2,1)}), bf16[8,8,128]{2,1,0:T(8,128)(2,1)S(1)}, u32[]{:S(2)}, u32[]{:S(2)}) async-start(bf16[8,8,128]{2,1,0:T(8,128)(2,1)} %bitcast.14), calls=%async_computation | async-start | bytes 32768 | tf_op jit(solution)/shard_map/all_to_all | solution.py:168

commit v2 on v1

v2 whole, which is shorter than its diff:
```python
import functools

import jax
import jax.numpy as jnp
from jax import lax
from jax.experimental import pallas as pl
from jax.experimental.pallas import tpu as pltpu
from jax.sharding import PartitionSpec as P


BF16, F32 = jnp.bfloat16, jnp.float32
NT = (((1,), (1,)), ((), ()))
VMEM_LIMIT = 40 << 20


def far(x):
    return pltpu.with_memory_space_constraint(x, pltpu.HBM)


def swap(x, axis, k):
    return lax.ppermute(x, axis, [(i, i ^ k) for i in range(lax.axis_size(axis))])


def project_kernel(per_chunk, ahead, chunk_ref, act_hbm, grad_hbm, wa_hbm, wg_hbm, out_ref, act, grad, wa, wg, sem, wsem):
    blocks, rows = act.shape[0], act.shape[1]

    def copies(i):
        chunk = chunk_ref[i // per_chunk] * per_chunk + i % per_chunk
        at = pl.ds(pl.multiple_of(chunk * rows, rows), rows)
        return (
            pltpu.make_async_copy(grad_hbm.at[at], grad.at[i], sem.at[0, i]),
            pltpu.make_async_copy(act_hbm.at[at], act.at[i], sem.at[1, i]),
        )

    weights = (
        pltpu.make_async_copy(wg_hbm, wg, wsem.at[0]),
        pltpu.make_async_copy(wa_hbm, wa, wsem.at[1]),
    )
    for copy in weights:
        copy.start()
    for i in range(min(ahead, blocks)):
        for copy in copies(i):
            copy.start()
    for copy in weights:
        copy.wait()

    def step(i, carry):
        for copy in copies(i):
            copy.wait()

        @pl.when(i + ahead < blocks)
        def _():
            for copy in copies(i + ahead):
                copy.start()

        left = lax.dot_general(act[i], wa[...], NT, preferred_element_type=F32)
        right = lax.dot_general(grad[i], wg[...], NT, preferred_element_type=F32)
        at = pl.ds(pl.multiple_of(i * rows, rows), rows)
        out_ref[at, :] = jnp.concatenate([left, right], axis=1).astype(out_ref.dtype)
        return carry

    lax.fori_loop(0, blocks, step, 0)


def project(chunks, activations, out_grads, wa, wg, rows, per_chunk, ahead):
    ff, d, k = activations.shape[1], out_grads.shape[1], wa.shape[0]
    count = chunks.shape[0]
    blocks, block = count * per_chunk, rows // per_chunk
    hbm = pl.BlockSpec(memory_space=pl.ANY)
    return pl.pallas_call(
        functools.partial(project_kernel, per_chunk, ahead),
        out_shape=jax.ShapeDtypeStruct((count * rows, 2 * k), BF16),
        in_specs=[pl.BlockSpec(memory_space=pltpu.SMEM)] + [hbm] * 4,
        out_specs=pl.BlockSpec(memory_space=pltpu.VMEM),
        scratch_shapes=[
            pltpu.VMEM((blocks, block, ff), BF16),
            pltpu.VMEM((blocks, block, d), BF16),
            pltpu.VMEM((k, ff), BF16),
            pltpu.VMEM((k, d), BF16),
            pltpu.SemaphoreType.DMA((2, blocks)),
            pltpu.SemaphoreType.DMA((2,)),
        ],
        compiler_params=pltpu.CompilerParams(vmem_limit_bytes=VMEM_LIMIT),
        cost_estimate=pl.CostEstimate(
            flops=2 * count * rows * (ff + d) * k,
            bytes_accessed=2 * count * rows * (ff + d),
            transcendentals=0,
        ),
    )(chunks, far(activations), far(out_grads), far(wa), far(wg))


def score_kernel(n_chunks, group, place_ref, bounds_ref, scale_ref, select_ref, labels_ref, *refs):
    chunks, held = refs[:n_chunks], refs[n_chunks : n_chunks + 2]
    out_ref, left, right, member, sketch, local = refs[n_chunks + 2 :]
    rows, k = chunks[0].shape[0], chunks[0].shape[1] // 2
    docs, nval = bounds_ref.shape[1], local.shape[0]
    for c, ref in enumerate(chunks):
        turned = ref[...].astype(F32).T
        left[:, c * rows : (c + 1) * rows] = turned[:k]
        right[:, c * rows : (c + 1) * rows] = turned[k:].astype(BF16)
        at = place_ref[c] * rows + lax.broadcasted_iota(jnp.int32, (rows, docs), 0)
        inside = (at >= bounds_ref[0:1, :]) & (at < bounds_ref[1:2, :])
        member[c * rows : (c + 1) * rows, :] = inside.astype(F32).astype(BF16)

    def sketch_step(i, carry):
        some = left[pl.ds(pl.multiple_of(i * group, group), group), :].astype(BF16)
        grads = right[...]
        outer = jnp.concatenate([some[j : j + 1, :] * grads for j in range(group)], axis=0)
        summed = jnp.dot(outer, member[...], preferred_element_type=F32)
        at = pl.ds(pl.multiple_of(i * group * k, group * k), group * k)
        sketch[at, :] = (summed * scale_ref[...]).astype(BF16)
        return carry

    lax.fori_loop(0, k // group, sketch_step, 0)
    wide = held[0].shape[1]
    blocks = held[0].shape[0] // nval
    local[...] = jnp.zeros_like(local)
    for half in range(2):

        def local_step(b, carry, half=half):
            start = pl.multiple_of(place_ref[n_chunks + half * blocks + b] * wide, wide)
            local[...] += jnp.dot(
                held[half][pl.ds(pl.multiple_of(b * nval, nval), nval), :],
                sketch[pl.ds(start, wide), :],
                preferred_element_type=F32,
            )
            return carry

        lax.fori_loop(0, blocks, local_step, 0)
    packed = lax.dot_general(
        select_ref[...], local[...].astype(BF16), NT, preferred_element_type=F32
    )
    out_ref[...] = (packed + labels_ref[...]).astype(BF16)


def score(place, bounds, scaling, select, labels, chunks, held, nval):
    tokens = len(chunks) * chunks[0].shape[0]
    k = chunks[0].shape[1] // 2
    docs = bounds.shape[1]
    vmem = pl.BlockSpec(memory_space=pltpu.VMEM)
    return pl.pallas_call(
        functools.partial(score_kernel, len(chunks), 8),
        out_shape=jax.ShapeDtypeStruct((select.shape[0], nval), BF16),
        in_specs=[pl.BlockSpec(memory_space=pltpu.SMEM)] + [vmem] * (4 + len(chunks) + 2),
        out_specs=vmem,
        scratch_shapes=[
            pltpu.VMEM((k, tokens), F32),
            pltpu.VMEM((k, tokens), BF16),
            pltpu.VMEM((tokens, docs), BF16),
            pltpu.VMEM((k * k, docs), BF16),
            pltpu.VMEM((nval, docs), F32),
        ],
        compiler_params=pltpu.CompilerParams(vmem_limit_bytes=16 << 20),
        cost_estimate=pl.CostEstimate(
            flops=2 * k * k * docs * (tokens + nval), bytes_accessed=2 * k * k * nval, transcendentals=0
        ),
        name="score",
    )(place, bounds, scaling, select, labels, *chunks, *held)


def shards(activations, out_grads, proj_in, proj_out, validation, doc_lengths, owner_rows):
    devices, parts = lax.axis_size("dp"), lax.axis_size("tensor")
    me, part = lax.axis_index("dp"), lax.axis_index("tensor")
    tokens, maxdoc = activations.shape[0], doc_lengths.shape[1]
    rows = tokens // parts

    nval = validation.shape[0]
    held, order = validation, [0]
    bits = [1 << i for i in range(devices.bit_length() - 1)]
    for bit in bits[1:]:
        held = jnp.concatenate([held, swap(held, "dp", bit)], axis=0)
        order += [b ^ bit for b in order]
    halves = (held, swap(held, "dp", bits[0]))
    order += [b ^ bits[0] for b in order]

    wa, wg = proj_in.T, proj_out.T
    peers = list(range(parts - 1, 0, -1))
    near = part ^ jnp.array(peers, jnp.int32)
    sent = project(near, activations, out_grads, wa, wg, rows, 1, 2)
    got = [swap(sent[i * rows : (i + 1) * rows], "tensor", peer) for i, peer in enumerate(peers)]
    mine = part + jnp.zeros((1,), jnp.int32)
    mine, _ = lax.optimization_barrier((mine, sent))
    total = project(mine, activations, out_grads, wa, wg, rows, 2, 2).astype(F32)
    for piece in got:
        total = total + piece.astype(F32)
    summed = total.astype(BF16)
    chunks = [summed] + [swap(summed, "tensor", peer) for peer in range(1, parts)]

    lengths, out_rows = doc_lengths[0], owner_rows[0]
    indices = jnp.arange(maxdoc, dtype=jnp.int32)
    starts = jnp.sum(jnp.where(indices[:, None] < indices[None, :], lengths[:, None], 0), axis=0)
    bounds = jnp.stack([starts, starts + lengths])
    scaling = (1.0 / jnp.sqrt(jnp.maximum(lengths, 1).astype(F32)))[None, :]

    per_owner = max(1, maxdoc // devices)
    height = -(-2 * per_owner // 8) * 8
    owners, out_slot = out_rows // maxdoc, out_rows % maxdoc
    earlier = (owners[None, :] == owners[:, None]) & (indices[None, :] < indices[:, None])
    target = owners * height + jnp.sum(earlier.astype(jnp.int32), axis=1)
    at = jnp.arange(devices * height, dtype=jnp.int32)
    select = (target[None, :] == at[:, None]).astype(BF16)
    label = jnp.where(lengths > 0, out_slot, -1)
    labels = jnp.sum(
        jnp.where(target[None, :] + per_owner == at[:, None], label[None, :], 0), axis=1
    )
    labels = jnp.broadcast_to(labels.astype(F32)[:, None], (devices * height, nval))
    place = jnp.concatenate(
        [part ^ jnp.arange(parts, dtype=jnp.int32), me ^ jnp.array(order, jnp.int32)]
    )

    payload = score(place, bounds, scaling, select, labels, chunks, halves, nval)
    got_rows = lax.all_to_all(
        payload.reshape(devices, height, nval), "dp", split_axis=0, concat_axis=0, tiled=True
    )
    data = got_rows[:, :per_owner].reshape(devices * per_owner, nval)
    tags = got_rows[:, per_owner : 2 * per_owner, :maxdoc].reshape(devices * per_owner, maxdoc)
    choose = (tags.astype(F32) == indices.astype(F32)[None, :]).astype(BF16)
    return lax.dot_general(
        choose, data, (((0,), (0,)), ((), ())), preferred_element_type=F32
    ).astype(BF16)


def solution(mesh):
    placed = (
        P("dp", "tensor"),
        P("dp", "tensor"),
        P("tensor", None),
        P("tensor", None),
        P("tensor", "dp"),
        P("dp", None),
        P("dp", None),
    )
    return jax.shard_map(
        shards, mesh=mesh, in_specs=placed, out_specs=P("dp", "tensor"), check_vma=False
    )
```

time: 59.5 us -> 56.5 us (0.950)
  local copies, waits for them, and re-layouts: 8.82 us -> 0.14 us
  waiting for transfers between devices: 10.8 us -> 18.2 us
  Pallas kernels: 20.2 us -> 18.2 us
  other arithmetic: 0.58 us -> 1.26 us
    unnamed x20 -> x10, local copies, waits for them, and re-layouts: 8.71 us -> 0.04 us
    ppermute x10 -> x9, waiting for transfers between devices: 6.02 us -> 13.5 us  [swap(): lax.ppermute(x, axis, [(i, i ^ k) for i in range(lax.axis_size(axis))])]
    pallas_call x5 -> x3, Pallas kernels: 20.2 us -> 18.2 us  [the longest x2 11.8 us: project(): pl.pallas_call(functools.partial(project_kernel, per_chunk, ahead), out_s...]
    xor x1 -> x2, other arithmetic: 0.01 us -> 0.7 us  [the longest x1 0.69 us: shards(): near = part ^ jnp.array(peers, jnp.int32)]
    ppermute x10 -> x9, starting transfers between devices: 13.9 us -> 13.7 us  [swap(): lax.ppermute(x, axis, [(i, i ^ k) for i in range(lax.axis_size(axis))])]
  transfers between devices with their start and end apart: 11 -> 10, of which waited for: 5 -> 5; matrix products, arithmetic and copies ran while one was open for 1% -> 1% of each run, Pallas kernels for 27% -> 7%
where the time goes in v2:
time: 56.5 us; the launch traced here: 56.3 us
  Pallas kernels  18.2 us (32%)
  waiting for transfers between devices  18.2 us (32%)
  starting transfers between devices  17.5 us (31%)
  other arithmetic  1.26 us (2%)
  matrix products  0.8 us (1%)
    ppermute x9, starting transfers between devices, swap(): lax.ppermute(x, axis, [(i, i ^ k) for i in range(lax.axis_size(axis))])  13.7 us
    ppermute x9, waiting for transfers between devices, swap(): lax.ppermute(x, axis, [(i, i ^ k) for i in range(lax.axis_size(axis))])  13.5 us
    pallas_call x2, Pallas kernels, project(): pl.pallas_call(functools.partial(project_kernel, per_chunk, ahead), out_s...  11.8 us
    pallas_call x1, Pallas kernels, score(): pl.pallas_call(functools.partial(score_kernel, len(chunks), 8), out_shape...  6.5 us
    all_to_all x1, waiting for transfers between devices, shards(): lax.all_to_all(payload.reshape(devices, height, nval), 'dp', split_axis=0...  4.75 us
    all_to_all x1, starting transfers between devices, shards(): lax.all_to_all(payload.reshape(devices, height, nval), 'dp', split_axis=0...  3.73 us
  transfers between devices with their start and end apart: 10, of which 5 were waited for; matrix products, arithmetic and copies ran while one was open for 1% of the time, Pallas kernels for 7%

profile of v2, /device:TPU:0, one launch (start us, length us, event | category | flops | bytes accessed | tf_op | source)
XLA Modules:
  0.0 56.3 jit_solution(11029906166748991787)
XLA Ops:
  0.0 0.7 %broadcast_xor_fusion.chunk_ref = s32[3]{0:T(128)S(1)} fusion(s32[3]{0:T(128)} %constant.50.clone, s32[]{:T(128)} %axis_index.22), kind=kLoop, calls=%fused_computation.39 | loop fusion | flops 3 | bytes 28 | tf_op jit(solution)/shard_map/xor | solution.py:178
  0.7 7.9 %shard_map.91 = bf16[768,128]{1,0:T(8,128)(2,1)S(1)} custom-call(s32[3]{0:T(128)S(1)} %broadcast_xor_fusion.chunk_ref, bf16[1024,7168]{1,0:T(8,128)(2,1)} %act_hbm.3, bf16[1024,2048]{1,0:T(8,128)(2,1)} %grad_hbm.3, bf16[64,7168]{1,0:T(8,128)(2,1)} %bitcast.32, bf16[64,2048]{1,0:T(8,128)(2,1)} %bitcast.34), custom_call_target="tpu_custom_call" | custom-call | flops 905969664 | bytes 14155776 | tf_op jit(solution)/shard_map/pallas_call | solution.py:70
  8.6 5.2 %collective-permute-start = (bf16[256,128]{1,0:T(8,128)(2,1)S(1)}, bf16[256,128]{1,0:T(8,128)(2,1)S(1)}, u32[]{:S(2)}, u32[]{:S(2)}) collective-permute-start(bf16[256,128]{1,0:T(8,128)(2,1)S(1)} %get-tuple-element.7), channel_id=1, source_target_pairs={{0,3},{1,2},{2,1},{3,0},{4,7},{5,6},{6,5},{7,4},{8,11},{9,10},{10,... | collective-permute-start | bytes 196616 | tf_op jit(solution)/shard_map/ppermute | solution.py:21
  13.8 0.0 collective-permute-start.1
  13.8 0.6 %collective-permute-start.2 = (bf16[256,128]{1,0:T(8,128)(2,1)S(1)}, bf16[256,128]{1,0:T(8,128)(2,1)S(1)}, u32[]{:S(2)}, u32[]{:S(2)}) collective-permute-start(bf16[256,128]{1,0:T(8,128)(2,1)S(1)} %get-tuple-element.8), channel_id=1, source_target_pairs={{0,1},{1,0},{2,3},{3,2},{4,5},{5,4},{6,7},{7,6},{8,9},{9,8},{10,11... | collective-permute-start | bytes 196616 | tf_op jit(solution)/shard_map/ppermute | solution.py:21
  14.5 0.0 copy-done
  14.5 1.6 %collective-permute-start.6 = (bf16[128,512]{1,0:T(8,128)(2,1)S(1)}, bf16[128,512]{1,0:T(8,128)(2,1)S(1)}, u32[]{:S(2)}, u32[]{:S(2)}) collective-permute-start(bf16[128,512]{1,0:T(8,128)(2,1)S(1)} %copy-done), channel_id=1, source_target_pairs={{0,8},{4,12},{8,0},{12,4},{16,24},{20,28},{24,16},{28,20},{1,9},{5... | collective-permute-start | bytes 393224 | tf_op jit(solution)/shard_map/ppermute | solution.py:21
  16.1 0.1 select_reduce_fusion.1
  16.2 0.0 copy-done.2
  16.3 0.2 convert_reduce_fusion
  16.5 3.0 %collective-permute-done.6 = bf16[128,512]{1,0:T(8,128)(2,1)S(1)} collective-permute-done((bf16[128,512]{1,0:T(8,128)(2,1)S(1)}, bf16[128,512]{1,0:T(8,128)(2,1)S(1)}, u32[]{:S(2)}, u32[]{:S(2)}) %collective-permute-start.6) | collective-permute-done | bytes 131104 | tf_op jit(solution)/shard_map/ppermute | solution.py:21
  19.5 1.7 %collective-permute-start.7 = (bf16[256,512]{1,0:T(8,128)(2,1)S(1)}, bf16[256,512]{1,0:T(8,128)(2,1)S(1)}, u32[]{:S(2)}, u32[]{:S(2)}) collective-permute-start(bf16[256,512]{1,0:T(8,128)(2,1)S(1)} %pad_maximum_fusion), channel_id=1, source_target_pairs={{0,16},{4,20},{8,24},{12,28},{16,0},{20,4},{24,8},{28,12},{1,17},{... | collective-permute-start | bytes 786440 | tf_op jit(solution)/shard_map/ppermute | solution.py:21
  21.2 0.1 select_reduce_fusion
  21.3 4.8 %collective-permute-done.7 = bf16[256,512]{1,0:T(8,128)(2,1)S(1)} collective-permute-done((bf16[256,512]{1,0:T(8,128)(2,1)S(1)}, bf16[256,512]{1,0:T(8,128)(2,1)S(1)}, u32[]{:S(2)}, u32[]{:S(2)}) %collective-permute-start.7) | collective-permute-done | bytes 262176 | tf_op jit(solution)/shard_map/ppermute | solution.py:21
  26.2 0.1 collective-permute-start.8
  26.3 3.9 %shard_map.92 = bf16[256,128]{1,0:T(8,128)(2,1)S(1)} custom-call(s32[1]{0:T(128)} %bitcast.8.chunk_ref, bf16[1024,7168]{1,0:T(8,128)(2,1)} %act_hbm.3, bf16[1024,2048]{1,0:T(8,128)(2,1)} %grad_hbm.3, bf16[64,7168]{1,0:T(8,128)(2,1)} %bitcast.33, bf16[64,2048]{1,0:T(8,128)(2,1)} %bitcast.35), custom_call_target="tpu_custom_call" | custom-call | flops 301989888 | bytes 4718592 | tf_op jit(solution)/shard_map/pallas_call | solution.py:70
  30.2 0.0 collective-permute-done
  30.2 0.0 collective-permute-done.1
  30.2 0.0 collective-permute-done.2
  30.2 1.3 %collective-permute-start.3 = (bf16[256,128]{1,0:T(8,128)(2,1)S(1)}, bf16[256,128]{1,0:T(8,128)(2,1)S(1)}, u32[]{:S(2)}, u32[]{:S(2)}) collective-permute-start(bf16[256,128]{1,0:T(8,128)(2,1)S(1)} %add_convert_fusion.refs_0_), channel_id=1, source_target_pairs={{0,1},{1,0},{2,3},{3,2},{4,5},{5,4},{6,7},{7,6},{8,9},{9,8},{10,11... | collective-permute-start | bytes 196616 | tf_op jit(solution)/shard_map/ppermute | solution.py:21
  31.6 2.8 %collective-permute-start.4 = (bf16[256,128]{1,0:T(8,128)(2,1)S(1)}, bf16[256,128]{1,0:T(8,128)(2,1)S(1)}, u32[]{:S(2)}, u32[]{:S(2)}) collective-permute-start(bf16[256,128]{1,0:T(8,128)(2,1)S(1)} %add_convert_fusion.refs_0_), channel_id=1, source_target_pairs={{0,2},{1,3},{2,0},{3,1},{4,6},{5,7},{6,4},{7,5},{8,10},{9,11},{10,... | collective-permute-start | bytes 196616 | tf_op jit(solution)/shard_map/ppermute | solution.py:21
  34.4 0.3 collective-permute-start.5
  34.7 0.1 pad_add_fusion.1.place_ref
  34.8 0.0 collective-permute-done.3.refs_1_
  34.8 3.9 %collective-permute-done.4.refs_2_ = bf16[256,128]{1,0:T(8,128)(2,1)S(1)} collective-permute-done((bf16[256,128]{1,0:T(8,128)(2,1)S(1)}, bf16[256,128]{1,0:T(8,128)(2,1)S(1)}, u32[]{:S(2)}, u32[]{:S(2)}) %collective-permute-start.4) | collective-permute-done | bytes 65568 | tf_op jit(solution)/shard_map/ppermute | solution.py:21
  38.7 1.8 %collective-permute-done.5.refs_3_ = bf16[256,128]{1,0:T(8,128)(2,1)S(1)} collective-permute-done((bf16[256,128]{1,0:T(8,128)(2,1)S(1)}, bf16[256,128]{1,0:T(8,128)(2,1)S(1)}, u32[]{:S(2)}, u32[]{:S(2)}) %collective-permute-start.5) | collective-permute-done | bytes 65568 | tf_op jit(solution)/shard_map/ppermute | solution.py:21
  40.4 0.0 collective-permute-done.8.refs_5_
  40.4 0.1 broadcast_in_dim.55.labels_ref
  40.5 6.5 %score.1 = bf16[64,128]{1,0:T(8,128)(2,1)} custom-call(s32[12]{0:T(128)S(1)} %pad_add_fusion.1.place_ref, s32[2,32]{1,0:T(2,128)S(1)} %pad_add_fusion.bounds_ref, f32[1,32]{1,0:T(1,128)S(1)} %convert_rsqrt_fusion.scale_ref, bf16[64,32]{1,0:T(8,128)(2,1)S(1)} %fusion.1.select_ref, f32[64,128]{1,0:T(8,128)S(1)} %broadcast_in_dim.55.labels_ref, ...), custom_call_target="tpu_custom_call" | custom-call | flops 301989888 | bytes 1048576 | tf_op jit(solution)/shard_map/score/pallas_call | solution.py:141
  47.0 3.7 %all-to-all-start = ((bf16[8,8,128]{2,1,0:T(8,128)(2,1)}), bf16[8,8,128]{2,1,0:T(8,128)(2,1)S(1)}, u32[]{:S(2)}, u32[]{:S(2)}) async-start(bf16[8,8,128]{2,1,0:T(8,128)(2,1)} %bitcast.11), calls=%async_computation | async-start | bytes 32768 | tf_op jit(solution)/shard_map/all_to_all | solution.py:212
  50.7 4.7 %all-to-all-done = bf16[8,8,128]{2,1,0:T(8,128)(2,1)S(1)} async-done(((bf16[8,8,128]{2,1,0:T(8,128)(2,1)}), bf16[8,8,128]{2,1,0:T(8,128)(2,1)S(1)}, u32[]{:S(2)}, u32[]{:S(2)}) %all-to-all-start) | async-done | bytes 16416 | tf_op jit(solution)/shard_map/all_to_all | solution.py:212
  55.5 0.8 %fusion = bf16[32,128]{1,0:T(8,128)(2,1)} fusion(bf16[8,8,128]{2,1,0:T(8,128)(2,1)S(1)} %all-to-all-done, f32[32]{0:T(128)S(1)} %iota_convert_fusion), kind=kOutput, calls=%fused_computation.1 | convolution fusion | flops 268288 | bytes 24704 | tf_op jit(solution)/shard_map/dot_general | solution.py:218
  (22 shorter events, 0.2 us)
Async XLA Ops:
  0.0 16.5 %copy-start.3 = (s32[8]{0:T(128)S(1)}, s32[8]{0:T(128)}, u32[]{:S(2)}) copy-start(s32[8]{0:T(128)} %constant.51.clone) | copy-start | bytes 100
  0.0 14.5 %copy-start = (bf16[128,512]{1,0:T(8,128)(2,1)S(1)}, bf16[128,512]{1,0:T(8,128)(2,1)}, u32[]{:S(2)}) copy-start(bf16[128,512]{1,0:T(8,128)(2,1)} %param.13) | copy-start | bytes 393220
  0.0 16.1 %copy-start.1 = (s32[1,32]{1,0:T(1,128)S(1)}, s32[1,32]{1,0:T(1,128)}, u32[]{:S(2)}) copy-start(s32[1,32]{1,0:T(1,128)} %param.14) | copy-start | bytes 388
  0.0 16.2 %copy-start.2 = (s32[1,32]{1,0:T(1,128)S(1)}, s32[1,32]{1,0:T(1,128)}, u32[]{:S(2)}) copy-start(s32[1,32]{1,0:T(1,128)} %param.15) | copy-start | bytes 388
  8.6 21.5 %collective-permute-start = (bf16[256,128]{1,0:T(8,128)(2,1)S(1)}, bf16[256,128]{1,0:T(8,128)(2,1)S(1)}, u32[]{:S(2)}, u32[]{:S(2)}) collective-permute-start(bf16[256,128]{1,0:T(8,128)(2,1)S(1)} %get-tuple-element.7), channel_id=1, source_target_pairs={{0,3},{1,2},{2,1},{3,0},{4,7},{5,6},{6,5},{7,4},{8,11},{9,10},{10,... | collective-permute-start | bytes 196616 | tf_op jit(solution)/shard_map/ppermute | solution.py:21
  13.8 16.3 %collective-permute-start.1 = (bf16[256,128]{1,0:T(8,128)(2,1)S(1)}, bf16[256,128]{1,0:T(8,128)(2,1)S(1)}, u32[]{:S(2)}, u32[]{:S(2)}) collective-permute-start(bf16[256,128]{1,0:T(8,128)(2,1)S(1)} %get-tuple-element.9), channel_id=1, source_target_pairs={{0,2},{1,3},{2,0},{3,1},{4,6},{5,7},{6,4},{7,5},{8,10},{9,11},{10,... | collective-permute-start | bytes 196616 | tf_op jit(solution)/shard_map/ppermute | solution.py:21
  13.8 16.4 %collective-permute-start.2 = (bf16[256,128]{1,0:T(8,128)(2,1)S(1)}, bf16[256,128]{1,0:T(8,128)(2,1)S(1)}, u32[]{:S(2)}, u32[]{:S(2)}) collective-permute-start(bf16[256,128]{1,0:T(8,128)(2,1)S(1)} %get-tuple-element.8), channel_id=1, source_target_pairs={{0,1},{1,0},{2,3},{3,2},{4,5},{5,4},{6,7},{7,6},{8,9},{9,8},{10,11... | collective-permute-start | bytes 196616 | tf_op jit(solution)/shard_map/ppermute | solution.py:21
  14.5 5.0 %collective-permute-start.6 = (bf16[128,512]{1,0:T(8,128)(2,1)S(1)}, bf16[128,512]{1,0:T(8,128)(2,1)S(1)}, u32[]{:S(2)}, u32[]{:S(2)}) collective-permute-start(bf16[128,512]{1,0:T(8,128)(2,1)S(1)} %copy-done), channel_id=1, source_target_pairs={{0,8},{4,12},{8,0},{12,4},{16,24},{20,28},{24,16},{28,20},{1,9},{5... | collective-permute-start | bytes 393224 | tf_op jit(solution)/shard_map/ppermute | solution.py:21
  19.5 6.7 %collective-permute-start.7 = (bf16[256,512]{1,0:T(8,128)(2,1)S(1)}, bf16[256,512]{1,0:T(8,128)(2,1)S(1)}, u32[]{:S(2)}, u32[]{:S(2)}) collective-permute-start(bf16[256,512]{1,0:T(8,128)(2,1)S(1)} %pad_maximum_fusion), channel_id=1, source_target_pairs={{0,16},{4,20},{8,24},{12,28},{16,0},{20,4},{24,8},{28,12},{1,17},{... | collective-permute-start | bytes 786440 | tf_op jit(solution)/shard_map/ppermute | solution.py:21
  26.2 14.2 %collective-permute-start.8 = (bf16[512,512]{1,0:T(8,128)(2,1)S(1)}, bf16[512,512]{1,0:T(8,128)(2,1)S(1)}, u32[]{:S(2)}, u32[]{:S(2)}) collective-permute-start(bf16[512,512]{1,0:T(8,128)(2,1)S(1)} %constant_dynamic-update-slice_fusion.refs_4_), channel_id=1, source_target_pairs={{0,4},{4,0},{8,12},{12,8},{16,20},{20,16},{24,28},{28,24},{1,5},{5... | collective-permute-start | bytes 1572872 | tf_op jit(solution)/shard_map/ppermute | solution.py:21
  30.2 4.6 %collective-permute-start.3 = (bf16[256,128]{1,0:T(8,128)(2,1)S(1)}, bf16[256,128]{1,0:T(8,128)(2,1)S(1)}, u32[]{:S(2)}, u32[]{:S(2)}) collective-permute-start(bf16[256,128]{1,0:T(8,128)(2,1)S(1)} %add_convert_fusion.refs_0_), channel_id=1, source_target_pairs={{0,1},{1,0},{2,3},{3,2},{4,5},{5,4},{6,7},{7,6},{8,9},{9,8},{10,11... | collective-permute-start | bytes 196616 | tf_op jit(solution)/shard_map/ppermute | solution.py:21
  31.6 7.1 %collective-permute-start.4 = (bf16[256,128]{1,0:T(8,128)(2,1)S(1)}, bf16[256,128]{1,0:T(8,128)(2,1)S(1)}, u32[]{:S(2)}, u32[]{:S(2)}) collective-permute-start(bf16[256,128]{1,0:T(8,128)(2,1)S(1)} %add_convert_fusion.refs_0_), channel_id=1, source_target_pairs={{0,2},{1,3},{2,0},{3,1},{4,6},{5,7},{6,4},{7,5},{8,10},{9,11},{10,... | collective-permute-start | bytes 196616 | tf_op jit(solution)/shard_map/ppermute | solution.py:21
  34.4 6.1 %collective-permute-start.5 = (bf16[256,128]{1,0:T(8,128)(2,1)S(1)}, bf16[256,128]{1,0:T(8,128)(2,1)S(1)}, u32[]{:S(2)}, u32[]{:S(2)}) collective-permute-start(bf16[256,128]{1,0:T(8,128)(2,1)S(1)} %add_convert_fusion.refs_0_), channel_id=1, source_target_pairs={{0,3},{1,2},{2,1},{3,0},{4,7},{5,6},{6,5},{7,4},{8,11},{9,10},{10,... | collective-permute-start | bytes 196616 | tf_op jit(solution)/shard_map/ppermute | solution.py:21
  47.0 8.5 %all-to-all-start = ((bf16[8,8,128]{2,1,0:T(8,128)(2,1)}), bf16[8,8,128]{2,1,0:T(8,128)(2,1)S(1)}, u32[]{:S(2)}, u32[]{:S(2)}) async-start(bf16[8,8,128]{2,1,0:T(8,128)(2,1)} %bitcast.11), calls=%async_computation | async-start | bytes 32768 | tf_op jit(solution)/shard_map/all_to_all | solution.py:212

commit v3 on v2

v3 whole, which is shorter than its diff:
```python
import functools

import jax
import jax.numpy as jnp
from jax import lax
from jax.experimental import pallas as pl
from jax.experimental.pallas import tpu as pltpu
from jax.sharding import PartitionSpec as P


BF16, F32 = jnp.bfloat16, jnp.float32
NT = (((1,), (1,)), ((), ()))
VMEM_LIMIT = 40 << 20


def far(x):
    return pltpu.with_memory_space_constraint(x, pltpu.HBM)


def swap(x, axis, k):
    return lax.ppermute(x, axis, [(i, i ^ k) for i in range(lax.axis_size(axis))])


def project_kernel(last, per_chunk, ahead, chunk_ref, act_hbm, grad_hbm, wa_hbm, wg_hbm, out_ref, act, grad, wa, wg, sem, wsem):
    blocks, rows = act.shape[0], act.shape[1]

    def copies(i):
        chunk = (chunk_ref[0] ^ (last - i // per_chunk)) * per_chunk + i % per_chunk
        at = pl.ds(pl.multiple_of(chunk * rows, rows), rows)
        return (
            pltpu.make_async_copy(grad_hbm.at[at], grad.at[i], sem.at[0, i]),
            pltpu.make_async_copy(act_hbm.at[at], act.at[i], sem.at[1, i]),
        )

    weights = (
        pltpu.make_async_copy(wg_hbm, wg, wsem.at[0]),
        pltpu.make_async_copy(wa_hbm, wa, wsem.at[1]),
    )
    for copy in weights:
        copy.start()
    for i in range(min(ahead, blocks)):
        for copy in copies(i):
            copy.start()
    for copy in weights:
        copy.wait()

    def step(i, carry):
        for copy in copies(i):
            copy.wait()

        @pl.when(i + ahead < blocks)
        def _():
            for copy in copies(i + ahead):
                copy.start()

        left = lax.dot_general(act[i], wa[...], NT, preferred_element_type=F32)
        right = lax.dot_general(grad[i], wg[...], NT, preferred_element_type=F32)
        at = pl.ds(pl.multiple_of(i % per_chunk * rows, rows), rows)
        out_ref[i // per_chunk, :, at] = jnp.concatenate([left, right], axis=1).T.astype(BF16)
        return carry

    lax.fori_loop(0, blocks, step, 0)


def project(part, last, count, activations, out_grads, wa, wg, rows, per_chunk, ahead):
    ff, d, k = activations.shape[1], out_grads.shape[1], wa.shape[0]
    blocks, block = count * per_chunk, rows // per_chunk
    hbm = pl.BlockSpec(memory_space=pl.ANY)
    return pl.pallas_call(
        functools.partial(project_kernel, last, per_chunk, ahead),
        out_shape=jax.ShapeDtypeStruct((count, 2 * k, rows), BF16),
        in_specs=[pl.BlockSpec(memory_space=pltpu.SMEM)] + [hbm] * 4,
        out_specs=pl.BlockSpec(memory_space=pltpu.VMEM),
        scratch_shapes=[
            pltpu.VMEM((blocks, block, ff), BF16),
            pltpu.VMEM((blocks, block, d), BF16),
            pltpu.VMEM((k, ff), BF16),
            pltpu.VMEM((k, d), BF16),
            pltpu.SemaphoreType.DMA((2, blocks)),
            pltpu.SemaphoreType.DMA((2,)),
        ],
        compiler_params=pltpu.CompilerParams(vmem_limit_bytes=VMEM_LIMIT),
        cost_estimate=pl.CostEstimate(
            flops=2 * count * rows * (ff + d) * k,
            bytes_accessed=2 * count * rows * (ff + d),
            transcendentals=0,
        ),
    )(part, far(activations), far(out_grads), far(wa), far(wg))


def score_kernel(n_chunks, low, place_ref, ends_ref, scale_ref, select_ref, labels_ref, *refs):
    chunks, held = refs[:n_chunks], refs[n_chunks : n_chunks + 2]
    out_ref, left, right, outer, sketch = refs[n_chunks + 2 :]
    k, rows = chunks[0].shape[0] // 2, chunks[0].shape[1]
    high = outer.shape[0] * outer.shape[2] // k
    docs, nval = low * high, out_ref.shape[1]
    for c, ref in enumerate(chunks):
        at = place_ref[c] * rows + lax.broadcasted_iota(jnp.int32, (docs, rows), 1)
        doc = jnp.sum((at >= ends_ref[:, :1]).astype(F32), axis=0, keepdims=True)
        div = jnp.floor(doc * (1.0 / low))
        mod = doc - div * low
        span = slice(c * rows, (c + 1) * rows)
        for m in range(low):
            mask = jnp.broadcast_to((mod == m).astype(F32), (k, rows)).astype(BF16)
            left[m * k : (m + 1) * k, span] = ref[:k, :] * mask
        for m in range(high):
            mask = jnp.broadcast_to((div == m).astype(F32), (k, rows)).astype(BF16)
            right[m * k : (m + 1) * k, span] = ref[k:, :] * mask
    lanes = outer.shape[2]
    sums = lax.dot_general(left[...], right[...], NT, preferred_element_type=F32)
    for m in range(outer.shape[0]):
        outer[m] = sums[:, m * lanes : (m + 1) * lanes]

    first = lax.broadcasted_iota(jnp.int32, (low, lanes), 1) < k
    for m in range(outer.shape[0]):
        scale = scale_ref[:, m * lanes : (m + 1) * lanes]
        for i in range(0, k, 2):
            even = outer[m, pl.ds(i, low, stride=k), :] * scale
            odd = outer[m, pl.ds(i + 1, low, stride=k), :] * scale
            pair = [
                jnp.where(first, even, pltpu.roll(odd, k, 1)),
                jnp.where(first, pltpu.roll(even, k, 1), odd),
            ]
            rows_at = slice(2 * m * low, 2 * (m + 1) * low)
            sketch[rows_at, i * k : i * k + lanes] = jnp.concatenate(pair, axis=0).astype(BF16)

    wide = held[0].shape[1]
    blocks = held[0].shape[0] // nval
    local = jnp.zeros((docs, nval), F32)
    for b in range(2 * blocks):
        start = pl.multiple_of(place_ref[n_chunks + b] * wide, wide)
        at = b % blocks * nval
        local += lax.dot_general(
            sketch[:, pl.ds(start, wide)],
            held[b // blocks][at : at + nval, :],
            NT,
            preferred_element_type=F32,
        )
    packed = jnp.dot(select_ref[...], local.astype(BF16), preferred_element_type=F32)
    out_ref[...] = (packed + labels_ref[...]).astype(BF16)


def score(place, ends, scale, select, labels, chunks, held, nval, low):
    k, rows = chunks[0].shape[0] // 2, chunks[0].shape[1]
    tokens = len(chunks) * rows
    docs = ends.shape[0]
    high = docs // low
    vmem = pl.BlockSpec(memory_space=pltpu.VMEM)
    return pl.pallas_call(
        functools.partial(score_kernel, len(chunks), low),
        out_shape=jax.ShapeDtypeStruct((select.shape[0], nval), BF16),
        in_specs=[pl.BlockSpec(memory_space=pltpu.SMEM)] + [vmem] * (4 + len(chunks) + 2),
        out_specs=vmem,
        scratch_shapes=[
            pltpu.VMEM((low * k, tokens), BF16),
            pltpu.VMEM((high * k, tokens), BF16),
            pltpu.VMEM((high // 2, low * k, 2 * k), F32),
            pltpu.VMEM((docs, k * k), BF16),
        ],
        compiler_params=pltpu.CompilerParams(vmem_limit_bytes=16 << 20),
        cost_estimate=pl.CostEstimate(
            flops=2 * k * k * docs * (tokens + nval), bytes_accessed=2 * k * k * nval, transcendentals=0
        ),
        name="score",
    )(place, ends, scale, select, labels, *chunks, *held)


def shards(activations, out_grads, proj_in, proj_out, validation, doc_lengths, owner_rows):
    devices, parts = lax.axis_size("dp"), lax.axis_size("tensor")
    me, part = lax.axis_index("dp"), lax.axis_index("tensor")
    tokens, maxdoc = activations.shape[0], doc_lengths.shape[1]
    rows = tokens // parts

    nval = validation.shape[0]
    held, order = validation, [0]
    bits = [1 << i for i in range(devices.bit_length() - 1)]
    for bit in bits[1:]:
        held = jnp.concatenate([held, swap(held, "dp", bit)], axis=0)
        order += [b ^ bit for b in order]
    halves = (held, swap(held, "dp", bits[0]))
    order += [b ^ bits[0] for b in order]

    wa, wg = proj_in.T, proj_out.T
    peers = list(range(parts - 1, 0, -1))
    place = part + jnp.zeros((1,), jnp.int32)
    sent = project(place, parts - 1, parts - 1, activations, out_grads, wa, wg, rows, 1, 2)
    got = [swap(sent[i], "tensor", peer) for i, peer in enumerate(peers)]
    place, _ = lax.optimization_barrier((place, sent))
    total = project(place, 0, 1, activations, out_grads, wa, wg, rows, 2, 2)[0].astype(F32)
    for piece in got:
        total = total + piece.astype(F32)
    summed = total.astype(BF16)
    chunks = [summed] + [swap(summed, "tensor", peer) for peer in range(1, parts)]

    lengths, out_rows = doc_lengths[0], owner_rows[0]
    indices = jnp.arange(maxdoc, dtype=jnp.int32)
    starts = jnp.sum(jnp.where(indices[:, None] < indices[None, :], lengths[:, None], 0), axis=0)
    low = maxdoc // 4
    ends = jnp.broadcast_to((starts + lengths)[:, None], (maxdoc, 128))
    scaling = 1.0 / jnp.sqrt(jnp.maximum(lengths, 1).astype(F32))
    scale = jnp.repeat(scaling.reshape(4, low).T, proj_in.shape[1], axis=1)

    per_owner = max(1, maxdoc // devices)
    height = -(-2 * per_owner // 8) * 8
    owners, out_slot = out_rows // maxdoc, out_rows % maxdoc
    earlier = (owners[None, :] == owners[:, None]) & (indices[None, :] < indices[:, None])
    target = owners * height + jnp.sum(earlier.astype(jnp.int32), axis=1)
    at = jnp.arange(devices * height, dtype=jnp.int32)
    select = (target[None, :] == at[:, None]).astype(BF16)
    label = jnp.where(lengths > 0, out_slot, -1)
    labels = jnp.sum(
        jnp.where(target[None, :] + per_owner == at[:, None], label[None, :], 0), axis=1
    )
    labels = jnp.broadcast_to(labels.astype(F32)[:, None], (devices * height, nval))
    place = jnp.concatenate(
        [part ^ jnp.arange(parts, dtype=jnp.int32), me ^ jnp.array(order, jnp.int32)]
    )

    payload = score(place, ends, scale, select, labels, chunks, halves, nval, low)
    got_rows = lax.all_to_all(
        payload.reshape(devices, height, nval), "dp", split_axis=0, concat_axis=0, tiled=True
    )
    data = got_rows[:, :per_owner].reshape(devices * per_owner, nval)
    tags = got_rows[:, per_owner : 2 * per_owner, :maxdoc].reshape(devices * per_owner, maxdoc)
    choose = (tags.astype(F32) == indices.astype(F32)[None, :]).astype(BF16)
    return lax.dot_general(
        choose, data, (((0,), (0,)), ((), ())), preferred_element_type=F32
    ).astype(BF16)


def solution(mesh):
    placed = (
        P("dp", "tensor"),
        P("dp", "tensor"),
        P("tensor", None),
        P("tensor", None),
        P("tensor", "dp"),
        P("dp", None),
        P("dp", None),
    )
    return jax.shard_map(
        shards, mesh=mesh, in_specs=placed, out_specs=P("dp", "tensor"), check_vma=False
    )
```

time: 56.5 us -> 52.6 us (0.931)
  Pallas kernels: 18.2 us -> 14.7 us
  other arithmetic: 1.26 us -> 0.58 us
    pallas_call x3, Pallas kernels: 18.2 us -> 14.7 us  [the longest x2 11.6 us: project(): pl.pallas_call(functools.partial(project_kernel, last, per_chunk, ahead),...]
    xor x1 -> x0, other arithmetic: 0.69 us -> none  [shards(): near = part ^ jnp.array(peers, jnp.int32)]
  transfers between devices with their start and end apart: 10 -> 10, of which waited for: 5 -> 5; matrix products, arithmetic and copies ran while one was open for 1% -> 2% of each run, Pallas kernels for 7% -> 8%
where the time goes in v3:
time: 52.6 us; the launch traced here: 52.4 us
  waiting for transfers between devices  18.2 us (35%)
  starting transfers between devices  17.5 us (33%)
  Pallas kernels  14.7 us (28%)
  matrix products  0.8 us (2%)
  other arithmetic  0.58 us (1%)
  local copies, waits for them, and re-layouts  0.53 us (1%)
    ppermute x9, starting transfers between devices, swap(): lax.ppermute(x, axis, [(i, i ^ k) for i in range(lax.axis_size(axis))])  13.7 us
    ppermute x9, waiting for transfers between devices, swap(): lax.ppermute(x, axis, [(i, i ^ k) for i in range(lax.axis_size(axis))])  13.4 us
    pallas_call x2, Pallas kernels, project(): pl.pallas_call(functools.partial(project_kernel, last, per_chunk, ahead),...  11.6 us
    all_to_all x1, waiting for transfers between devices, shards(): lax.all_to_all(payload.reshape(devices, height, nval), 'dp', split_axis=0...  4.75 us
    all_to_all x1, starting transfers between devices, shards(): lax.all_to_all(payload.reshape(devices, height, nval), 'dp', split_axis=0...  3.73 us
    pallas_call x1, Pallas kernels, score(): pl.pallas_call(functools.partial(score_kernel, len(chunks), low), out_sha...  3.06 us
  transfers between devices with their start and end apart: 10, of which 5 were waited for; matrix products, arithmetic and copies ran while one was open for 2% of the time, Pallas kernels for 8%

profile of v3, /device:TPU:0, one launch (start us, length us, event | category | flops | bytes accessed | tf_op | source)
XLA Modules:
  0.0 52.4 jit_solution(12047805377655202306)
XLA Ops:
  0.0 7.6 %shard_map.82 = bf16[3,128,256]{2,1,0:T(8,128)(2,1)S(1)} custom-call(s32[1]{0:T(128)} %bitcast.8.chunk_ref, bf16[1024,7168]{1,0:T(8,128)(2,1)} %act_hbm.3, bf16[1024,2048]{1,0:T(8,128)(2,1)} %grad_hbm.3, bf16[64,7168]{1,0:T(8,128)(2,1)} %bitcast.41, bf16[64,2048]{1,0:T(8,128)(2,1)} %bitcast.43), custom_call_target="tpu_custom_call" | custom-call | flops 905969664 | bytes 14155776 | tf_op jit(solution)/shard_map/pallas_call | solution.py:69
  7.6 5.2 %collective-permute-start = (bf16[128,256]{1,0:T(8,128)(2,1)S(1)}, bf16[128,256]{1,0:T(8,128)(2,1)S(1)}, u32[]{:S(2)}, u32[]{:S(2)}) collective-permute-start(bf16[128,256]{1,0:T(8,128)(2,1)S(1)} %get-tuple-element.7), channel_id=1, source_target_pairs={{0,3},{1,2},{2,1},{3,0},{4,7},{5,6},{6,5},{7,4},{8,11},{9,10},{10,... | collective-permute-start | bytes 196616 | tf_op jit(solution)/shard_map/ppermute | solution.py:21
  12.8 0.0 collective-permute-start.1
  12.8 0.6 %collective-permute-start.2 = (bf16[128,256]{1,0:T(8,128)(2,1)S(1)}, bf16[128,256]{1,0:T(8,128)(2,1)S(1)}, u32[]{:S(2)}, u32[]{:S(2)}) collective-permute-start(bf16[128,256]{1,0:T(8,128)(2,1)S(1)} %get-tuple-element.8), channel_id=1, source_target_pairs={{0,1},{1,0},{2,3},{3,2},{4,5},{5,4},{6,7},{7,6},{8,9},{9,8},{10,11... | collective-permute-start | bytes 196616 | tf_op jit(solution)/shard_map/ppermute | solution.py:21
  13.5 1.6 %collective-permute-start.6 = (bf16[128,512]{1,0:T(8,128)(2,1)S(1)}, bf16[128,512]{1,0:T(8,128)(2,1)S(1)}, u32[]{:S(2)}, u32[]{:S(2)}) collective-permute-start(bf16[128,512]{1,0:T(8,128)(2,1)S(1)} %copy-done), channel_id=1, source_target_pairs={{0,8},{4,12},{8,0},{12,4},{16,24},{20,28},{24,16},{28,20},{1,9},{5... | collective-permute-start | bytes 393224 | tf_op jit(solution)/shard_map/ppermute | solution.py:21
  15.2 0.2 convert_reduce_fusion
  15.4 0.1 select_reduce_fusion.1
  15.5 3.0 %collective-permute-done.6 = bf16[128,512]{1,0:T(8,128)(2,1)S(1)} collective-permute-done((bf16[128,512]{1,0:T(8,128)(2,1)S(1)}, bf16[128,512]{1,0:T(8,128)(2,1)S(1)}, u32[]{:S(2)}, u32[]{:S(2)}) %collective-permute-start.6) | collective-permute-done | bytes 131104 | tf_op jit(solution)/shard_map/ppermute | solution.py:21
  18.5 1.7 %collective-permute-start.7 = (bf16[256,512]{1,0:T(8,128)(2,1)S(1)}, bf16[256,512]{1,0:T(8,128)(2,1)S(1)}, u32[]{:S(2)}, u32[]{:S(2)}) collective-permute-start(bf16[256,512]{1,0:T(8,128)(2,1)S(1)} %pad_maximum_fusion), channel_id=1, source_target_pairs={{0,16},{4,20},{8,24},{12,28},{16,0},{20,4},{24,8},{28,12},{1,17},{... | collective-permute-start | bytes 786440 | tf_op jit(solution)/shard_map/ppermute | solution.py:21
  20.2 0.1 select_reduce_fusion
  20.3 4.8 %collective-permute-done.7 = bf16[256,512]{1,0:T(8,128)(2,1)S(1)} collective-permute-done((bf16[256,512]{1,0:T(8,128)(2,1)S(1)}, bf16[256,512]{1,0:T(8,128)(2,1)S(1)}, u32[]{:S(2)}, u32[]{:S(2)}) %collective-permute-start.7) | collective-permute-done | bytes 262176 | tf_op jit(solution)/shard_map/ppermute | solution.py:21
  25.2 0.1 collective-permute-start.8
  25.3 0.1 sqrt.6
  25.4 0.1 copy.14
  25.5 0.1 broadcast_in_dim.61
  25.6 0.1 reshape.68.scale_ref
  25.6 4.0 %shard_map.83 = bf16[1,128,256]{2,1,0:T(8,128)(2,1)S(1)} custom-call(s32[1]{0:T(128)} %bitcast.8.chunk_ref, bf16[1024,7168]{1,0:T(8,128)(2,1)} %act_hbm.3, bf16[1024,2048]{1,0:T(8,128)(2,1)} %grad_hbm.3, bf16[64,7168]{1,0:T(8,128)(2,1)} %bitcast.42, bf16[64,2048]{1,0:T(8,128)(2,1)} %bitcast.44), custom_call_target="tpu_custom_call" | custom-call | flops 301989888 | bytes 4718592 | tf_op jit(solution)/shard_map/pallas_call | solution.py:69
  29.7 0.0 collective-permute-done.1
  29.7 0.0 collective-permute-done.2
  29.7 1.3 %collective-permute-start.3 = (bf16[128,256]{1,0:T(8,128)(2,1)S(1)}, bf16[128,256]{1,0:T(8,128)(2,1)S(1)}, u32[]{:S(2)}, u32[]{:S(2)}) collective-permute-start(bf16[128,256]{1,0:T(8,128)(2,1)S(1)} %fusion.3.refs_0_), channel_id=1, source_target_pairs={{0,1},{1,0},{2,3},{3,2},{4,5},{5,4},{6,7},{7,6},{8,9},{9,8},{10,11... | collective-permute-start | bytes 196616 | tf_op jit(solution)/shard_map/ppermute | solution.py:21
  31.1 2.8 %collective-permute-start.4 = (bf16[128,256]{1,0:T(8,128)(2,1)S(1)}, bf16[128,256]{1,0:T(8,128)(2,1)S(1)}, u32[]{:S(2)}, u32[]{:S(2)}) collective-permute-start(bf16[128,256]{1,0:T(8,128)(2,1)S(1)} %fusion.3.refs_0_), channel_id=1, source_target_pairs={{0,2},{1,3},{2,0},{3,1},{4,6},{5,7},{6,4},{7,5},{8,10},{9,11},{10,... | collective-permute-start | bytes 196616 | tf_op jit(solution)/shard_map/ppermute | solution.py:21
  33.8 0.4 collective-permute-start.5
  34.2 0.1 pad_add_fusion.place_ref
  34.3 0.0 collective-permute-done.3.refs_1_
  34.3 3.9 %collective-permute-done.4.refs_2_ = bf16[128,256]{1,0:T(8,128)(2,1)S(1)} collective-permute-done((bf16[128,256]{1,0:T(8,128)(2,1)S(1)}, bf16[128,256]{1,0:T(8,128)(2,1)S(1)}, u32[]{:S(2)}, u32[]{:S(2)}) %collective-permute-start.4) | collective-permute-done | bytes 65568 | tf_op jit(solution)/shard_map/ppermute | solution.py:21
  38.1 1.8 %collective-permute-done.5.refs_3_ = bf16[128,256]{1,0:T(8,128)(2,1)S(1)} collective-permute-done((bf16[128,256]{1,0:T(8,128)(2,1)S(1)}, bf16[128,256]{1,0:T(8,128)(2,1)S(1)}, u32[]{:S(2)}, u32[]{:S(2)}) %collective-permute-start.5) | collective-permute-done | bytes 65568 | tf_op jit(solution)/shard_map/ppermute | solution.py:21
  39.9 0.1 broadcast_in_dim.65.labels_ref
  40.0 0.1 broadcast_in_dim.60.ends_ref
  40.0 3.1 %score.1 = bf16[64,128]{1,0:T(8,128)(2,1)} custom-call(s32[12]{0:T(128)S(1)} %pad_add_fusion.place_ref, s32[32,128]{1,0:T(8,128)S(1)} %broadcast_in_dim.60.ends_ref, f32[8,256]{1,0:T(8,128)S(1)} %reshape.68.scale_ref, bf16[64,32]{1,0:T(8,128)(2,1)S(1)} %fusion.4.select_ref, f32[64,128]{1,0:T(8,128)S(1)} %broadcast_in_dim.65.labels_ref, ...), custom_call_target="tpu_custom_call" | custom-call | flops 301989888 | bytes 1048576 | tf_op jit(solution)/shard_map/score/pallas_call | solution.py:149
  43.1 3.7 %all-to-all-start = ((bf16[8,8,128]{2,1,0:T(8,128)(2,1)}), bf16[8,8,128]{2,1,0:T(8,128)(2,1)S(1)}, u32[]{:S(2)}, u32[]{:S(2)}) async-start(bf16[8,8,128]{2,1,0:T(8,128)(2,1)} %bitcast.15), calls=%async_computation | async-start | bytes 32768 | tf_op jit(solution)/shard_map/all_to_all | solution.py:220
  46.8 4.7 %all-to-all-done = bf16[8,8,128]{2,1,0:T(8,128)(2,1)S(1)} async-done(((bf16[8,8,128]{2,1,0:T(8,128)(2,1)}), bf16[8,8,128]{2,1,0:T(8,128)(2,1)S(1)}, u32[]{:S(2)}, u32[]{:S(2)}) %all-to-all-start) | async-done | bytes 16416 | tf_op jit(solution)/shard_map/all_to_all | solution.py:220
  51.6 0.8 %fusion = bf16[32,128]{1,0:T(8,128)(2,1)} fusion(bf16[8,8,128]{2,1,0:T(8,128)(2,1)S(1)} %all-to-all-done, f32[32]{0:T(128)S(1)} %iota_convert_fusion), kind=kOutput, calls=%fused_computation.1 | convolution fusion | flops 268288 | bytes 24704 | tf_op jit(solution)/shard_map/dot_general | solution.py:226
  (26 shorter events, 0.2 us)
Async XLA Ops:
  0.0 15.5 %copy-start.3 = (s32[8]{0:T(128)S(1)}, s32[8]{0:T(128)}, u32[]{:S(2)}) copy-start(s32[8]{0:T(128)} %constant.48.clone) | copy-start | bytes 100
  0.0 13.5 %copy-start = (bf16[128,512]{1,0:T(8,128)(2,1)S(1)}, bf16[128,512]{1,0:T(8,128)(2,1)}, u32[]{:S(2)}) copy-start(bf16[128,512]{1,0:T(8,128)(2,1)} %param.12) | copy-start | bytes 393220
  0.0 15.1 %copy-start.1 = (s32[1,32]{1,0:T(1,128)S(1)}, s32[1,32]{1,0:T(1,128)}, u32[]{:S(2)}) copy-start(s32[1,32]{1,0:T(1,128)} %param.14) | copy-start | bytes 388
  0.0 15.1 %copy-start.2 = (s32[1,32]{1,0:T(1,128)S(1)}, s32[1,32]{1,0:T(1,128)}, u32[]{:S(2)}) copy-start(s32[1,32]{1,0:T(1,128)} %param.13) | copy-start | bytes 388
  7.6 22.0 %collective-permute-start = (bf16[128,256]{1,0:T(8,128)(2,1)S(1)}, bf16[128,256]{1,0:T(8,128)(2,1)S(1)}, u32[]{:S(2)}, u32[]{:S(2)}) collective-permute-start(bf16[128,256]{1,0:T(8,128)(2,1)S(1)} %get-tuple-element.7), channel_id=1, source_target_pairs={{0,3},{1,2},{2,1},{3,0},{4,7},{5,6},{6,5},{7,4},{8,11},{9,10},{10,... | collective-permute-start | bytes 196616 | tf_op jit(solution)/shard_map/ppermute | solution.py:21
  12.8 16.8 %collective-permute-start.1 = (bf16[128,256]{1,0:T(8,128)(2,1)S(1)}, bf16[128,256]{1,0:T(8,128)(2,1)S(1)}, u32[]{:S(2)}, u32[]{:S(2)}) collective-permute-start(bf16[128,256]{1,0:T(8,128)(2,1)S(1)} %get-tuple-element.9), channel_id=1, source_target_pairs={{0,2},{1,3},{2,0},{3,1},{4,6},{5,7},{6,4},{7,5},{8,10},{9,11},{10,... | collective-permute-start | bytes 196616 | tf_op jit(solution)/shard_map/ppermute | solution.py:21
  12.8 16.8 %collective-permute-start.2 = (bf16[128,256]{1,0:T(8,128)(2,1)S(1)}, bf16[128,256]{1,0:T(8,128)(2,1)S(1)}, u32[]{:S(2)}, u32[]{:S(2)}) collective-permute-start(bf16[128,256]{1,0:T(8,128)(2,1)S(1)} %get-tuple-element.8), channel_id=1, source_target_pairs={{0,1},{1,0},{2,3},{3,2},{4,5},{5,4},{6,7},{7,6},{8,9},{9,8},{10,11... | collective-permute-start | bytes 196616 | tf_op jit(solution)/shard_map/ppermute | solution.py:21
  13.5 5.0 %collective-permute-start.6 = (bf16[128,512]{1,0:T(8,128)(2,1)S(1)}, bf16[128,512]{1,0:T(8,128)(2,1)S(1)}, u32[]{:S(2)}, u32[]{:S(2)}) collective-permute-start(bf16[128,512]{1,0:T(8,128)(2,1)S(1)} %copy-done), channel_id=1, source_target_pairs={{0,8},{4,12},{8,0},{12,4},{16,24},{20,28},{24,16},{28,20},{1,9},{5... | collective-permute-start | bytes 393224 | tf_op jit(solution)/shard_map/ppermute | solution.py:21
  18.5 6.7 %collective-permute-start.7 = (bf16[256,512]{1,0:T(8,128)(2,1)S(1)}, bf16[256,512]{1,0:T(8,128)(2,1)S(1)}, u32[]{:S(2)}, u32[]{:S(2)}) collective-permute-start(bf16[256,512]{1,0:T(8,128)(2,1)S(1)} %pad_maximum_fusion), channel_id=1, source_target_pairs={{0,16},{4,20},{8,24},{12,28},{16,0},{20,4},{24,8},{28,12},{1,17},{... | collective-permute-start | bytes 786440 | tf_op jit(solution)/shard_map/ppermute | solution.py:21
  25.2 14.7 %collective-permute-start.8 = (bf16[512,512]{1,0:T(8,128)(2,1)S(1)}, bf16[512,512]{1,0:T(8,128)(2,1)S(1)}, u32[]{:S(2)}, u32[]{:S(2)}) collective-permute-start(bf16[512,512]{1,0:T(8,128)(2,1)S(1)} %constant_dynamic-update-slice_fusion.refs_4_), channel_id=1, source_target_pairs={{0,4},{4,0},{8,12},{12,8},{16,20},{20,16},{24,28},{28,24},{1,5},{5... | collective-permute-start | bytes 1572872 | tf_op jit(solution)/shard_map/ppermute | solution.py:21
  29.7 4.5 %collective-permute-start.3 = (bf16[128,256]{1,0:T(8,128)(2,1)S(1)}, bf16[128,256]{1,0:T(8,128)(2,1)S(1)}, u32[]{:S(2)}, u32[]{:S(2)}) collective-permute-start(bf16[128,256]{1,0:T(8,128)(2,1)S(1)} %fusion.3.refs_0_), channel_id=1, source_target_pairs={{0,1},{1,0},{2,3},{3,2},{4,5},{5,4},{6,7},{7,6},{8,9},{9,8},{10,11... | collective-permute-start | bytes 196616 | tf_op jit(solution)/shard_map/ppermute | solution.py:21
  31.1 7.1 %collective-permute-start.4 = (bf16[128,256]{1,0:T(8,128)(2,1)S(1)}, bf16[128,256]{1,0:T(8,128)(2,1)S(1)}, u32[]{:S(2)}, u32[]{:S(2)}) collective-permute-start(bf16[128,256]{1,0:T(8,128)(2,1)S(1)} %fusion.3.refs_0_), channel_id=1, source_target_pairs={{0,2},{1,3},{2,0},{3,1},{4,6},{5,7},{6,4},{7,5},{8,10},{9,11},{10,... | collective-permute-start | bytes 196616 | tf_op jit(solution)/shard_map/ppermute | solution.py:21
  33.8 6.1 %collective-permute-start.5 = (bf16[128,256]{1,0:T(8,128)(2,1)S(1)}, bf16[128,256]{1,0:T(8,128)(2,1)S(1)}, u32[]{:S(2)}, u32[]{:S(2)}) collective-permute-start(bf16[128,256]{1,0:T(8,128)(2,1)S(1)} %fusion.3.refs_0_), channel_id=1, source_target_pairs={{0,3},{1,2},{2,1},{3,0},{4,7},{5,6},{6,5},{7,4},{8,11},{9,10},{10,... | collective-permute-start | bytes 196616 | tf_op jit(solution)/shard_map/ppermute | solution.py:21
  43.1 8.5 %all-to-all-start = ((bf16[8,8,128]{2,1,0:T(8,128)(2,1)}), bf16[8,8,128]{2,1,0:T(8,128)(2,1)S(1)}, u32[]{:S(2)}, u32[]{:S(2)}) async-start(bf16[8,8,128]{2,1,0:T(8,128)(2,1)} %bitcast.15), calls=%async_computation | async-start | bytes 32768 | tf_op jit(solution)/shard_map/all_to_all | solution.py:220

commit v4 on v3

v4 whole, which is shorter than its diff:
```python
import functools

import jax
import jax.numpy as jnp
from jax import lax
from jax.experimental import pallas as pl
from jax.experimental.pallas import tpu as pltpu
from jax.sharding import PartitionSpec as P


BF16, F32 = jnp.bfloat16, jnp.float32
NT = (((1,), (1,)), ((), ()))
VMEM_LIMIT = 24 << 20


def far(x):
    return pltpu.with_memory_space_constraint(x, pltpu.HBM)


def swap(x, axis, k):
    return lax.ppermute(x, axis, [(i, i ^ k) for i in range(lax.axis_size(axis))])


def both_projections(act, grad, wa, wg):
    left = lax.dot_general(act, wa, NT, preferred_element_type=F32)
    right = lax.dot_general(grad, wg, NT, preferred_element_type=F32)
    return jnp.concatenate([left, right], axis=1).T.astype(BF16)


def peers_kernel(
    ahead, act_hbm, grad_hbm, wa_hbm, wg_hbm, out_ref, grad_own, wa, wg, act, grad, sem, wsem
):
    count, rows = act.shape[0], act.shape[1]
    part = lax.axis_index("tensor")

    def rows_of(chunk):
        return pl.ds(pl.multiple_of(chunk * rows, rows), rows)

    def copies(i):
        at = rows_of(part ^ (count - i))
        return (
            pltpu.make_async_copy(grad_hbm.at[at], grad.at[i], sem.at[0, i]),
            pltpu.make_async_copy(act_hbm.at[at], act.at[i], sem.at[1, i]),
        )

    weights = (
        pltpu.make_async_copy(wg_hbm, wg, wsem.at[0]),
        pltpu.make_async_copy(wa_hbm, wa, wsem.at[1]),
    )
    own = pltpu.make_async_copy(grad_hbm.at[rows_of(part)], grad_own, wsem.at[2])
    for copy in weights:
        copy.start()
    for i in range(min(ahead, count)):
        for copy in copies(i):
            copy.start()
    for copy in weights:
        copy.wait()

    def step(i, carry):
        for copy in copies(i):
            copy.wait()

        @pl.when(i + ahead < count)
        def _():
            for copy in copies(i + ahead):
                copy.start()

        @pl.when(i + ahead == count)
        def _():
            own.start()

        out_ref[i] = both_projections(act[i], grad[i], wa[...], wg[...])
        return carry

    lax.fori_loop(0, count, step, 0)
    own.wait()


def project_peers(parts, activations, out_grads, wa, wg):
    (tokens, ff), d, k = activations.shape, out_grads.shape[1], wa.shape[0]
    rows, count = tokens // parts, parts - 1
    hbm, vmem = pl.BlockSpec(memory_space=pl.ANY), pl.BlockSpec(memory_space=pltpu.VMEM)
    return pl.pallas_call(
        functools.partial(peers_kernel, min(2, count)),
        out_shape=[
            jax.ShapeDtypeStruct(shape, BF16)
            for shape in ((count, 2 * k, rows), (rows, d), (k, ff), (k, d))
        ],
        in_specs=[hbm] * 4,
        out_specs=[vmem] * 4,
        scratch_shapes=[
            pltpu.VMEM((count, rows, ff), BF16),
            pltpu.VMEM((count, rows, d), BF16),
            pltpu.SemaphoreType.DMA((2, count)),
            pltpu.SemaphoreType.DMA((3,)),
        ],
        compiler_params=pltpu.CompilerParams(vmem_limit_bytes=VMEM_LIMIT),
        cost_estimate=pl.CostEstimate(
            flops=2 * tokens * (ff + d) * k, bytes_accessed=2 * tokens * (ff + d), transcendentals=0
        ),
        name="project_peers",
    )(far(activations), far(out_grads), far(wa), far(wg))


def own_kernel(act_hbm, grad_ref, wa_ref, wg_ref, out_ref, act, sem):
    blocks, rows = act.shape[0], act.shape[1]
    part = lax.axis_index("tensor")

    def copy(i):
        start = pl.multiple_of((part * blocks + i) * rows, rows)
        return pltpu.make_async_copy(act_hbm.at[pl.ds(start, rows)], act.at[i], sem.at[i])

    for i in range(blocks):
        copy(i).start()

    def step(i, carry):
        copy(i).wait()
        at = pl.ds(pl.multiple_of(i * rows, rows), rows)
        out_ref[:, at] = both_projections(act[i], grad_ref[at, :], wa_ref[...], wg_ref[...])
        return carry

    lax.fori_loop(0, blocks, step, 0)


def project_own(activations, grad, wa, wg, blocks):
    hbm, vmem = pl.BlockSpec(memory_space=pl.ANY), pl.BlockSpec(memory_space=pltpu.VMEM)
    ff, (rows, d), k = activations.shape[1], grad.shape, wa.shape[0]
    return pl.pallas_call(
        own_kernel,
        out_shape=jax.ShapeDtypeStruct((2 * k, rows), BF16),
        in_specs=[hbm] + [vmem] * 3,
        out_specs=vmem,
        scratch_shapes=[
            pltpu.VMEM((blocks, rows // blocks, ff), BF16),
            pltpu.SemaphoreType.DMA((blocks,)),
        ],
        compiler_params=pltpu.CompilerParams(vmem_limit_bytes=VMEM_LIMIT),
        cost_estimate=pl.CostEstimate(
            flops=2 * rows * (ff + d) * k, bytes_accessed=2 * rows * (ff + d), transcendentals=0
        ),
        name="project_own",
    )(far(activations), grad, wa, wg)


def score_kernel(n_chunks, low, n_blocks, ends_ref, scale_ref, select_ref, labels_ref, *refs):
    chunks, held = refs[:n_chunks], refs[n_chunks : n_chunks + 2]
    out_ref, acts, left, right, outer, sketch = refs[n_chunks + 2 :]
    k, rows = chunks[0].shape[0] // 2, chunks[0].shape[1]
    high = outer.shape[0] * outer.shape[2] // k
    docs = low * high
    part, me = lax.axis_index("tensor"), lax.axis_index("dp")
    for c, ref in enumerate(chunks):
        at = (part ^ c) * rows + lax.broadcasted_iota(jnp.int32, (docs, rows), 1)
        doc = jnp.sum((at >= ends_ref[:, :1]).astype(F32), axis=0, keepdims=True)
        div = jnp.floor(doc * (1.0 / low))
        of_mod = lax.broadcasted_iota(jnp.int32, (low, rows), 0).astype(F32)
        mod = (jnp.broadcast_to(doc - div * low, (low, rows)) == of_mod).astype(F32)
        span = slice(c * rows, (c + 1) * rows)
        acts[...] = ref[:k, :].astype(F32)
        for i in range(0, k, 2):
            pair = [jnp.broadcast_to(acts[j : j + 1, :], (low, rows)) * mod for j in (i, i + 1)]
            left[i * low : (i + 2) * low, span] = jnp.concatenate(pair, axis=0).astype(BF16)
        for m in range(high):
            mask = jnp.broadcast_to((div == m).astype(F32), (k, rows)).astype(BF16)
            right[m * k : (m + 1) * k, span] = ref[k:, :] * mask
    lanes = outer.shape[2]
    sums = lax.dot_general(left[...], right[...], NT, preferred_element_type=F32)
    for m in range(outer.shape[0]):
        outer[m] = sums[:, m * lanes : (m + 1) * lanes]

    first = lax.broadcasted_iota(jnp.int32, (low, lanes), 1) < k
    per_block = k // n_blocks
    for m in range(outer.shape[0]):
        scale = scale_ref[:, m * lanes : (m + 1) * lanes]
        for i in range(0, k, 2):
            even = outer[m, i * low : (i + 1) * low, :] * scale
            odd = outer[m, (i + 1) * low : (i + 2) * low, :] * scale
            pair = [
                jnp.where(first, even, pltpu.roll(odd, k, 1)),
                jnp.where(first, pltpu.roll(even, k, 1), odd),
            ]
            apart = me ^ (i // per_block)
            at = (apart // 2 + apart % 2 * (n_blocks // 2)) * (per_block * k) + i % per_block * k
            rows_at = slice(2 * m * low, 2 * (m + 1) * low)
            sketch[rows_at, pl.ds(pl.multiple_of(at, lanes), lanes)] = jnp.concatenate(pair, axis=0).astype(BF16)

    half = held[0].shape[1]
    local = sum(
        lax.dot_general(
            ref[...], sketch[:, h * half : (h + 1) * half], NT, preferred_element_type=F32
        )
        for h, ref in enumerate(held)
    )
    packed = lax.dot_general(
        select_ref[...], local.astype(BF16), NT, preferred_element_type=F32
    )
    out_ref[...] = (packed + labels_ref[...]).astype(BF16)


def score(ends, scale, select, labels, chunks, held, nval, low, n_blocks):
    k, rows = chunks[0].shape[0] // 2, chunks[0].shape[1]
    tokens = len(chunks) * rows
    docs = ends.shape[0]
    high = docs // low
    vmem = pl.BlockSpec(memory_space=pltpu.VMEM)
    return pl.pallas_call(
        functools.partial(score_kernel, len(chunks), low, n_blocks),
        out_shape=jax.ShapeDtypeStruct((select.shape[0], nval), BF16),
        in_specs=[vmem] * (4 + len(chunks) + 2),
        out_specs=vmem,
        scratch_shapes=[
            pltpu.VMEM((k, rows), F32),
            pltpu.VMEM((low * k, tokens), BF16),
            pltpu.VMEM((high * k, tokens), BF16),
            pltpu.VMEM((high // 2, low * k, 2 * k), F32),
            pltpu.VMEM((docs, k * k), BF16),
        ],
        compiler_params=pltpu.CompilerParams(vmem_limit_bytes=16 << 20),
        cost_estimate=pl.CostEstimate(
            flops=2 * k * k * docs * (tokens + nval), bytes_accessed=2 * k * k * nval, transcendentals=0
        ),
        name="score",
    )(ends, scale, select, labels, *chunks, *held)


def shards(activations, out_grads, proj_in, proj_out, validation, doc_lengths, owner_rows):
    devices, parts = lax.axis_size("dp"), lax.axis_size("tensor")
    maxdoc = doc_lengths.shape[1]

    nval = validation.shape[0]
    held = validation
    bits = [1 << i for i in range(devices.bit_length() - 1)]
    for bit in bits[1:]:
        held = jnp.concatenate([held, swap(held, "dp", bit)], axis=1)
    halves = (held, swap(held, "dp", bits[0]))

    wa, wg = proj_in.T, proj_out.T
    peers = list(range(parts - 1, 0, -1))
    sent, *kept = project_peers(parts, activations, out_grads, wa, wg)
    got = [swap(sent[i], "tensor", peer) for i, peer in enumerate(peers)]
    total = project_own(activations, *kept, 2).astype(F32)
    for piece in got:
        total = total + piece.astype(F32)
    summed = total.astype(BF16)
    summed, lengths, out_rows = lax.optimization_barrier((summed, doc_lengths[0], owner_rows[0]))
    chunks = [summed] + [swap(summed, "tensor", peer) for peer in range(1, parts)]

    indices = jnp.arange(maxdoc, dtype=jnp.int32)
    starts = jnp.sum(jnp.where(indices[:, None] < indices[None, :], lengths[:, None], 0), axis=0)
    low = maxdoc // 4
    ends = jnp.broadcast_to((starts + lengths)[:, None], (maxdoc, 128))
    scaling = 1.0 / jnp.sqrt(jnp.maximum(lengths, 1).astype(F32))
    scale = jnp.repeat(scaling.reshape(4, low).T, proj_in.shape[1], axis=1)

    per_owner = max(1, maxdoc // devices)
    height = -(-2 * per_owner // 8) * 8
    owners, out_slot = out_rows // maxdoc, out_rows % maxdoc
    earlier = (owners[None, :] == owners[:, None]) & (indices[None, :] < indices[:, None])
    target = owners * height + jnp.sum(earlier.astype(jnp.int32), axis=1)
    at = jnp.arange(devices * height, dtype=jnp.int32)
    select = (target[None, :] == at[:, None]).astype(BF16)
    label = jnp.where(lengths > 0, out_slot, -1)
    labels = jnp.sum(
        jnp.where(target[None, :] + per_owner == at[:, None], label[None, :], 0), axis=1
    )
    labels = jnp.broadcast_to(labels.astype(F32)[:, None], (devices * height, nval))

    payload = score(ends, scale, select, labels, chunks, halves, nval, low, devices)
    got_rows = lax.all_to_all(
        payload.reshape(devices, height, nval), "dp", split_axis=0, concat_axis=0, tiled=True
    )
    data = got_rows[:, :per_owner].reshape(devices * per_owner, nval)
    tags = got_rows[:, per_owner : 2 * per_owner, :maxdoc].reshape(devices * per_owner, maxdoc)
    choose = (tags.astype(F32) == indices.astype(F32)[None, :]).astype(BF16)
    return lax.dot_general(
        choose, data, (((0,), (0,)), ((), ())), preferred_element_type=F32
    ).astype(BF16)


def solution(mesh):
    placed = (
        P("dp", "tensor"),
        P("dp", "tensor"),
        P("tensor", None),
        P("tensor", None),
        P("tensor", "dp"),
        P("dp", None),
        P("dp", None),
    )
    return jax.shard_map(
        shards, mesh=mesh, in_specs=placed, out_specs=P("dp", "tensor"), check_vma=False
    )
```

time: 52.6 us -> 44.4 us (0.84)
  waiting for transfers between devices: 18.2 us -> 11.7 us
  Pallas kernels: 14.7 us -> 13.3 us
    ppermute x9, waiting for transfers between devices: 13.4 us -> 6.9 us  [swap(): lax.ppermute(x, axis, [(i, i ^ k) for i in range(lax.axis_size(axis))])]
    pallas_call x3, Pallas kernels: 14.7 us -> 13.3 us  [the longest x1 7.62 us: project_peers(): pl.pallas_call(functools.partial(peers_kernel, min(2, count)), out_shape=...]
  transfers between devices with their start and end apart: 10 -> 10, of which waited for: 5 -> 3; matrix products, arithmetic and copies ran while one was open for 2% -> 2% of each run, Pallas kernels for 8% -> 8%
where the time goes in v4:
time: 44.4 us; the launch traced here: 44.2 us
  starting transfers between devices  17.4 us (39%)
  Pallas kernels  13.3 us (30%)
  waiting for transfers between devices  11.7 us (26%)
  matrix products  0.8 us (2%)
  local copies, waits for them, and re-layouts  0.53 us (1%)
  other arithmetic  0.46 us (1%)
    ppermute x9, starting transfers between devices, swap(): lax.ppermute(x, axis, [(i, i ^ k) for i in range(lax.axis_size(axis))])  13.5 us
    pallas_call x1, Pallas kernels, project_peers(): pl.pallas_call(functools.partial(peers_kernel, min(2, count)), out_shape=...  7.62 us
    ppermute x9, waiting for transfers between devices, swap(): lax.ppermute(x, axis, [(i, i ^ k) for i in range(lax.axis_size(axis))])  6.9 us
    all_to_all x1, waiting for transfers between devices, shards(): lax.all_to_all(payload.reshape(devices, height, nval), 'dp', split_axis=0...  4.75 us
    all_to_all x1, starting transfers between devices, shards(): lax.all_to_all(payload.reshape(devices, height, nval), 'dp', split_axis=0...  3.83 us
    pallas_call x1, Pallas kernels, project_own(): pl.pallas_call(own_kernel, out_shape=jax.ShapeDtypeStruct((2 * k, rows),...  3.32 us
    pallas_call x1, Pallas kernels, score(): pl.pallas_call(functools.partial(score_kernel, len(chunks), low, n_blocks...  2.32 us
  transfers between devices with their start and end apart: 10, of which 3 were waited for; matrix products, arithmetic and copies ran while one was open for 2% of the time, Pallas kernels for 8%

profile of v4, /device:TPU:0, one launch (start us, length us, event | category | flops | bytes accessed | tf_op | source)
XLA Modules:
  0.0 44.2 jit_solution(10679256073119030645)
XLA Ops:
  0.0 7.6 %project_peers.1 = (bf16[3,128,256]{2,1,0:T(8,128)(2,1)S(1)}, bf16[256,2048]{1,0:T(8,128)(2,1)S(1)}, bf16[64,7168]{1,0:T(8,128)(2,1)S(1)}, bf16[64,2048]{1,0:T(8,128)(2,1)S(1)}) custom-call(bf16[1024,7168]{1,0:T(8,128)(2,1)} %act_hbm.3, bf16[1024,2048]{1,0:T(8,128)(2,1)} %grad_hbm.1, bf16[64,7168]{1,0:T(8,128)(2,1)} %bitcast.16, bf16[64,2048]{1,0:T(8,128)(2,1)} %bitcast.17), custom_call_target="tpu_custom_call" | custom-call | flops 1207959552 | bytes 18874368 | tf_op jit(solution)/shard_map/project_peers/pallas_call | solution.py:83
  7.7 5.1 %collective-permute-start = (bf16[128,256]{1,0:T(8,128)(2,1)S(1)}, bf16[128,256]{1,0:T(8,128)(2,1)S(1)}, u32[]{:S(2)}, u32[]{:S(2)}) collective-permute-start(bf16[128,256]{1,0:T(8,128)(2,1)S(1)} %get-tuple-element.21), channel_id=1, source_target_pairs={{0,3},{1,2},{2,1},{3,0},{4,7},{5,6},{6,5},{7,4},{8,11},{9,10},{10,... | collective-permute-start | bytes 196616 | tf_op jit(solution)/shard_map/ppermute | solution.py:21
  12.8 0.0 collective-permute-start.1
  12.8 0.6 %collective-permute-start.2 = (bf16[128,256]{1,0:T(8,128)(2,1)S(1)}, bf16[128,256]{1,0:T(8,128)(2,1)S(1)}, u32[]{:S(2)}, u32[]{:S(2)}) collective-permute-start(bf16[128,256]{1,0:T(8,128)(2,1)S(1)} %get-tuple-element.22), channel_id=1, source_target_pairs={{0,1},{1,0},{2,3},{3,2},{4,5},{5,4},{6,7},{7,6},{8,9},{9,8},{10,11... | collective-permute-start | bytes 196616 | tf_op jit(solution)/shard_map/ppermute | solution.py:21
  13.4 1.6 %collective-permute-start.6 = (bf16[128,512]{1,0:T(8,128)(2,1)S(1)}, bf16[128,512]{1,0:T(8,128)(2,1)S(1)}, u32[]{:S(2)}, u32[]{:S(2)}) collective-permute-start(bf16[128,512]{1,0:T(8,128)(2,1)S(1)} %copy-done), channel_id=1, source_target_pairs={{0,8},{4,12},{8,0},{12,4},{16,24},{20,28},{24,16},{28,20},{1,9},{5... | collective-permute-start | bytes 393224 | tf_op jit(solution)/shard_map/ppermute | solution.py:21
  15.1 3.3 %project_own.1 = bf16[128,256]{1,0:T(8,128)(2,1)S(1)} custom-call(bf16[1024,7168]{1,0:T(8,128)(2,1)} %act_hbm.3, bf16[256,2048]{1,0:T(8,128)(2,1)S(1)} %get-tuple-element.12.grad_ref, bf16[64,7168]{1,0:T(8,128)(2,1)S(1)} %get-tuple-element.13.wa_ref, bf16[64,2048]{1,0:T(8,128)(2,1)S(1)} %get-tuple-element.14.wg_ref), custom_call_target="tpu_custom_call" | custom-call | flops 301989888 | bytes 4718592 | tf_op jit(solution)/shard_map/project_own/pallas_call | solution.py:128
  18.4 0.0 collective-permute-done
  18.4 0.0 collective-permute-done.1
  18.4 0.0 collective-permute-done.2
  18.5 1.3 %collective-permute-start.3 = (bf16[128,256]{1,0:T(8,128)(2,1)S(1)}, bf16[128,256]{1,0:T(8,128)(2,1)S(1)}, u32[]{:S(2)}, u32[]{:S(2)}) collective-permute-start(bf16[128,256]{1,0:T(8,128)(2,1)S(1)} %add_convert_fusion.refs_0_), channel_id=1, source_target_pairs={{0,1},{1,0},{2,3},{3,2},{4,5},{5,4},{6,7},{7,6},{8,9},{9,8},{10,11... | collective-permute-start | bytes 196616 | tf_op jit(solution)/shard_map/ppermute | solution.py:21
  19.8 2.9 %collective-permute-start.4 = (bf16[128,256]{1,0:T(8,128)(2,1)S(1)}, bf16[128,256]{1,0:T(8,128)(2,1)S(1)}, u32[]{:S(2)}, u32[]{:S(2)}) collective-permute-start(bf16[128,256]{1,0:T(8,128)(2,1)S(1)} %add_convert_fusion.refs_0_), channel_id=1, source_target_pairs={{0,2},{1,3},{2,0},{3,1},{4,6},{5,7},{6,4},{7,5},{8,10},{9,11},{10,... | collective-permute-start | bytes 196616 | tf_op jit(solution)/shard_map/ppermute | solution.py:21
  22.7 0.2 collective-permute-start.5
  23.0 0.1 select_reduce_fusion.1
  23.1 0.2 convert_reduce_fusion
  23.2 0.0 collective-permute-done.6
  23.3 1.6 %collective-permute-start.7 = (bf16[128,1024]{1,0:T(8,128)(2,1)S(1)}, bf16[128,1024]{1,0:T(8,128)(2,1)S(1)}, u32[]{:S(2)}, u32[]{:S(2)}) collective-permute-start(bf16[128,1024]{1,0:T(8,128)(2,1)S(1)} %pad_maximum_fusion), channel_id=1, source_target_pairs={{0,16},{4,20},{8,24},{12,28},{16,0},{20,4},{24,8},{28,12},{1,17},{... | collective-permute-start | bytes 786440 | tf_op jit(solution)/shard_map/ppermute | solution.py:21
  24.9 5.5 %collective-permute-done.7 = bf16[128,1024]{1,0:T(8,128)(2,1)S(1)} collective-permute-done((bf16[128,1024]{1,0:T(8,128)(2,1)S(1)}, bf16[128,1024]{1,0:T(8,128)(2,1)S(1)}, u32[]{:S(2)}, u32[]{:S(2)}) %collective-permute-start.7) | collective-permute-done | bytes 262176 | tf_op jit(solution)/shard_map/ppermute | solution.py:21
  30.4 0.1 collective-permute-start.8
  30.5 0.1 select_reduce_fusion
  30.6 0.1 reshape.32
  30.7 0.1 copy.13
  30.7 0.1 broadcast_in_dim.35
  30.8 0.1 reshape.33.scale_ref
  30.9 0.0 collective-permute-done.4.refs_2_
  30.9 0.0 collective-permute-done.5.refs_3_
  30.9 1.4 %collective-permute-done.8.refs_5_ = bf16[128,2048]{1,0:T(8,128)(2,1)S(1)} collective-permute-done((bf16[128,2048]{1,0:T(8,128)(2,1)S(1)}, bf16[128,2048]{1,0:T(8,128)(2,1)S(1)}, u32[]{:S(2)}, u32[]{:S(2)}) %collective-permute-start.8) | collective-permute-done | bytes 524320 | tf_op jit(solution)/shard_map/ppermute | solution.py:21
  32.3 0.1 broadcast_in_dim.38.labels_ref
  32.4 0.1 broadcast_in_dim.30.ends_ref
  32.5 2.3 %score.1 = bf16[64,128]{1,0:T(8,128)(2,1)} custom-call(s32[32,128]{1,0:T(8,128)S(1)} %broadcast_in_dim.30.ends_ref, f32[8,256]{1,0:T(8,128)S(1)} %reshape.33.scale_ref, bf16[64,32]{1,0:T(8,128)(2,1)S(1)} %fusion.1.select_ref, f32[64,128]{1,0:T(8,128)S(1)} %broadcast_in_dim.38.labels_ref, bf16[128,256]{1,0:T(8,128)(2,1)S(1)} %add_convert_fusion.refs_0_, ...), custom_call_target="tpu_custom_call" | custom-call | flops 301989888 | bytes 1048576 | tf_op jit(solution)/shard_map/score/pallas_call | solution.py:206
  34.8 3.8 %all-to-all-start = ((bf16[8,8,128]{2,1,0:T(8,128)(2,1)}), bf16[8,8,128]{2,1,0:T(8,128)(2,1)S(1)}, u32[]{:S(2)}, u32[]{:S(2)}) async-start(bf16[8,8,128]{2,1,0:T(8,128)(2,1)} %bitcast.8), calls=%async_computation | async-start | bytes 32768 | tf_op jit(solution)/shard_map/all_to_all | solution.py:269
  38.6 4.7 %all-to-all-done = bf16[8,8,128]{2,1,0:T(8,128)(2,1)S(1)} async-done(((bf16[8,8,128]{2,1,0:T(8,128)(2,1)}), bf16[8,8,128]{2,1,0:T(8,128)(2,1)S(1)}, u32[]{:S(2)}, u32[]{:S(2)}) %all-to-all-start) | async-done | bytes 16416 | tf_op jit(solution)/shard_map/all_to_all | solution.py:269
  43.4 0.8 %fusion = bf16[32,128]{1,0:T(8,128)(2,1)} fusion(bf16[8,8,128]{2,1,0:T(8,128)(2,1)S(1)} %all-to-all-done, f32[32]{0:T(128)S(1)} %iota_convert_fusion), kind=kOutput, calls=%fused_computation.1 | convolution fusion | flops 268288 | bytes 24704 | tf_op jit(solution)/shard_map/dot_general | solution.py:275
  (19 shorter events, 0.2 us)
Async XLA Ops:
  0.0 13.4 %copy-start = (bf16[128,512]{1,0:T(8,128)(2,1)S(1)}, bf16[128,512]{1,0:T(8,128)(2,1)}, u32[]{:S(2)}) copy-start(bf16[128,512]{1,0:T(8,128)(2,1)} %param.11) | copy-start | bytes 393220
  0.0 22.9 %copy-start.2 = (s32[1,32]{1,0:T(1,128)S(1)}, s32[1,32]{1,0:T(1,128)}, u32[]{:S(2)}) copy-start(s32[1,32]{1,0:T(1,128)} %param.12) | copy-start | bytes 388
  0.0 23.0 %copy-start.1 = (s32[1,32]{1,0:T(1,128)S(1)}, s32[1,32]{1,0:T(1,128)}, u32[]{:S(2)}) copy-start(s32[1,32]{1,0:T(1,128)} %param.13) | copy-start | bytes 388
  7.7 10.8 %collective-permute-start = (bf16[128,256]{1,0:T(8,128)(2,1)S(1)}, bf16[128,256]{1,0:T(8,128)(2,1)S(1)}, u32[]{:S(2)}, u32[]{:S(2)}) collective-permute-start(bf16[128,256]{1,0:T(8,128)(2,1)S(1)} %get-tuple-element.21), channel_id=1, source_target_pairs={{0,3},{1,2},{2,1},{3,0},{4,7},{5,6},{6,5},{7,4},{8,11},{9,10},{10,... | collective-permute-start | bytes 196616 | tf_op jit(solution)/shard_map/ppermute | solution.py:21
  12.8 5.6 %collective-permute-start.1 = (bf16[128,256]{1,0:T(8,128)(2,1)S(1)}, bf16[128,256]{1,0:T(8,128)(2,1)S(1)}, u32[]{:S(2)}, u32[]{:S(2)}) collective-permute-start(bf16[128,256]{1,0:T(8,128)(2,1)S(1)} %get-tuple-element.23), channel_id=1, source_target_pairs={{0,2},{1,3},{2,0},{3,1},{4,6},{5,7},{6,4},{7,5},{8,10},{9,11},{10,... | collective-permute-start | bytes 196616 | tf_op jit(solution)/shard_map/ppermute | solution.py:21
  12.8 5.6 %collective-permute-start.2 = (bf16[128,256]{1,0:T(8,128)(2,1)S(1)}, bf16[128,256]{1,0:T(8,128)(2,1)S(1)}, u32[]{:S(2)}, u32[]{:S(2)}) collective-permute-start(bf16[128,256]{1,0:T(8,128)(2,1)S(1)} %get-tuple-element.22), channel_id=1, source_target_pairs={{0,1},{1,0},{2,3},{3,2},{4,5},{5,4},{6,7},{7,6},{8,9},{9,8},{10,11... | collective-permute-start | bytes 196616 | tf_op jit(solution)/shard_map/ppermute | solution.py:21
  13.4 9.8 %collective-permute-start.6 = (bf16[128,512]{1,0:T(8,128)(2,1)S(1)}, bf16[128,512]{1,0:T(8,128)(2,1)S(1)}, u32[]{:S(2)}, u32[]{:S(2)}) collective-permute-start(bf16[128,512]{1,0:T(8,128)(2,1)S(1)} %copy-done), channel_id=1, source_target_pairs={{0,8},{4,12},{8,0},{12,4},{16,24},{20,28},{24,16},{28,20},{1,9},{5... | collective-permute-start | bytes 393224 | tf_op jit(solution)/shard_map/ppermute | solution.py:21
  18.5 12.4 %collective-permute-start.3 = (bf16[128,256]{1,0:T(8,128)(2,1)S(1)}, bf16[128,256]{1,0:T(8,128)(2,1)S(1)}, u32[]{:S(2)}, u32[]{:S(2)}) collective-permute-start(bf16[128,256]{1,0:T(8,128)(2,1)S(1)} %add_convert_fusion.refs_0_), channel_id=1, source_target_pairs={{0,1},{1,0},{2,3},{3,2},{4,5},{5,4},{6,7},{7,6},{8,9},{9,8},{10,11... | collective-permute-start | bytes 196616 | tf_op jit(solution)/shard_map/ppermute | solution.py:21
  19.8 11.1 %collective-permute-start.4 = (bf16[128,256]{1,0:T(8,128)(2,1)S(1)}, bf16[128,256]{1,0:T(8,128)(2,1)S(1)}, u32[]{:S(2)}, u32[]{:S(2)}) collective-permute-start(bf16[128,256]{1,0:T(8,128)(2,1)S(1)} %add_convert_fusion.refs_0_), channel_id=1, source_target_pairs={{0,2},{1,3},{2,0},{3,1},{4,6},{5,7},{6,4},{7,5},{8,10},{9,11},{10,... | collective-permute-start | bytes 196616 | tf_op jit(solution)/shard_map/ppermute | solution.py:21
  22.7 8.2 %collective-permute-start.5 = (bf16[128,256]{1,0:T(8,128)(2,1)S(1)}, bf16[128,256]{1,0:T(8,128)(2,1)S(1)}, u32[]{:S(2)}, u32[]{:S(2)}) collective-permute-start(bf16[128,256]{1,0:T(8,128)(2,1)S(1)} %add_convert_fusion.refs_0_), channel_id=1, source_target_pairs={{0,3},{1,2},{2,1},{3,0},{4,7},{5,6},{6,5},{7,4},{8,11},{9,10},{10,... | collective-permute-start | bytes 196616 | tf_op jit(solution)/shard_map/ppermute | solution.py:21
  23.3 7.1 %collective-permute-start.7 = (bf16[128,1024]{1,0:T(8,128)(2,1)S(1)}, bf16[128,1024]{1,0:T(8,128)(2,1)S(1)}, u32[]{:S(2)}, u32[]{:S(2)}) collective-permute-start(bf16[128,1024]{1,0:T(8,128)(2,1)S(1)} %pad_maximum_fusion), channel_id=1, source_target_pairs={{0,16},{4,20},{8,24},{12,28},{16,0},{20,4},{24,8},{28,12},{1,17},{... | collective-permute-start | bytes 786440 | tf_op jit(solution)/shard_map/ppermute | solution.py:21
  30.4 2.0 %collective-permute-start.8 = (bf16[128,2048]{1,0:T(8,128)(2,1)S(1)}, bf16[128,2048]{1,0:T(8,128)(2,1)S(1)}, u32[]{:S(2)}, u32[]{:S(2)}) collective-permute-start(bf16[128,2048]{1,0:T(8,128)(2,1)S(1)} %constant_dynamic-update-slice_fusion.refs_4_), channel_id=1, source_target_pairs={{0,4},{4,0},{8,12},{12,8},{16,20},{20,16},{24,28},{28,24},{1,5},{5... | collective-permute-start | bytes 1572872 | tf_op jit(solution)/shard_map/ppermute | solution.py:21
  34.8 8.6 %all-to-all-start = ((bf16[8,8,128]{2,1,0:T(8,128)(2,1)}), bf16[8,8,128]{2,1,0:T(8,128)(2,1)S(1)}, u32[]{:S(2)}, u32[]{:S(2)}) async-start(bf16[8,8,128]{2,1,0:T(8,128)(2,1)} %bitcast.8), calls=%async_computation | async-start | bytes 32768 | tf_op jit(solution)/shard_map/all_to_all | solution.py:269

commit v5 on v4

--- a/solution.py
+++ b/solution.py
@@ -36,11 +36,20 @@
     def rows_of(chunk):
         return pl.ds(pl.multiple_of(chunk * rows, rows), rows)
 
+    def act_copies(at, i):
+        wide = act.shape[2] // 2
+        return [
+            pltpu.make_async_copy(
+                act_hbm.at[at, pl.ds(j * wide, wide)], act.at[i, :, pl.ds(j * wide, wide)], sem.at[1 + j, i]
+            )
+            for j in range(2)
+        ]
+
     def copies(i):
         at = rows_of(part ^ (count - i))
         return (
             pltpu.make_async_copy(grad_hbm.at[at], grad.at[i], sem.at[0, i]),
-            pltpu.make_async_copy(act_hbm.at[at], act.at[i], sem.at[1, i]),
+            *act_copies(at, i),
         )
 
     weights = (
@@ -50,11 +59,13 @@
     own = pltpu.make_async_copy(grad_hbm.at[rows_of(part)], grad_own, wsem.at[2])
     for copy in weights:
         copy.start()
-    for i in range(min(ahead, count)):
+    for copy in copies(0):
+        copy.start()
+    for copy in weights:
+        copy.wait()
+    for i in range(1, min(ahead, count)):
         for copy in copies(i):
             copy.start()
-    for copy in weights:
-        copy.wait()
 
     def step(i, carry):
         for copy in copies(i):
@@ -91,7 +102,7 @@
         scratch_shapes=[
             pltpu.VMEM((count, rows, ff), BF16),
             pltpu.VMEM((count, rows, d), BF16),
-            pltpu.SemaphoreType.DMA((2, count)),
+            pltpu.SemaphoreType.DMA((3, count)),
             pltpu.SemaphoreType.DMA((3,)),
         ],
         compiler_params=pltpu.CompilerParams(vmem_limit_bytes=VMEM_LIMIT),
@@ -144,7 +155,7 @@
 
 def score_kernel(n_chunks, low, n_blocks, ends_ref, scale_ref, select_ref, labels_ref, *refs):
     chunks, held = refs[:n_chunks], refs[n_chunks : n_chunks + 2]
-    out_ref, acts, left, right, outer, sketch = refs[n_chunks + 2 :]
+    near_ref, far_ref, acts, left, right, outer, sketch = refs[n_chunks + 2 :]
     k, rows = chunks[0].shape[0] // 2, chunks[0].shape[1]
     high = outer.shape[0] * outer.shape[2] // k
     docs = low * high
@@ -194,7 +205,8 @@
     packed = lax.dot_general(
         select_ref[...], local.astype(BF16), NT, preferred_element_type=F32
     )
-    out_ref[...] = (packed + labels_ref[...]).astype(BF16)
+    packed = (packed + labels_ref[...]).astype(BF16)
+    near_ref[...], far_ref[...] = packed[: near_ref.shape[0]], packed[near_ref.shape[0] :]
 
 
 def score(ends, scale, select, labels, chunks, held, nval, low, n_blocks):
@@ -205,9 +217,9 @@
     vmem = pl.BlockSpec(memory_space=pltpu.VMEM)
     return pl.pallas_call(
         functools.partial(score_kernel, len(chunks), low, n_blocks),
-        out_shape=jax.ShapeDtypeStruct((select.shape[0], nval), BF16),
+        out_shape=[jax.ShapeDtypeStruct((select.shape[0] // 2, nval), BF16)] * 2,
         in_specs=[vmem] * (4 + len(chunks) + 2),
-        out_specs=vmem,
+        out_specs=[vmem] * 2,
         scratch_shapes=[
             pltpu.VMEM((k, rows), F32),
             pltpu.VMEM((low * k, tokens), BF16),
@@ -256,7 +268,9 @@
     height = -(-2 * per_owner // 8) * 8
     owners, out_slot = out_rows // maxdoc, out_rows % maxdoc
     earlier = (owners[None, :] == owners[:, None]) & (indices[None, :] < indices[:, None])
-    target = owners * height + jnp.sum(earlier.astype(jnp.int32), axis=1)
+    within = jnp.sum(earlier.astype(jnp.int32), axis=1)
+    apart = owners ^ lax.axis_index("dp")
+    target = (apart // 2 + apart % 2 * (devices // 2)) * height + within
     at = jnp.arange(devices * height, dtype=jnp.int32)
     select = (target[None, :] == at[:, None]).astype(BF16)
     label = jnp.where(lengths > 0, out_slot, -1)
@@ -265,10 +279,12 @@
     )
     labels = jnp.broadcast_to(labels.astype(F32)[:, None], (devices * height, nval))
 
-    payload = score(ends, scale, select, labels, chunks, halves, nval, low, devices)
-    got_rows = lax.all_to_all(
-        payload.reshape(devices, height, nval), "dp", split_axis=0, concat_axis=0, tiled=True
-    )
+    near, away = score(ends, scale, select, labels, chunks, halves, nval, low, devices)
+    crossed = swap(away, "dp", 1)
+    blocks = [slice(i * height, (i + 1) * height) for i in range(devices // 2)]
+    rows = [jnp.concatenate([near[at], crossed[at]], axis=0) for at in blocks]
+    rows = rows[:1] + [swap(rows[i], "dp", 2 * i) for i in range(1, devices // 2)]
+    got_rows = jnp.concatenate(rows, axis=0).reshape(devices, height, nval)
     data = got_rows[:, :per_owner].reshape(devices * per_owner, nval)
     tags = got_rows[:, per_owner : 2 * per_owner, :maxdoc].reshape(devices * per_owner, maxdoc)
     choose = (tags.astype(F32) == indices.astype(F32)[None, :]).astype(BF16)

time: 44.4 us -> 43 us (0.968)
  Pallas kernels: 13.3 us -> 12.5 us
  waiting for transfers between devices: 11.7 us -> 11.1 us
    all_to_all x1 -> x0, waiting for transfers between devices: 4.75 us -> none  [shards(): lax.all_to_all(payload.reshape(devices, height, nval), 'dp', split_axis=0...]
    ppermute x9 -> x13, waiting for transfers between devices: 6.9 us -> 11.1 us  [swap(): lax.ppermute(x, axis, [(i, i ^ k) for i in range(lax.axis_size(axis))])]
    all_to_all x1 -> x0, starting transfers between devices: 3.83 us -> none  [shards(): lax.all_to_all(payload.reshape(devices, height, nval), 'dp', split_axis=0...]
    ppermute x9 -> x13, starting transfers between devices: 13.5 us -> 17.2 us  [swap(): lax.ppermute(x, axis, [(i, i ^ k) for i in range(lax.axis_size(axis))])]
    pallas_call x1, Pallas kernels: 2.32 us -> 1.71 us  [score(): pl.pallas_call(functools.partial(score_kernel, len(chunks), low, n_blocks...]
  transfers between devices with their start and end apart: 10 -> 13, of which waited for: 3 -> 5; matrix products, arithmetic and copies ran while one was open for 2% -> 2% of each run, Pallas kernels for 8% -> 8%
where the time goes in v5:
time: 43 us; the launch traced here: 42.9 us
  starting transfers between devices  17.2 us (40%)
  Pallas kernels  12.5 us (29%)
  waiting for transfers between devices  11.1 us (26%)
  matrix products  0.79 us (2%)
  local copies, waits for them, and re-layouts  0.58 us (1%)
  other arithmetic  0.48 us (1%)
    ppermute x13, starting transfers between devices, swap(): lax.ppermute(x, axis, [(i, i ^ k) for i in range(lax.axis_size(axis))])  17.2 us
    ppermute x13, waiting for transfers between devices, swap(): lax.ppermute(x, axis, [(i, i ^ k) for i in range(lax.axis_size(axis))])  11.1 us
    pallas_call x1, Pallas kernels, project_peers(): pl.pallas_call(functools.partial(peers_kernel, min(2, count)), out_shape=...  7.52 us
    pallas_call x1, Pallas kernels, project_own(): pl.pallas_call(own_kernel, out_shape=jax.ShapeDtypeStruct((2 * k, rows),...  3.31 us
    pallas_call x1, Pallas kernels, score(): pl.pallas_call(functools.partial(score_kernel, len(chunks), low, n_blocks...  1.71 us
  transfers between devices with their start and end apart: 13, of which 5 were waited for; matrix products, arithmetic and copies ran while one was open for 2% of the time, Pallas kernels for 8%

profile of v5, /device:TPU:0, one launch (start us, length us, event | category | flops | bytes accessed | tf_op | source)
XLA Modules:
  0.0 42.9 jit_solution(5301605968121617765)
XLA Ops:
  0.0 7.5 %project_peers.1 = (bf16[3,128,256]{2,1,0:T(8,128)(2,1)S(1)}, bf16[256,2048]{1,0:T(8,128)(2,1)S(1)}, bf16[64,7168]{1,0:T(8,128)(2,1)S(1)}, bf16[64,2048]{1,0:T(8,128)(2,1)S(1)}) custom-call(bf16[1024,7168]{1,0:T(8,128)(2,1)} %act_hbm.3, bf16[1024,2048]{1,0:T(8,128)(2,1)} %grad_hbm.1, bf16[64,7168]{1,0:T(8,128)(2,1)} %bitcast.16, bf16[64,2048]{1,0:T(8,128)(2,1)} %bitcast.17), custom_call_target="tpu_custom_call" | custom-call | flops 1207959552 | bytes 18874368 | tf_op jit(solution)/shard_map/project_peers/pallas_call | solution.py:94
  7.6 5.1 %collective-permute-start = (bf16[128,256]{1,0:T(8,128)(2,1)S(1)}, bf16[128,256]{1,0:T(8,128)(2,1)S(1)}, u32[]{:S(2)}, u32[]{:S(2)}) collective-permute-start(bf16[128,256]{1,0:T(8,128)(2,1)S(1)} %get-tuple-element.25), channel_id=1, source_target_pairs={{0,3},{1,2},{2,1},{3,0},{4,7},{5,6},{6,5},{7,4},{8,11},{9,10},{10,... | collective-permute-start | bytes 196616 | tf_op jit(solution)/shard_map/ppermute | solution.py:21
  12.7 0.6 %collective-permute-start.2 = (bf16[128,256]{1,0:T(8,128)(2,1)S(1)}, bf16[128,256]{1,0:T(8,128)(2,1)S(1)}, u32[]{:S(2)}, u32[]{:S(2)}) collective-permute-start(bf16[128,256]{1,0:T(8,128)(2,1)S(1)} %get-tuple-element.26), channel_id=1, source_target_pairs={{0,1},{1,0},{2,3},{3,2},{4,5},{5,4},{6,7},{7,6},{8,9},{9,8},{10,11... | collective-permute-start | bytes 196616 | tf_op jit(solution)/shard_map/ppermute | solution.py:21
  13.3 1.6 %collective-permute-start.6 = (bf16[128,512]{1,0:T(8,128)(2,1)S(1)}, bf16[128,512]{1,0:T(8,128)(2,1)S(1)}, u32[]{:S(2)}, u32[]{:S(2)}) collective-permute-start(bf16[128,512]{1,0:T(8,128)(2,1)S(1)} %copy-done), channel_id=1, source_target_pairs={{0,8},{4,12},{8,0},{12,4},{16,24},{20,28},{24,16},{28,20},{1,9},{5... | collective-permute-start | bytes 393224 | tf_op jit(solution)/shard_map/ppermute | solution.py:21
  15.0 3.3 %project_own.1 = bf16[128,256]{1,0:T(8,128)(2,1)S(1)} custom-call(bf16[1024,7168]{1,0:T(8,128)(2,1)} %act_hbm.3, bf16[256,2048]{1,0:T(8,128)(2,1)S(1)} %get-tuple-element.14.grad_ref, bf16[64,7168]{1,0:T(8,128)(2,1)S(1)} %get-tuple-element.15.wa_ref, bf16[64,2048]{1,0:T(8,128)(2,1)S(1)} %get-tuple-element.16.wg_ref), custom_call_target="tpu_custom_call" | custom-call | flops 301989888 | bytes 4718592 | tf_op jit(solution)/shard_map/project_own/pallas_call | solution.py:139
  18.3 0.0 collective-permute-done
  18.4 1.3 %collective-permute-start.3 = (bf16[128,256]{1,0:T(8,128)(2,1)S(1)}, bf16[128,256]{1,0:T(8,128)(2,1)S(1)}, u32[]{:S(2)}, u32[]{:S(2)}) collective-permute-start(bf16[128,256]{1,0:T(8,128)(2,1)S(1)} %add_convert_fusion.refs_0_), channel_id=1, source_target_pairs={{0,1},{1,0},{2,3},{3,2},{4,5},{5,4},{6,7},{7,6},{8,9},{9,8},{10,11... | collective-permute-start | bytes 196616 | tf_op jit(solution)/shard_map/ppermute | solution.py:21
  19.7 2.9 %collective-permute-start.4 = (bf16[128,256]{1,0:T(8,128)(2,1)S(1)}, bf16[128,256]{1,0:T(8,128)(2,1)S(1)}, u32[]{:S(2)}, u32[]{:S(2)}) collective-permute-start(bf16[128,256]{1,0:T(8,128)(2,1)S(1)} %add_convert_fusion.refs_0_), channel_id=1, source_target_pairs={{0,2},{1,3},{2,0},{3,1},{4,6},{5,7},{6,4},{7,5},{8,10},{9,11},{10,... | collective-permute-start | bytes 196616 | tf_op jit(solution)/shard_map/ppermute | solution.py:21
  22.6 0.2 collective-permute-start.5
  22.9 0.1 select_reduce_fusion.1
  23.0 0.2 convert_reduce_fusion
  23.2 1.6 %collective-permute-start.7 = (bf16[128,1024]{1,0:T(8,128)(2,1)S(1)}, bf16[128,1024]{1,0:T(8,128)(2,1)S(1)}, u32[]{:S(2)}, u32[]{:S(2)}) collective-permute-start(bf16[128,1024]{1,0:T(8,128)(2,1)S(1)} %pad_maximum_fusion), channel_id=1, source_target_pairs={{0,16},{4,20},{8,24},{12,28},{16,0},{20,4},{24,8},{28,12},{1,17},{... | collective-permute-start | bytes 786440 | tf_op jit(solution)/shard_map/ppermute | solution.py:21
  24.8 5.4 %collective-permute-done.7 = bf16[128,1024]{1,0:T(8,128)(2,1)S(1)} collective-permute-done((bf16[128,1024]{1,0:T(8,128)(2,1)S(1)}, bf16[128,1024]{1,0:T(8,128)(2,1)S(1)}, u32[]{:S(2)}, u32[]{:S(2)}) %collective-permute-start.7) | collective-permute-done | bytes 262176 | tf_op jit(solution)/shard_map/ppermute | solution.py:21
  30.2 0.1 collective-permute-start.8
  30.4 0.1 select_reduce_fusion
  30.5 0.1 reshape.32
  30.5 0.1 copy.11
  30.6 0.1 broadcast_in_dim.35
  30.7 0.1 reshape.33.scale_ref
  30.8 0.0 collective-permute-done.5.refs_3_
  30.8 1.4 %collective-permute-done.8.refs_5_ = bf16[128,2048]{1,0:T(8,128)(2,1)S(1)} collective-permute-done((bf16[128,2048]{1,0:T(8,128)(2,1)S(1)}, bf16[128,2048]{1,0:T(8,128)(2,1)S(1)}, u32[]{:S(2)}, u32[]{:S(2)}) %collective-permute-start.8) | collective-permute-done | bytes 524320 | tf_op jit(solution)/shard_map/ppermute | solution.py:21
  32.2 0.1 broadcast_in_dim.38.labels_ref
  32.3 0.1 broadcast_in_dim.30.ends_ref
  32.4 1.7 %score.1 = (bf16[32,128]{1,0:T(8,128)(2,1)S(1)}, bf16[32,128]{1,0:T(8,128)(2,1)S(1)}) custom-call(s32[32,128]{1,0:T(8,128)S(1)} %broadcast_in_dim.30.ends_ref, f32[8,256]{1,0:T(8,128)S(1)} %reshape.33.scale_ref, bf16[64,32]{1,0:T(8,128)(2,1)S(1)} %fusion.1.select_ref, f32[64,128]{1,0:T(8,128)S(1)} %broadcast_in_dim.38.labels_ref, ...), custom_call_target="tpu_custom_call" | custom-call | flops 301989888 | bytes 1048576 | tf_op jit(solution)/shard_map/score/pallas_call | solution.py:218
  34.1 0.2 collective-permute-start.9
  34.3 1.0 %collective-permute-done.9 = bf16[32,128]{1,0:T(8,128)(2,1)S(1)} collective-permute-done((bf16[32,128]{1,0:T(8,128)(2,1)S(1)}, bf16[32,128]{1,0:T(8,128)(2,1)S(1)}, u32[]{:S(2)}, u32[]{:S(2)}) %collective-permute-start.9) | collective-permute-done | bytes 8224 | tf_op jit(solution)/shard_map/ppermute | solution.py:21
  35.3 2.6 %collective-permute-start.12 = (bf16[16,128]{1,0:T(8,128)(2,1)S(1)}, bf16[16,128]{1,0:T(8,128)(2,1)S(1)}, u32[]{:S(2)}, u32[]{:S(2)}) collective-permute-start(bf16[16,128]{1,0:T(8,128)(2,1)S(1)} %pad_maximum_fusion.3), channel_id=1, source_target_pairs={{0,24},{4,28},{8,16},{12,20},{16,8},{20,12},{24,0},{28,4},{1,25},{... | collective-permute-start | bytes 12296 | tf_op jit(solution)/shard_map/ppermute | solution.py:21
  37.9 0.5 %collective-permute-start.10 = (bf16[16,128]{1,0:T(8,128)(2,1)S(1)}, bf16[16,128]{1,0:T(8,128)(2,1)S(1)}, u32[]{:S(2)}, u32[]{:S(2)}) collective-permute-start(bf16[16,128]{1,0:T(8,128)(2,1)S(1)} %pad_maximum_fusion.1), channel_id=1, source_target_pairs={{0,8},{4,12},{8,0},{12,4},{16,24},{20,28},{24,16},{28,20},{1,9},{5... | collective-permute-start | bytes 12296 | tf_op jit(solution)/shard_map/ppermute | solution.py:21
  38.4 0.4 collective-permute-start.11
  38.8 2.7 %collective-permute-done.10 = bf16[16,128]{1,0:T(8,128)(2,1)S(1)} collective-permute-done((bf16[16,128]{1,0:T(8,128)(2,1)S(1)}, bf16[16,128]{1,0:T(8,128)(2,1)S(1)}, u32[]{:S(2)}, u32[]{:S(2)}) %collective-permute-start.10) | collective-permute-done | bytes 4128 | tf_op jit(solution)/shard_map/ppermute | solution.py:21
  41.5 0.5 %collective-permute-done.11 = bf16[16,128]{1,0:T(8,128)(2,1)S(1)} collective-permute-done((bf16[16,128]{1,0:T(8,128)(2,1)S(1)}, bf16[16,128]{1,0:T(8,128)(2,1)S(1)}, u32[]{:S(2)}, u32[]{:S(2)}) %collective-permute-start.11) | collective-permute-done | bytes 4128 | tf_op jit(solution)/shard_map/ppermute | solution.py:21
  42.1 0.8 %fusion = bf16[32,128]{1,0:T(8,128)(2,1)} fusion(bf16[8,4,128]{2,1,0:T(4,128)(2,1)S(1)} %slice.57, bf16[8,4,32]{2,1,0:T(4,128)(2,1)S(1)} %slice.56, f32[32]{0:T(128)S(1)} %iota_convert_fusion), kind=kOutput, calls=%fused_computation.1 | convolution fusion | flops 268288 | bytes 18560 | tf_op jit(solution)/shard_map/dot_general | solution.py:291
  (35 shorter events, 0.3 us)
Async XLA Ops:
  0.0 13.3 %copy-start = (bf16[128,512]{1,0:T(8,128)(2,1)S(1)}, bf16[128,512]{1,0:T(8,128)(2,1)}, u32[]{:S(2)}) copy-start(bf16[128,512]{1,0:T(8,128)(2,1)} %param.11) | copy-start | bytes 393220
  0.0 22.9 %copy-start.2 = (s32[1,32]{1,0:T(1,128)S(1)}, s32[1,32]{1,0:T(1,128)}, u32[]{:S(2)}) copy-start(s32[1,32]{1,0:T(1,128)} %param.12) | copy-start | bytes 388
  0.0 22.9 %copy-start.1 = (s32[1,32]{1,0:T(1,128)S(1)}, s32[1,32]{1,0:T(1,128)}, u32[]{:S(2)}) copy-start(s32[1,32]{1,0:T(1,128)} %param.13) | copy-start | bytes 388
  7.6 10.8 %collective-permute-start = (bf16[128,256]{1,0:T(8,128)(2,1)S(1)}, bf16[128,256]{1,0:T(8,128)(2,1)S(1)}, u32[]{:S(2)}, u32[]{:S(2)}) collective-permute-start(bf16[128,256]{1,0:T(8,128)(2,1)S(1)} %get-tuple-element.25), channel_id=1, source_target_pairs={{0,3},{1,2},{2,1},{3,0},{4,7},{5,6},{6,5},{7,4},{8,11},{9,10},{10,... | collective-permute-start | bytes 196616 | tf_op jit(solution)/shard_map/ppermute | solution.py:21
  12.7 5.6 %collective-permute-start.1 = (bf16[128,256]{1,0:T(8,128)(2,1)S(1)}, bf16[128,256]{1,0:T(8,128)(2,1)S(1)}, u32[]{:S(2)}, u32[]{:S(2)}) collective-permute-start(bf16[128,256]{1,0:T(8,128)(2,1)S(1)} %get-tuple-element.27), channel_id=1, source_target_pairs={{0,2},{1,3},{2,0},{3,1},{4,6},{5,7},{6,4},{7,5},{8,10},{9,11},{10,... | collective-permute-start | bytes 196616 | tf_op jit(solution)/shard_map/ppermute | solution.py:21
  12.7 5.6 %collective-permute-start.2 = (bf16[128,256]{1,0:T(8,128)(2,1)S(1)}, bf16[128,256]{1,0:T(8,128)(2,1)S(1)}, u32[]{:S(2)}, u32[]{:S(2)}) collective-permute-start(bf16[128,256]{1,0:T(8,128)(2,1)S(1)} %get-tuple-element.26), channel_id=1, source_target_pairs={{0,1},{1,0},{2,3},{3,2},{4,5},{5,4},{6,7},{7,6},{8,9},{9,8},{10,11... | collective-permute-start | bytes 196616 | tf_op jit(solution)/shard_map/ppermute | solution.py:21
  13.3 9.8 %collective-permute-start.6 = (bf16[128,512]{1,0:T(8,128)(2,1)S(1)}, bf16[128,512]{1,0:T(8,128)(2,1)S(1)}, u32[]{:S(2)}, u32[]{:S(2)}) collective-permute-start(bf16[128,512]{1,0:T(8,128)(2,1)S(1)} %copy-done), channel_id=1, source_target_pairs={{0,8},{4,12},{8,0},{12,4},{16,24},{20,28},{24,16},{28,20},{1,9},{5... | collective-permute-start | bytes 393224 | tf_op jit(solution)/shard_map/ppermute | solution.py:21
  18.4 12.4 %collective-permute-start.3 = (bf16[128,256]{1,0:T(8,128)(2,1)S(1)}, bf16[128,256]{1,0:T(8,128)(2,1)S(1)}, u32[]{:S(2)}, u32[]{:S(2)}) collective-permute-start(bf16[128,256]{1,0:T(8,128)(2,1)S(1)} %add_convert_fusion.refs_0_), channel_id=1, source_target_pairs={{0,1},{1,0},{2,3},{3,2},{4,5},{5,4},{6,7},{7,6},{8,9},{9,8},{10,11... | collective-permute-start | bytes 196616 | tf_op jit(solution)/shard_map/ppermute | solution.py:21
  19.7 11.1 %collective-permute-start.4 = (bf16[128,256]{1,0:T(8,128)(2,1)S(1)}, bf16[128,256]{1,0:T(8,128)(2,1)S(1)}, u32[]{:S(2)}, u32[]{:S(2)}) collective-permute-start(bf16[128,256]{1,0:T(8,128)(2,1)S(1)} %add_convert_fusion.refs_0_), channel_id=1, source_target_pairs={{0,2},{1,3},{2,0},{3,1},{4,6},{5,7},{6,4},{7,5},{8,10},{9,11},{10,... | collective-permute-start | bytes 196616 | tf_op jit(solution)/shard_map/ppermute | solution.py:21
  22.6 8.2 %collective-permute-start.5 = (bf16[128,256]{1,0:T(8,128)(2,1)S(1)}, bf16[128,256]{1,0:T(8,128)(2,1)S(1)}, u32[]{:S(2)}, u32[]{:S(2)}) collective-permute-start(bf16[128,256]{1,0:T(8,128)(2,1)S(1)} %add_convert_fusion.refs_0_), channel_id=1, source_target_pairs={{0,3},{1,2},{2,1},{3,0},{4,7},{5,6},{6,5},{7,4},{8,11},{9,10},{10,... | collective-permute-start | bytes 196616 | tf_op jit(solution)/shard_map/ppermute | solution.py:21
  23.2 7.0 %collective-permute-start.7 = (bf16[128,1024]{1,0:T(8,128)(2,1)S(1)}, bf16[128,1024]{1,0:T(8,128)(2,1)S(1)}, u32[]{:S(2)}, u32[]{:S(2)}) collective-permute-start(bf16[128,1024]{1,0:T(8,128)(2,1)S(1)} %pad_maximum_fusion), channel_id=1, source_target_pairs={{0,16},{4,20},{8,24},{12,28},{16,0},{20,4},{24,8},{28,12},{1,17},{... | collective-permute-start | bytes 786440 | tf_op jit(solution)/shard_map/ppermute | solution.py:21
  30.2 2.0 %collective-permute-start.8 = (bf16[128,2048]{1,0:T(8,128)(2,1)S(1)}, bf16[128,2048]{1,0:T(8,128)(2,1)S(1)}, u32[]{:S(2)}, u32[]{:S(2)}) collective-permute-start(bf16[128,2048]{1,0:T(8,128)(2,1)S(1)} %constant_dynamic-update-slice_fusion.refs_4_), channel_id=1, source_target_pairs={{0,4},{4,0},{8,12},{12,8},{16,20},{20,16},{24,28},{28,24},{1,5},{5... | collective-permute-start | bytes 1572872 | tf_op jit(solution)/shard_map/ppermute | solution.py:21
  34.1 1.2 %collective-permute-start.9 = (bf16[32,128]{1,0:T(8,128)(2,1)S(1)}, bf16[32,128]{1,0:T(8,128)(2,1)S(1)}, u32[]{:S(2)}, u32[]{:S(2)}) collective-permute-start(bf16[32,128]{1,0:T(8,128)(2,1)S(1)} %get-tuple-element.22), channel_id=1, source_target_pairs={{0,4},{4,0},{8,12},{12,8},{16,20},{20,16},{24,28},{28,24},{1,5},{5... | collective-permute-start | bytes 24584 | tf_op jit(solution)/shard_map/ppermute | solution.py:21
  35.3 6.7 %collective-permute-start.12 = (bf16[16,128]{1,0:T(8,128)(2,1)S(1)}, bf16[16,128]{1,0:T(8,128)(2,1)S(1)}, u32[]{:S(2)}, u32[]{:S(2)}) collective-permute-start(bf16[16,128]{1,0:T(8,128)(2,1)S(1)} %pad_maximum_fusion.3), channel_id=1, source_target_pairs={{0,24},{4,28},{8,16},{12,20},{16,8},{20,12},{24,0},{28,4},{1,25},{... | collective-permute-start | bytes 12296 | tf_op jit(solution)/shard_map/ppermute | solution.py:21
  37.9 3.6 %collective-permute-start.10 = (bf16[16,128]{1,0:T(8,128)(2,1)S(1)}, bf16[16,128]{1,0:T(8,128)(2,1)S(1)}, u32[]{:S(2)}, u32[]{:S(2)}) collective-permute-start(bf16[16,128]{1,0:T(8,128)(2,1)S(1)} %pad_maximum_fusion.1), channel_id=1, source_target_pairs={{0,8},{4,12},{8,0},{12,4},{16,24},{20,28},{24,16},{28,20},{1,9},{5... | collective-permute-start | bytes 12296 | tf_op jit(solution)/shard_map/ppermute | solution.py:21
  38.4 3.6 %collective-permute-start.11 = (bf16[16,128]{1,0:T(8,128)(2,1)S(1)}, bf16[16,128]{1,0:T(8,128)(2,1)S(1)}, u32[]{:S(2)}, u32[]{:S(2)}) collective-permute-start(bf16[16,128]{1,0:T(8,128)(2,1)S(1)} %pad_maximum_fusion.2), channel_id=1, source_target_pairs={{0,16},{4,20},{8,24},{12,28},{16,0},{20,4},{24,8},{28,12},{1,17},{... | collective-permute-start | bytes 12296 | tf_op jit(solution)/shard_map/ppermute | solution.py:21

commit v6 on v5

--- a/solution.py
+++ b/solution.py
@@ -153,15 +153,12 @@
     )(far(activations), grad, wa, wg)
 
 
-def score_kernel(n_chunks, low, n_blocks, ends_ref, scale_ref, select_ref, labels_ref, *refs):
-    chunks, held = refs[:n_chunks], refs[n_chunks : n_chunks + 2]
-    near_ref, far_ref, acts, left, right, outer, sketch = refs[n_chunks + 2 :]
+def outer_sums(offsets, low, ends_ref, chunks, acts, left, right):
     k, rows = chunks[0].shape[0] // 2, chunks[0].shape[1]
-    high = outer.shape[0] * outer.shape[2] // k
-    docs = low * high
-    part, me = lax.axis_index("tensor"), lax.axis_index("dp")
+    docs, high = ends_ref.shape[0], right.shape[0] // k
+    part = lax.axis_index("tensor")
     for c, ref in enumerate(chunks):
-        at = (part ^ c) * rows + lax.broadcasted_iota(jnp.int32, (docs, rows), 1)
+        at = (part ^ offsets[c]) * rows + lax.broadcasted_iota(jnp.int32, (docs, rows), 1)
         doc = jnp.sum((at >= ends_ref[:, :1]).astype(F32), axis=0, keepdims=True)
         div = jnp.floor(doc * (1.0 / low))
         of_mod = lax.broadcasted_iota(jnp.int32, (low, rows), 0).astype(F32)
@@ -174,26 +171,64 @@
         for m in range(high):
             mask = jnp.broadcast_to((div == m).astype(F32), (k, rows)).astype(BF16)
             right[m * k : (m + 1) * k, span] = ref[k:, :] * mask
-    lanes = outer.shape[2]
-    sums = lax.dot_general(left[...], right[...], NT, preferred_element_type=F32)
+    return lax.dot_general(left[...], right[...], NT, preferred_element_type=F32)
+
+
+def sums_scratch(count, k, rows, low, high):
+    return [
+        pltpu.VMEM((k, rows), F32),
+        pltpu.VMEM((low * k, count * rows), BF16),
+        pltpu.VMEM((high * k, count * rows), BF16),
+    ]
+
+
+def early_kernel(offsets, low, ends_ref, *refs):
+    *chunks, out_ref, acts, left, right = refs
+    out_ref[...] = outer_sums(offsets, low, ends_ref, chunks, acts, left, right)
+
+
+def early_sums(offsets, ends, chunks, low):
+    vmem = pl.BlockSpec(memory_space=pltpu.VMEM)
+    k, rows = chunks[0].shape[0] // 2, chunks[0].shape[1]
+    high = ends.shape[0] // low
+    return pl.pallas_call(
+        functools.partial(early_kernel, offsets, low),
+        out_shape=jax.ShapeDtypeStruct((low * k, high * k), F32),
+        in_specs=[vmem] * (1 + len(chunks)),
+        out_specs=vmem,
+        scratch_shapes=sums_scratch(len(chunks), k, rows, low, high),
+        compiler_params=pltpu.CompilerParams(vmem_limit_bytes=8 << 20),
+        name="early_sums",
+    )(ends, *chunks)
+
+
+def score_kernel(offsets, low, n_blocks, ends_ref, scale_ref, select_ref, labels_ref, early_ref, *refs):
+    n_chunks = len(offsets)
+    chunks, held = refs[:n_chunks], refs[n_chunks : n_chunks + 2]
+    near_ref, far_ref, acts, left, right, outer, sketch = refs[n_chunks + 2 :]
+    k = chunks[0].shape[0] // 2
+    me, lanes = lax.axis_index("dp"), outer.shape[2]
+    sums = outer_sums(offsets, low, ends_ref, chunks, acts, left, right) + early_ref[...]
     for m in range(outer.shape[0]):
         outer[m] = sums[:, m * lanes : (m + 1) * lanes]
 
     first = lax.broadcasted_iota(jnp.int32, (low, lanes), 1) < k
     per_block = k // n_blocks
-    for m in range(outer.shape[0]):
-        scale = scale_ref[:, m * lanes : (m + 1) * lanes]
-        for i in range(0, k, 2):
-            even = outer[m, i * low : (i + 1) * low, :] * scale
-            odd = outer[m, (i + 1) * low : (i + 2) * low, :] * scale
-            pair = [
-                jnp.where(first, even, pltpu.roll(odd, k, 1)),
-                jnp.where(first, pltpu.roll(even, k, 1), odd),
-            ]
-            apart = me ^ (i // per_block)
-            at = (apart // 2 + apart % 2 * (n_blocks // 2)) * (per_block * k) + i % per_block * k
-            rows_at = slice(2 * m * low, 2 * (m + 1) * low)
-            sketch[rows_at, pl.ds(pl.multiple_of(at, lanes), lanes)] = jnp.concatenate(pair, axis=0).astype(BF16)
+    for block in range(n_blocks):
+        apart = me ^ block
+        base = pl.multiple_of((apart // 2 + apart % 2 * (n_blocks // 2)) * (per_block * k), lanes)
+        for i in range(block * per_block, (block + 1) * per_block, 2):
+            at = pl.ds(base + (i - block * per_block) * k, lanes)
+            for m in range(outer.shape[0]):
+                scale = scale_ref[:, m * lanes : (m + 1) * lanes]
+                even = outer[m, i * low : (i + 1) * low, :] * scale
+                odd = outer[m, (i + 1) * low : (i + 2) * low, :] * scale
+                pair = [
+                    jnp.where(first, even, pltpu.roll(odd, k, 1)),
+                    jnp.where(first, pltpu.roll(even, k, 1), odd),
+                ]
+                rows_at = slice(2 * m * low, 2 * (m + 1) * low)
+                sketch[rows_at, at] = jnp.concatenate(pair, axis=0).astype(BF16)
 
     half = held[0].shape[1]
     local = sum(
@@ -209,30 +244,26 @@
     near_ref[...], far_ref[...] = packed[: near_ref.shape[0]], packed[near_ref.shape[0] :]
 
 
-def score(ends, scale, select, labels, chunks, held, nval, low, n_blocks):
+def score(offsets, ends, scale, select, labels, early, chunks, held, nval, low, n_blocks):
     k, rows = chunks[0].shape[0] // 2, chunks[0].shape[1]
-    tokens = len(chunks) * rows
     docs = ends.shape[0]
     high = docs // low
     vmem = pl.BlockSpec(memory_space=pltpu.VMEM)
     return pl.pallas_call(
-        functools.partial(score_kernel, len(chunks), low, n_blocks),
+        functools.partial(score_kernel, offsets, low, n_blocks),
         out_shape=[jax.ShapeDtypeStruct((select.shape[0] // 2, nval), BF16)] * 2,
-        in_specs=[vmem] * (4 + len(chunks) + 2),
+        in_specs=[vmem] * (5 + len(chunks) + 2),
         out_specs=[vmem] * 2,
-        scratch_shapes=[
-            pltpu.VMEM((k, rows), F32),
-            pltpu.VMEM((low * k, tokens), BF16),
-            pltpu.VMEM((high * k, tokens), BF16),
-            pltpu.VMEM((high // 2, low * k, 2 * k), F32),
-            pltpu.VMEM((docs, k * k), BF16),
-        ],
+        scratch_shapes=sums_scratch(len(chunks), k, rows, low, high)
+        + [pltpu.VMEM((high // 2, low * k, 2 * k), F32), pltpu.VMEM((docs, k * k), BF16)],
         compiler_params=pltpu.CompilerParams(vmem_limit_bytes=16 << 20),
         cost_estimate=pl.CostEstimate(
-            flops=2 * k * k * docs * (tokens + nval), bytes_accessed=2 * k * k * nval, transcendentals=0
+            flops=2 * k * k * docs * (len(chunks) * rows + nval),
+            bytes_accessed=2 * k * k * nval,
+            transcendentals=0,
         ),
         name="score",
-    )(ends, scale, select, labels, *chunks, *held)
+    )(ends, scale, select, labels, early, *chunks, *held)
 
 
 def shards(activations, out_grads, proj_in, proj_out, validation, doc_lengths, owner_rows):
@@ -279,7 +310,12 @@
     )
     labels = jnp.broadcast_to(labels.astype(F32)[:, None], (devices * height, nval))
 
-    near, away = score(ends, scale, select, labels, chunks, halves, nval, low, devices)
+    soon = [0, 2]
+    late = [c for c in range(parts) if c not in soon]
+    early = early_sums(soon, ends, [chunks[c] for c in soon], low)
+    near, away = score(
+        late, ends, scale, select, labels, early, [chunks[c] for c in late], halves, nval, low, devices
+    )
     crossed = swap(away, "dp", 1)
     blocks = [slice(i * height, (i + 1) * height) for i in range(devices // 2)]
     rows = [jnp.concatenate([near[at], crossed[at]], axis=0) for at in blocks]

time: 43 us -> 42.5 us (0.988)
  waiting for transfers between devices: 11.1 us -> 10.6 us
    ppermute x13, waiting for transfers between devices: 11.1 us -> 10.6 us  [swap(): lax.ppermute(x, axis, [(i, i ^ k) for i in range(lax.axis_size(axis))])]
    pallas_call x1 -> x2, Pallas kernels: 1.71 us -> 1.76 us  [the longest x1 1.32 us: score(): pl.pallas_call(functools.partial(score_kernel, offsets, low, n_blocks), o...]
  transfers between devices with their start and end apart: 13 -> 13, of which waited for: 5 -> 5; matrix products, arithmetic and copies ran while one was open for 2% -> 2% of each run, Pallas kernels for 8% -> 9%
where the time goes in v6:
time: 42.5 us; the launch traced here: 42.4 us
  starting transfers between devices  17.2 us (40%)
  Pallas kernels  12.6 us (30%)
  waiting for transfers between devices  10.6 us (25%)
  matrix products  0.79 us (2%)
  local copies, waits for them, and re-layouts  0.58 us (1%)
  other arithmetic  0.48 us (1%)
    ppermute x13, starting transfers between devices, swap(): lax.ppermute(x, axis, [(i, i ^ k) for i in range(lax.axis_size(axis))])  17.2 us
    ppermute x13, waiting for transfers between devices, swap(): lax.ppermute(x, axis, [(i, i ^ k) for i in range(lax.axis_size(axis))])  10.6 us
    pallas_call x1, Pallas kernels, project_peers(): pl.pallas_call(functools.partial(peers_kernel, min(2, count)), out_shape=...  7.52 us
    pallas_call x1, Pallas kernels, project_own(): pl.pallas_call(own_kernel, out_shape=jax.ShapeDtypeStruct((2 * k, rows),...  3.31 us
    pallas_call x1, Pallas kernels, score(): pl.pallas_call(functools.partial(score_kernel, offsets, low, n_blocks), o...  1.32 us
  transfers between devices with their start and end apart: 13, of which 5 were waited for; matrix products, arithmetic and copies ran while one was open for 2% of the time, Pallas kernels for 9%

profile of v6, /device:TPU:0, one launch (start us, length us, event | category | flops | bytes accessed | tf_op | source)
XLA Modules:
  0.0 42.4 jit_solution(4048918736596037072)
XLA Ops:
  0.0 7.5 %project_peers.1 = (bf16[3,128,256]{2,1,0:T(8,128)(2,1)S(1)}, bf16[256,2048]{1,0:T(8,128)(2,1)S(1)}, bf16[64,7168]{1,0:T(8,128)(2,1)S(1)}, bf16[64,2048]{1,0:T(8,128)(2,1)S(1)}) custom-call(bf16[1024,7168]{1,0:T(8,128)(2,1)} %act_hbm.3, bf16[1024,2048]{1,0:T(8,128)(2,1)} %grad_hbm.1, bf16[64,7168]{1,0:T(8,128)(2,1)} %bitcast.16, bf16[64,2048]{1,0:T(8,128)(2,1)} %bitcast.17), custom_call_target="tpu_custom_call" | custom-call | flops 1207959552 | bytes 18874368 | tf_op jit(solution)/shard_map/project_peers/pallas_call | solution.py:94
  7.6 5.1 %collective-permute-start = (bf16[128,256]{1,0:T(8,128)(2,1)S(1)}, bf16[128,256]{1,0:T(8,128)(2,1)S(1)}, u32[]{:S(2)}, u32[]{:S(2)}) collective-permute-start(bf16[128,256]{1,0:T(8,128)(2,1)S(1)} %get-tuple-element.25), channel_id=1, source_target_pairs={{0,3},{1,2},{2,1},{3,0},{4,7},{5,6},{6,5},{7,4},{8,11},{9,10},{10,... | collective-permute-start | bytes 196616 | tf_op jit(solution)/shard_map/ppermute | solution.py:21
  12.7 0.6 %collective-permute-start.2 = (bf16[128,256]{1,0:T(8,128)(2,1)S(1)}, bf16[128,256]{1,0:T(8,128)(2,1)S(1)}, u32[]{:S(2)}, u32[]{:S(2)}) collective-permute-start(bf16[128,256]{1,0:T(8,128)(2,1)S(1)} %get-tuple-element.26), channel_id=1, source_target_pairs={{0,1},{1,0},{2,3},{3,2},{4,5},{5,4},{6,7},{7,6},{8,9},{9,8},{10,11... | collective-permute-start | bytes 196616 | tf_op jit(solution)/shard_map/ppermute | solution.py:21
  13.3 1.6 %collective-permute-start.6 = (bf16[128,512]{1,0:T(8,128)(2,1)S(1)}, bf16[128,512]{1,0:T(8,128)(2,1)S(1)}, u32[]{:S(2)}, u32[]{:S(2)}) collective-permute-start(bf16[128,512]{1,0:T(8,128)(2,1)S(1)} %copy-done), channel_id=1, source_target_pairs={{0,8},{4,12},{8,0},{12,4},{16,24},{20,28},{24,16},{28,20},{1,9},{5... | collective-permute-start | bytes 393224 | tf_op jit(solution)/shard_map/ppermute | solution.py:21
  15.0 3.3 %project_own.1 = bf16[128,256]{1,0:T(8,128)(2,1)S(1)} custom-call(bf16[1024,7168]{1,0:T(8,128)(2,1)} %act_hbm.3, bf16[256,2048]{1,0:T(8,128)(2,1)S(1)} %get-tuple-element.14.grad_ref, bf16[64,7168]{1,0:T(8,128)(2,1)S(1)} %get-tuple-element.15.wa_ref, bf16[64,2048]{1,0:T(8,128)(2,1)S(1)} %get-tuple-element.16.wg_ref), custom_call_target="tpu_custom_call" | custom-call | flops 301989888 | bytes 4718592 | tf_op jit(solution)/shard_map/project_own/pallas_call | solution.py:139
  18.3 0.0 collective-permute-done
  18.4 2.2 %collective-permute-start.3 = (bf16[128,256]{1,0:T(8,128)(2,1)S(1)}, bf16[128,256]{1,0:T(8,128)(2,1)S(1)}, u32[]{:S(2)}, u32[]{:S(2)}) collective-permute-start(bf16[128,256]{1,0:T(8,128)(2,1)S(1)} %add_convert_fusion.refs_0_), channel_id=1, source_target_pairs={{0,2},{1,3},{2,0},{3,1},{4,6},{5,7},{6,4},{7,5},{8,10},{9,11},{10,... | collective-permute-start | bytes 196616 | tf_op jit(solution)/shard_map/ppermute | solution.py:21
  20.6 2.0 %collective-permute-start.4 = (bf16[128,256]{1,0:T(8,128)(2,1)S(1)}, bf16[128,256]{1,0:T(8,128)(2,1)S(1)}, u32[]{:S(2)}, u32[]{:S(2)}) collective-permute-start(bf16[128,256]{1,0:T(8,128)(2,1)S(1)} %add_convert_fusion.refs_0_), channel_id=1, source_target_pairs={{0,1},{1,0},{2,3},{3,2},{4,5},{5,4},{6,7},{7,6},{8,9},{9,8},{10,11... | collective-permute-start | bytes 196616 | tf_op jit(solution)/shard_map/ppermute | solution.py:21
  22.6 0.2 collective-permute-start.5
  22.9 0.1 select_reduce_fusion.1
  23.0 0.2 convert_reduce_fusion
  23.2 1.6 %collective-permute-start.7 = (bf16[128,1024]{1,0:T(8,128)(2,1)S(1)}, bf16[128,1024]{1,0:T(8,128)(2,1)S(1)}, u32[]{:S(2)}, u32[]{:S(2)}) collective-permute-start(bf16[128,1024]{1,0:T(8,128)(2,1)S(1)} %pad_maximum_fusion), channel_id=1, source_target_pairs={{0,16},{4,20},{8,24},{12,28},{16,0},{20,4},{24,8},{28,12},{1,17},{... | collective-permute-start | bytes 786440 | tf_op jit(solution)/shard_map/ppermute | solution.py:21
  24.8 5.4 %collective-permute-done.7 = bf16[128,1024]{1,0:T(8,128)(2,1)S(1)} collective-permute-done((bf16[128,1024]{1,0:T(8,128)(2,1)S(1)}, bf16[128,1024]{1,0:T(8,128)(2,1)S(1)}, u32[]{:S(2)}, u32[]{:S(2)}) %collective-permute-start.7) | collective-permute-done | bytes 262176 | tf_op jit(solution)/shard_map/ppermute | solution.py:21
  30.2 0.1 collective-permute-start.8
  30.4 0.1 select_reduce_fusion
  30.5 0.1 reshape.32
  30.5 0.1 copy.11
  30.6 0.1 broadcast_in_dim.35
  30.7 0.1 reshape.33.scale_ref
  30.8 0.1 broadcast_in_dim.30.ends_ref
  30.9 0.4 %early_sums.1.early_ref = f32[512,256]{1,0:T(8,128)S(1)} custom-call(s32[32,128]{1,0:T(8,128)S(1)} %broadcast_in_dim.30.ends_ref, bf16[128,256]{1,0:T(8,128)(2,1)S(1)} %add_convert_fusion.refs_0_, bf16[128,256]{1,0:T(8,128)(2,1)S(1)} %collective-permute-done.3.refs_1_), custom_call_target="tpu_custom_call" | custom-call | tf_op jit(solution)/shard_map/early_sums/pallas_call | solution.py:194
  31.3 0.9 %collective-permute-done.8.refs_3_ = bf16[128,2048]{1,0:T(8,128)(2,1)S(1)} collective-permute-done((bf16[128,2048]{1,0:T(8,128)(2,1)S(1)}, bf16[128,2048]{1,0:T(8,128)(2,1)S(1)}, u32[]{:S(2)}, u32[]{:S(2)}) %collective-permute-start.8) | collective-permute-done | bytes 524320 | tf_op jit(solution)/shard_map/ppermute | solution.py:21
  32.2 0.1 broadcast_in_dim.38.labels_ref
  32.3 1.3 %score.1 = (bf16[32,128]{1,0:T(8,128)(2,1)S(1)}, bf16[32,128]{1,0:T(8,128)(2,1)S(1)}) custom-call(s32[32,128]{1,0:T(8,128)S(1)} %broadcast_in_dim.30.ends_ref, f32[8,256]{1,0:T(8,128)S(1)} %reshape.33.scale_ref, bf16[64,32]{1,0:T(8,128)(2,1)S(1)} %fusion.1.select_ref, f32[64,128]{1,0:T(8,128)S(1)} %broadcast_in_dim.38.labels_ref, ...), custom_call_target="tpu_custom_call" | custom-call | flops 167772160 | bytes 1048576 | tf_op jit(solution)/shard_map/score/pallas_call | solution.py:252
  33.6 0.2 collective-permute-start.9
  33.8 1.0 %collective-permute-done.9 = bf16[32,128]{1,0:T(8,128)(2,1)S(1)} collective-permute-done((bf16[32,128]{1,0:T(8,128)(2,1)S(1)}, bf16[32,128]{1,0:T(8,128)(2,1)S(1)}, u32[]{:S(2)}, u32[]{:S(2)}) %collective-permute-start.9) | collective-permute-done | bytes 8224 | tf_op jit(solution)/shard_map/ppermute | solution.py:21
  34.8 2.6 %collective-permute-start.12 = (bf16[16,128]{1,0:T(8,128)(2,1)S(1)}, bf16[16,128]{1,0:T(8,128)(2,1)S(1)}, u32[]{:S(2)}, u32[]{:S(2)}) collective-permute-start(bf16[16,128]{1,0:T(8,128)(2,1)S(1)} %pad_maximum_fusion.3), channel_id=1, source_target_pairs={{0,24},{4,28},{8,16},{12,20},{16,8},{20,12},{24,0},{28,4},{1,25},{... | collective-permute-start | bytes 12296 | tf_op jit(solution)/shard_map/ppermute | solution.py:21
  37.4 0.5 %collective-permute-start.10 = (bf16[16,128]{1,0:T(8,128)(2,1)S(1)}, bf16[16,128]{1,0:T(8,128)(2,1)S(1)}, u32[]{:S(2)}, u32[]{:S(2)}) collective-permute-start(bf16[16,128]{1,0:T(8,128)(2,1)S(1)} %pad_maximum_fusion.1), channel_id=1, source_target_pairs={{0,8},{4,12},{8,0},{12,4},{16,24},{20,28},{24,16},{28,20},{1,9},{5... | collective-permute-start | bytes 12296 | tf_op jit(solution)/shard_map/ppermute | solution.py:21
  37.9 0.4 collective-permute-start.11
  38.3 2.7 %collective-permute-done.10 = bf16[16,128]{1,0:T(8,128)(2,1)S(1)} collective-permute-done((bf16[16,128]{1,0:T(8,128)(2,1)S(1)}, bf16[16,128]{1,0:T(8,128)(2,1)S(1)}, u32[]{:S(2)}, u32[]{:S(2)}) %collective-permute-start.10) | collective-permute-done | bytes 4128 | tf_op jit(solution)/shard_map/ppermute | solution.py:21
  41.0 0.5 %collective-permute-done.11 = bf16[16,128]{1,0:T(8,128)(2,1)S(1)} collective-permute-done((bf16[16,128]{1,0:T(8,128)(2,1)S(1)}, bf16[16,128]{1,0:T(8,128)(2,1)S(1)}, u32[]{:S(2)}, u32[]{:S(2)}) %collective-permute-start.11) | collective-permute-done | bytes 4128 | tf_op jit(solution)/shard_map/ppermute | solution.py:21
  41.6 0.8 %fusion = bf16[32,128]{1,0:T(8,128)(2,1)} fusion(bf16[8,4,128]{2,1,0:T(4,128)(2,1)S(1)} %slice.57, bf16[8,4,32]{2,1,0:T(4,128)(2,1)S(1)} %slice.56, f32[32]{0:T(128)S(1)} %iota_convert_fusion), kind=kOutput, calls=%fused_computation.1 | convolution fusion | flops 268288 | bytes 18560 | tf_op jit(solution)/shard_map/dot_general | solution.py:327
  (36 shorter events, 0.3 us)
Async XLA Ops:
  0.0 13.3 %copy-start = (bf16[128,512]{1,0:T(8,128)(2,1)S(1)}, bf16[128,512]{1,0:T(8,128)(2,1)}, u32[]{:S(2)}) copy-start(bf16[128,512]{1,0:T(8,128)(2,1)} %param.11) | copy-start | bytes 393220
  0.0 22.9 %copy-start.2 = (s32[1,32]{1,0:T(1,128)S(1)}, s32[1,32]{1,0:T(1,128)}, u32[]{:S(2)}) copy-start(s32[1,32]{1,0:T(1,128)} %param.12) | copy-start | bytes 388
  0.0 22.9 %copy-start.1 = (s32[1,32]{1,0:T(1,128)S(1)}, s32[1,32]{1,0:T(1,128)}, u32[]{:S(2)}) copy-start(s32[1,32]{1,0:T(1,128)} %param.13) | copy-start | bytes 388
  7.6 10.8 %collective-permute-start = (bf16[128,256]{1,0:T(8,128)(2,1)S(1)}, bf16[128,256]{1,0:T(8,128)(2,1)S(1)}, u32[]{:S(2)}, u32[]{:S(2)}) collective-permute-start(bf16[128,256]{1,0:T(8,128)(2,1)S(1)} %get-tuple-element.25), channel_id=1, source_target_pairs={{0,3},{1,2},{2,1},{3,0},{4,7},{5,6},{6,5},{7,4},{8,11},{9,10},{10,... | collective-permute-start | bytes 196616 | tf_op jit(solution)/shard_map/ppermute | solution.py:21
  12.7 5.6 %collective-permute-start.1 = (bf16[128,256]{1,0:T(8,128)(2,1)S(1)}, bf16[128,256]{1,0:T(8,128)(2,1)S(1)}, u32[]{:S(2)}, u32[]{:S(2)}) collective-permute-start(bf16[128,256]{1,0:T(8,128)(2,1)S(1)} %get-tuple-element.27), channel_id=1, source_target_pairs={{0,2},{1,3},{2,0},{3,1},{4,6},{5,7},{6,4},{7,5},{8,10},{9,11},{10,... | collective-permute-start | bytes 196616 | tf_op jit(solution)/shard_map/ppermute | solution.py:21
  12.7 5.6 %collective-permute-start.2 = (bf16[128,256]{1,0:T(8,128)(2,1)S(1)}, bf16[128,256]{1,0:T(8,128)(2,1)S(1)}, u32[]{:S(2)}, u32[]{:S(2)}) collective-permute-start(bf16[128,256]{1,0:T(8,128)(2,1)S(1)} %get-tuple-element.26), channel_id=1, source_target_pairs={{0,1},{1,0},{2,3},{3,2},{4,5},{5,4},{6,7},{7,6},{8,9},{9,8},{10,11... | collective-permute-start | bytes 196616 | tf_op jit(solution)/shard_map/ppermute | solution.py:21
  13.3 9.8 %collective-permute-start.6 = (bf16[128,512]{1,0:T(8,128)(2,1)S(1)}, bf16[128,512]{1,0:T(8,128)(2,1)S(1)}, u32[]{:S(2)}, u32[]{:S(2)}) collective-permute-start(bf16[128,512]{1,0:T(8,128)(2,1)S(1)} %copy-done), channel_id=1, source_target_pairs={{0,8},{4,12},{8,0},{12,4},{16,24},{20,28},{24,16},{28,20},{1,9},{5... | collective-permute-start | bytes 393224 | tf_op jit(solution)/shard_map/ppermute | solution.py:21
  18.4 12.4 %collective-permute-start.3 = (bf16[128,256]{1,0:T(8,128)(2,1)S(1)}, bf16[128,256]{1,0:T(8,128)(2,1)S(1)}, u32[]{:S(2)}, u32[]{:S(2)}) collective-permute-start(bf16[128,256]{1,0:T(8,128)(2,1)S(1)} %add_convert_fusion.refs_0_), channel_id=1, source_target_pairs={{0,2},{1,3},{2,0},{3,1},{4,6},{5,7},{6,4},{7,5},{8,10},{9,11},{10,... | collective-permute-start | bytes 196616 | tf_op jit(solution)/shard_map/ppermute | solution.py:21
  20.6 10.7 %collective-permute-start.4 = (bf16[128,256]{1,0:T(8,128)(2,1)S(1)}, bf16[128,256]{1,0:T(8,128)(2,1)S(1)}, u32[]{:S(2)}, u32[]{:S(2)}) collective-permute-start(bf16[128,256]{1,0:T(8,128)(2,1)S(1)} %add_convert_fusion.refs_0_), channel_id=1, source_target_pairs={{0,1},{1,0},{2,3},{3,2},{4,5},{5,4},{6,7},{7,6},{8,9},{9,8},{10,11... | collective-permute-start | bytes 196616 | tf_op jit(solution)/shard_map/ppermute | solution.py:21
  22.6 8.7 %collective-permute-start.5 = (bf16[128,256]{1,0:T(8,128)(2,1)S(1)}, bf16[128,256]{1,0:T(8,128)(2,1)S(1)}, u32[]{:S(2)}, u32[]{:S(2)}) collective-permute-start(bf16[128,256]{1,0:T(8,128)(2,1)S(1)} %add_convert_fusion.refs_0_), channel_id=1, source_target_pairs={{0,3},{1,2},{2,1},{3,0},{4,7},{5,6},{6,5},{7,4},{8,11},{9,10},{10,... | collective-permute-start | bytes 196616 | tf_op jit(solution)/shard_map/ppermute | solution.py:21
  23.2 7.0 %collective-permute-start.7 = (bf16[128,1024]{1,0:T(8,128)(2,1)S(1)}, bf16[128,1024]{1,0:T(8,128)(2,1)S(1)}, u32[]{:S(2)}, u32[]{:S(2)}) collective-permute-start(bf16[128,1024]{1,0:T(8,128)(2,1)S(1)} %pad_maximum_fusion), channel_id=1, source_target_pairs={{0,16},{4,20},{8,24},{12,28},{16,0},{20,4},{24,8},{28,12},{1,17},{... | collective-permute-start | bytes 786440 | tf_op jit(solution)/shard_map/ppermute | solution.py:21
  30.2 2.0 %collective-permute-start.8 = (bf16[128,2048]{1,0:T(8,128)(2,1)S(1)}, bf16[128,2048]{1,0:T(8,128)(2,1)S(1)}, u32[]{:S(2)}, u32[]{:S(2)}) collective-permute-start(bf16[128,2048]{1,0:T(8,128)(2,1)S(1)} %constant_dynamic-update-slice_fusion.refs_2_), channel_id=1, source_target_pairs={{0,4},{4,0},{8,12},{12,8},{16,20},{20,16},{24,28},{28,24},{1,5},{5... | collective-permute-start | bytes 1572872 | tf_op jit(solution)/shard_map/ppermute | solution.py:21
  33.6 1.2 %collective-permute-start.9 = (bf16[32,128]{1,0:T(8,128)(2,1)S(1)}, bf16[32,128]{1,0:T(8,128)(2,1)S(1)}, u32[]{:S(2)}, u32[]{:S(2)}) collective-permute-start(bf16[32,128]{1,0:T(8,128)(2,1)S(1)} %get-tuple-element.22), channel_id=1, source_target_pairs={{0,4},{4,0},{8,12},{12,8},{16,20},{20,16},{24,28},{28,24},{1,5},{5... | collective-permute-start | bytes 24584 | tf_op jit(solution)/shard_map/ppermute | solution.py:21
  34.8 6.7 %collective-permute-start.12 = (bf16[16,128]{1,0:T(8,128)(2,1)S(1)}, bf16[16,128]{1,0:T(8,128)(2,1)S(1)}, u32[]{:S(2)}, u32[]{:S(2)}) collective-permute-start(bf16[16,128]{1,0:T(8,128)(2,1)S(1)} %pad_maximum_fusion.3), channel_id=1, source_target_pairs={{0,24},{4,28},{8,16},{12,20},{16,8},{20,12},{24,0},{28,4},{1,25},{... | collective-permute-start | bytes 12296 | tf_op jit(solution)/shard_map/ppermute | solution.py:21
  37.4 3.6 %collective-permute-start.10 = (bf16[16,128]{1,0:T(8,128)(2,1)S(1)}, bf16[16,128]{1,0:T(8,128)(2,1)S(1)}, u32[]{:S(2)}, u32[]{:S(2)}) collective-permute-start(bf16[16,128]{1,0:T(8,128)(2,1)S(1)} %pad_maximum_fusion.1), channel_id=1, source_target_pairs={{0,8},{4,12},{8,0},{12,4},{16,24},{20,28},{24,16},{28,20},{1,9},{5... | collective-permute-start | bytes 12296 | tf_op jit(solution)/shard_map/ppermute | solution.py:21
  37.9 3.6 %collective-permute-start.11 = (bf16[16,128]{1,0:T(8,128)(2,1)S(1)}, bf16[16,128]{1,0:T(8,128)(2,1)S(1)}, u32[]{:S(2)}, u32[]{:S(2)}) collective-permute-start(bf16[16,128]{1,0:T(8,128)(2,1)S(1)} %pad_maximum_fusion.2), channel_id=1, source_target_pairs={{0,16},{4,20},{8,24},{12,28},{16,0},{20,4},{24,8},{28,12},{1,17},{... | collective-permute-start | bytes 12296 | tf_op jit(solution)/shard_map/ppermute | solution.py:21

commit v7 on v6

--- a/solution.py
+++ b/solution.py
@@ -28,8 +28,9 @@
 
 
 def peers_kernel(
-    ahead, act_hbm, grad_hbm, wa_hbm, wg_hbm, out_ref, grad_own, wa, wg, act, grad, sem, wsem
+    ahead, act_hbm, grad_hbm, wa_hbm, wg_hbm, *refs
 ):
+    *outs, grad_own, wa, wg, act, grad, sem, wsem = refs
     count, rows = act.shape[0], act.shape[1]
     part = lax.axis_index("tensor")
 
@@ -80,7 +81,13 @@
         def _():
             own.start()
 
-        out_ref[i] = both_projections(act[i], grad[i], wa[...], wg[...])
+        both = both_projections(act[i], grad[i], wa[...], wg[...])
+        for j, ref in enumerate(outs):
+
+            @pl.when(i == j)
+            def _(ref=ref):
+                ref[...] = both
+
         return carry
 
     lax.fori_loop(0, count, step, 0)
@@ -92,13 +99,13 @@
     rows, count = tokens // parts, parts - 1
     hbm, vmem = pl.BlockSpec(memory_space=pl.ANY), pl.BlockSpec(memory_space=pltpu.VMEM)
     return pl.pallas_call(
-        functools.partial(peers_kernel, min(2, count)),
+        functools.partial(peers_kernel, min(3, count)),
         out_shape=[
             jax.ShapeDtypeStruct(shape, BF16)
-            for shape in ((count, 2 * k, rows), (rows, d), (k, ff), (k, d))
+            for shape in [(2 * k, rows)] * count + [(rows, d), (k, ff), (k, d)]
         ],
         in_specs=[hbm] * 4,
-        out_specs=[vmem] * 4,
+        out_specs=[vmem] * (count + 3),
         scratch_shapes=[
             pltpu.VMEM((count, rows, ff), BF16),
             pltpu.VMEM((count, rows, d), BF16),
@@ -220,9 +227,8 @@
         for i in range(block * per_block, (block + 1) * per_block, 2):
             at = pl.ds(base + (i - block * per_block) * k, lanes)
             for m in range(outer.shape[0]):
-                scale = scale_ref[:, m * lanes : (m + 1) * lanes]
-                even = outer[m, i * low : (i + 1) * low, :] * scale
-                odd = outer[m, (i + 1) * low : (i + 2) * low, :] * scale
+                even = outer[m, i * low : (i + 1) * low, :]
+                odd = outer[m, (i + 1) * low : (i + 2) * low, :]
                 pair = [
                     jnp.where(first, even, pltpu.roll(odd, k, 1)),
                     jnp.where(first, pltpu.roll(even, k, 1), odd),
@@ -238,7 +244,7 @@
         for h, ref in enumerate(held)
     )
     packed = lax.dot_general(
-        select_ref[...], local.astype(BF16), NT, preferred_element_type=F32
+        select_ref[...], (local * scale_ref[...]).astype(BF16), NT, preferred_element_type=F32
     )
     packed = (packed + labels_ref[...]).astype(BF16)
     near_ref[...], far_ref[...] = packed[: near_ref.shape[0]], packed[near_ref.shape[0] :]
@@ -279,7 +285,8 @@
 
     wa, wg = proj_in.T, proj_out.T
     peers = list(range(parts - 1, 0, -1))
-    sent, *kept = project_peers(parts, activations, out_grads, wa, wg)
+    made = project_peers(parts, activations, out_grads, wa, wg)
+    sent, kept = made[: parts - 1], made[parts - 1 :]
     got = [swap(sent[i], "tensor", peer) for i, peer in enumerate(peers)]
     total = project_own(activations, *kept, 2).astype(F32)
     for piece in got:
@@ -292,8 +299,7 @@
     starts = jnp.sum(jnp.where(indices[:, None] < indices[None, :], lengths[:, None], 0), axis=0)
     low = maxdoc // 4
     ends = jnp.broadcast_to((starts + lengths)[:, None], (maxdoc, 128))
-    scaling = 1.0 / jnp.sqrt(jnp.maximum(lengths, 1).astype(F32))
-    scale = jnp.repeat(scaling.reshape(4, low).T, proj_in.shape[1], axis=1)
+    scale = (1.0 / jnp.sqrt(jnp.maximum(lengths, 1).astype(F32)))[None, :]
 
     per_owner = max(1, maxdoc // devices)
     height = -(-2 * per_owner // 8) * 8

time: 42.5 us -> 42.5 us (level)
  transfers between devices with their start and end apart: 13 -> 13, of which waited for: 5 -> 5; matrix products, arithmetic and copies ran while one was open for 2% -> 1% of each run, Pallas kernels for 9% -> 9%
where the time goes in v7:
time: 42.5 us; the launch traced here: 42.4 us
  starting transfers between devices  17.2 us (40%)
  Pallas kernels  12.6 us (30%)
  waiting for transfers between devices  10.9 us (26%)
  matrix products  0.79 us (2%)
  other arithmetic  0.48 us (1%)
    ppermute x13, starting transfers between devices, swap(): lax.ppermute(x, axis, [(i, i ^ k) for i in range(lax.axis_size(axis))])  17.2 us
    ppermute x13, waiting for transfers between devices, swap(): lax.ppermute(x, axis, [(i, i ^ k) for i in range(lax.axis_size(axis))])  10.9 us
    pallas_call x1, Pallas kernels, project_peers(): pl.pallas_call(functools.partial(peers_kernel, min(3, count)), out_shape=...  7.53 us
    pallas_call x1, Pallas kernels, project_own(): pl.pallas_call(own_kernel, out_shape=jax.ShapeDtypeStruct((2 * k, rows),...  3.31 us
    pallas_call x1, Pallas kernels, score(): pl.pallas_call(functools.partial(score_kernel, offsets, low, n_blocks), o...  1.32 us
  transfers between devices with their start and end apart: 13, of which 5 were waited for; matrix products, arithmetic and copies ran while one was open for 1% of the time, Pallas kernels for 9%

profile of v7, /device:TPU:0, one launch (start us, length us, event | category | flops | bytes accessed | tf_op | source)
XLA Modules:
  0.0 42.4 jit_solution(13219454955802629777)
XLA Ops:
  0.0 7.5 %project_peers.1 = (bf16[128,256]{1,0:T(8,128)(2,1)S(1)}, bf16[128,256]{1,0:T(8,128)(2,1)S(1)}, bf16[128,256]{1,0:T(8,128)(2,1)S(1)}, bf16[256,2048]{1,0:T(8,128...) custom-call(bf16[1024,7168]{1,0:T(8,128)(2,1)} %act_hbm.3, bf16[1024,2048]{1,0:T(8,128)(2,1)} %grad_hbm.1, ...), custom_call_target="tpu_custom_call" | custom-call | flops 1207959552 | bytes 18874368 | tf_op jit(solution)/shard_map/project_peers/pallas_call | solution.py:101
  7.5 5.1 %collective-permute-start = (bf16[128,256]{1,0:T(8,128)(2,1)S(1)}, bf16[128,256]{1,0:T(8,128)(2,1)S(1)}, u32[]{:S(2)}, u32[]{:S(2)}) collective-permute-start(bf16[128,256]{1,0:T(8,128)(2,1)S(1)} %get-tuple-element.19), channel_id=1, source_target_pairs={{0,3},{1,2},{2,1},{3,0},{4,7},{5,6},{6,5},{7,4},{8,11},{9,10},{10,... | collective-permute-start | bytes 196616 | tf_op jit(solution)/shard_map/ppermute | solution.py:21
  12.7 0.0 collective-permute-start.1
  12.7 0.6 %collective-permute-start.2 = (bf16[128,256]{1,0:T(8,128)(2,1)S(1)}, bf16[128,256]{1,0:T(8,128)(2,1)S(1)}, u32[]{:S(2)}, u32[]{:S(2)}) collective-permute-start(bf16[128,256]{1,0:T(8,128)(2,1)S(1)} %get-tuple-element.21), channel_id=1, source_target_pairs={{0,1},{1,0},{2,3},{3,2},{4,5},{5,4},{6,7},{7,6},{8,9},{9,8},{10,11... | collective-permute-start | bytes 196616 | tf_op jit(solution)/shard_map/ppermute | solution.py:21
  13.3 1.6 %collective-permute-start.6 = (bf16[128,512]{1,0:T(8,128)(2,1)S(1)}, bf16[128,512]{1,0:T(8,128)(2,1)S(1)}, u32[]{:S(2)}, u32[]{:S(2)}) collective-permute-start(bf16[128,512]{1,0:T(8,128)(2,1)S(1)} %copy-done), channel_id=1, source_target_pairs={{0,8},{4,12},{8,0},{12,4},{16,24},{20,28},{24,16},{28,20},{1,9},{5... | collective-permute-start | bytes 393224 | tf_op jit(solution)/shard_map/ppermute | solution.py:21
  15.0 3.3 %project_own.1 = bf16[128,256]{1,0:T(8,128)(2,1)S(1)} custom-call(bf16[1024,7168]{1,0:T(8,128)(2,1)} %act_hbm.3, bf16[256,2048]{1,0:T(8,128)(2,1)S(1)} %get-tuple-element.16.grad_ref, bf16[64,7168]{1,0:T(8,128)(2,1)S(1)} %get-tuple-element.17.wa_ref, bf16[64,2048]{1,0:T(8,128)(2,1)S(1)} %get-tuple-element.18.wg_ref), custom_call_target="tpu_custom_call" | custom-call | flops 301989888 | bytes 4718592 | tf_op jit(solution)/shard_map/project_own/pallas_call | solution.py:146
  18.3 0.0 collective-permute-done
  18.3 0.0 collective-permute-done.2
  18.4 2.2 %collective-permute-start.3 = (bf16[128,256]{1,0:T(8,128)(2,1)S(1)}, bf16[128,256]{1,0:T(8,128)(2,1)S(1)}, u32[]{:S(2)}, u32[]{:S(2)}) collective-permute-start(bf16[128,256]{1,0:T(8,128)(2,1)S(1)} %add_convert_fusion.refs_0_), channel_id=1, source_target_pairs={{0,2},{1,3},{2,0},{3,1},{4,6},{5,7},{6,4},{7,5},{8,10},{9,11},{10,... | collective-permute-start | bytes 196616 | tf_op jit(solution)/shard_map/ppermute | solution.py:21
  20.6 2.0 %collective-permute-start.4 = (bf16[128,256]{1,0:T(8,128)(2,1)S(1)}, bf16[128,256]{1,0:T(8,128)(2,1)S(1)}, u32[]{:S(2)}, u32[]{:S(2)}) collective-permute-start(bf16[128,256]{1,0:T(8,128)(2,1)S(1)} %add_convert_fusion.refs_0_), channel_id=1, source_target_pairs={{0,1},{1,0},{2,3},{3,2},{4,5},{5,4},{6,7},{7,6},{8,9},{9,8},{10,11... | collective-permute-start | bytes 196616 | tf_op jit(solution)/shard_map/ppermute | solution.py:21
  22.6 0.2 collective-permute-start.5
  22.8 0.1 select_reduce_fusion.1
  22.9 0.2 convert_reduce_fusion
  23.2 1.6 %collective-permute-start.7 = (bf16[128,1024]{1,0:T(8,128)(2,1)S(1)}, bf16[128,1024]{1,0:T(8,128)(2,1)S(1)}, u32[]{:S(2)}, u32[]{:S(2)}) collective-permute-start(bf16[128,1024]{1,0:T(8,128)(2,1)S(1)} %pad_maximum_fusion), channel_id=1, source_target_pairs={{0,16},{4,20},{8,24},{12,28},{16,0},{20,4},{24,8},{28,12},{1,17},{... | collective-permute-start | bytes 786440 | tf_op jit(solution)/shard_map/ppermute | solution.py:21
  24.8 5.4 %collective-permute-done.7 = bf16[128,1024]{1,0:T(8,128)(2,1)S(1)} collective-permute-done((bf16[128,1024]{1,0:T(8,128)(2,1)S(1)}, bf16[128,1024]{1,0:T(8,128)(2,1)S(1)}, u32[]{:S(2)}, u32[]{:S(2)}) %collective-permute-start.7) | collective-permute-done | bytes 262176 | tf_op jit(solution)/shard_map/ppermute | solution.py:21
  30.2 0.1 collective-permute-start.8
  30.3 0.1 select_reduce_fusion
  30.5 0.1 broadcast_in_dim.30.ends_ref
  30.5 0.4 %early_sums.1.early_ref = f32[512,256]{1,0:T(8,128)S(1)} custom-call(s32[32,128]{1,0:T(8,128)S(1)} %broadcast_in_dim.30.ends_ref, bf16[128,256]{1,0:T(8,128)(2,1)S(1)} %add_convert_fusion.refs_0_, bf16[128,256]{1,0:T(8,128)(2,1)S(1)} %collective-permute-done.3.refs_1_), custom_call_target="tpu_custom_call" | custom-call | tf_op jit(solution)/shard_map/early_sums/pallas_call | solution.py:201
  31.0 0.0 collective-permute-done.5.refs_1_
  31.0 1.2 %collective-permute-done.8.refs_3_ = bf16[128,2048]{1,0:T(8,128)(2,1)S(1)} collective-permute-done((bf16[128,2048]{1,0:T(8,128)(2,1)S(1)}, bf16[128,2048]{1,0:T(8,128)(2,1)S(1)}, u32[]{:S(2)}, u32[]{:S(2)}) %collective-permute-start.8) | collective-permute-done | bytes 524320 | tf_op jit(solution)/shard_map/ppermute | solution.py:21
  32.2 0.1 broadcast_in_dim.38.labels_ref
  32.3 1.3 %score.1 = (bf16[32,128]{1,0:T(8,128)(2,1)S(1)}, bf16[32,128]{1,0:T(8,128)(2,1)S(1)}) custom-call(s32[32,128]{1,0:T(8,128)S(1)} %broadcast_in_dim.30.ends_ref, f32[1,32]{1,0:T(1,128)S(1)} %rsqrt_bitcast_fusion.scale_ref, bf16[64,32]{1,0:T(8,128)(2,1)S(1)} %fusion.1.select_ref, f32[64,128]{1,0:T(8,128)S(1)} %broadcast_in_dim.38.labels_ref, ...), custom_call_target="tpu_custom_call" | custom-call | flops 167772160 | bytes 1048576 | tf_op jit(solution)/shard_map/score/pallas_call | solution.py:258
  33.6 0.2 collective-permute-start.9
  33.8 1.0 %collective-permute-done.9 = bf16[32,128]{1,0:T(8,128)(2,1)S(1)} collective-permute-done((bf16[32,128]{1,0:T(8,128)(2,1)S(1)}, bf16[32,128]{1,0:T(8,128)(2,1)S(1)}, u32[]{:S(2)}, u32[]{:S(2)}) %collective-permute-start.9) | collective-permute-done | bytes 8224 | tf_op jit(solution)/shard_map/ppermute | solution.py:21
  34.8 2.6 %collective-permute-start.12 = (bf16[16,128]{1,0:T(8,128)(2,1)S(1)}, bf16[16,128]{1,0:T(8,128)(2,1)S(1)}, u32[]{:S(2)}, u32[]{:S(2)}) collective-permute-start(bf16[16,128]{1,0:T(8,128)(2,1)S(1)} %pad_maximum_fusion.3), channel_id=1, source_target_pairs={{0,24},{4,28},{8,16},{12,20},{16,8},{20,12},{24,0},{28,4},{1,25},{... | collective-permute-start | bytes 12296 | tf_op jit(solution)/shard_map/ppermute | solution.py:21
  37.4 0.5 %collective-permute-start.10 = (bf16[16,128]{1,0:T(8,128)(2,1)S(1)}, bf16[16,128]{1,0:T(8,128)(2,1)S(1)}, u32[]{:S(2)}, u32[]{:S(2)}) collective-permute-start(bf16[16,128]{1,0:T(8,128)(2,1)S(1)} %pad_maximum_fusion.1), channel_id=1, source_target_pairs={{0,8},{4,12},{8,0},{12,4},{16,24},{20,28},{24,16},{28,20},{1,9},{5... | collective-permute-start | bytes 12296 | tf_op jit(solution)/shard_map/ppermute | solution.py:21
  37.9 0.4 collective-permute-start.11
  38.3 2.7 %collective-permute-done.10 = bf16[16,128]{1,0:T(8,128)(2,1)S(1)} collective-permute-done((bf16[16,128]{1,0:T(8,128)(2,1)S(1)}, bf16[16,128]{1,0:T(8,128)(2,1)S(1)}, u32[]{:S(2)}, u32[]{:S(2)}) %collective-permute-start.10) | collective-permute-done | bytes 4128 | tf_op jit(solution)/shard_map/ppermute | solution.py:21
  41.0 0.5 %collective-permute-done.11 = bf16[16,128]{1,0:T(8,128)(2,1)S(1)} collective-permute-done((bf16[16,128]{1,0:T(8,128)(2,1)S(1)}, bf16[16,128]{1,0:T(8,128)(2,1)S(1)}, u32[]{:S(2)}, u32[]{:S(2)}) %collective-permute-start.11) | collective-permute-done | bytes 4128 | tf_op jit(solution)/shard_map/ppermute | solution.py:21
  41.6 0.0 collective-permute-done.12
  41.6 0.8 %fusion = bf16[32,128]{1,0:T(8,128)(2,1)} fusion(bf16[8,4,128]{2,1,0:T(4,128)(2,1)S(1)} %slice.45, bf16[8,4,32]{2,1,0:T(4,128)(2,1)S(1)} %slice.44, f32[32]{0:T(128)S(1)} %iota_convert_fusion), kind=kOutput, calls=%fused_computation.1 | convolution fusion | flops 268288 | bytes 18560 | tf_op jit(solution)/shard_map/dot_general | solution.py:333
  (31 shorter events, 0.2 us)
Async XLA Ops:
  0.0 13.3 %copy-start = (bf16[128,512]{1,0:T(8,128)(2,1)S(1)}, bf16[128,512]{1,0:T(8,128)(2,1)}, u32[]{:S(2)}) copy-start(bf16[128,512]{1,0:T(8,128)(2,1)} %param.11) | copy-start | bytes 393220
  0.0 22.8 %copy-start.2 = (s32[1,32]{1,0:T(1,128)S(1)}, s32[1,32]{1,0:T(1,128)}, u32[]{:S(2)}) copy-start(s32[1,32]{1,0:T(1,128)} %param.12) | copy-start | bytes 388
  0.0 22.9 %copy-start.1 = (s32[1,32]{1,0:T(1,128)S(1)}, s32[1,32]{1,0:T(1,128)}, u32[]{:S(2)}) copy-start(s32[1,32]{1,0:T(1,128)} %param.13) | copy-start | bytes 388
  7.5 10.8 %collective-permute-start = (bf16[128,256]{1,0:T(8,128)(2,1)S(1)}, bf16[128,256]{1,0:T(8,128)(2,1)S(1)}, u32[]{:S(2)}, u32[]{:S(2)}) collective-permute-start(bf16[128,256]{1,0:T(8,128)(2,1)S(1)} %get-tuple-element.19), channel_id=1, source_target_pairs={{0,3},{1,2},{2,1},{3,0},{4,7},{5,6},{6,5},{7,4},{8,11},{9,10},{10,... | collective-permute-start | bytes 196616 | tf_op jit(solution)/shard_map/ppermute | solution.py:21
  12.7 5.6 %collective-permute-start.1 = (bf16[128,256]{1,0:T(8,128)(2,1)S(1)}, bf16[128,256]{1,0:T(8,128)(2,1)S(1)}, u32[]{:S(2)}, u32[]{:S(2)}) collective-permute-start(bf16[128,256]{1,0:T(8,128)(2,1)S(1)} %get-tuple-element.20), channel_id=1, source_target_pairs={{0,2},{1,3},{2,0},{3,1},{4,6},{5,7},{6,4},{7,5},{8,10},{9,11},{10,... | collective-permute-start | bytes 196616 | tf_op jit(solution)/shard_map/ppermute | solution.py:21
  12.7 5.6 %collective-permute-start.2 = (bf16[128,256]{1,0:T(8,128)(2,1)S(1)}, bf16[128,256]{1,0:T(8,128)(2,1)S(1)}, u32[]{:S(2)}, u32[]{:S(2)}) collective-permute-start(bf16[128,256]{1,0:T(8,128)(2,1)S(1)} %get-tuple-element.21), channel_id=1, source_target_pairs={{0,1},{1,0},{2,3},{3,2},{4,5},{5,4},{6,7},{7,6},{8,9},{9,8},{10,11... | collective-permute-start | bytes 196616 | tf_op jit(solution)/shard_map/ppermute | solution.py:21
  13.3 9.8 %collective-permute-start.6 = (bf16[128,512]{1,0:T(8,128)(2,1)S(1)}, bf16[128,512]{1,0:T(8,128)(2,1)S(1)}, u32[]{:S(2)}, u32[]{:S(2)}) collective-permute-start(bf16[128,512]{1,0:T(8,128)(2,1)S(1)} %copy-done), channel_id=1, source_target_pairs={{0,8},{4,12},{8,0},{12,4},{16,24},{20,28},{24,16},{28,20},{1,9},{5... | collective-permute-start | bytes 393224 | tf_op jit(solution)/shard_map/ppermute | solution.py:21
  18.4 12.1 %collective-permute-start.3 = (bf16[128,256]{1,0:T(8,128)(2,1)S(1)}, bf16[128,256]{1,0:T(8,128)(2,1)S(1)}, u32[]{:S(2)}, u32[]{:S(2)}) collective-permute-start(bf16[128,256]{1,0:T(8,128)(2,1)S(1)} %add_convert_fusion.refs_0_), channel_id=1, source_target_pairs={{0,2},{1,3},{2,0},{3,1},{4,6},{5,7},{6,4},{7,5},{8,10},{9,11},{10,... | collective-permute-start | bytes 196616 | tf_op jit(solution)/shard_map/ppermute | solution.py:21
  20.6 10.4 %collective-permute-start.4 = (bf16[128,256]{1,0:T(8,128)(2,1)S(1)}, bf16[128,256]{1,0:T(8,128)(2,1)S(1)}, u32[]{:S(2)}, u32[]{:S(2)}) collective-permute-start(bf16[128,256]{1,0:T(8,128)(2,1)S(1)} %add_convert_fusion.refs_0_), channel_id=1, source_target_pairs={{0,1},{1,0},{2,3},{3,2},{4,5},{5,4},{6,7},{7,6},{8,9},{9,8},{10,11... | collective-permute-start | bytes 196616 | tf_op jit(solution)/shard_map/ppermute | solution.py:21
  22.6 8.4 %collective-permute-start.5 = (bf16[128,256]{1,0:T(8,128)(2,1)S(1)}, bf16[128,256]{1,0:T(8,128)(2,1)S(1)}, u32[]{:S(2)}, u32[]{:S(2)}) collective-permute-start(bf16[128,256]{1,0:T(8,128)(2,1)S(1)} %add_convert_fusion.refs_0_), channel_id=1, source_target_pairs={{0,3},{1,2},{2,1},{3,0},{4,7},{5,6},{6,5},{7,4},{8,11},{9,10},{10,... | collective-permute-start | bytes 196616 | tf_op jit(solution)/shard_map/ppermute | solution.py:21
  23.2 7.0 %collective-permute-start.7 = (bf16[128,1024]{1,0:T(8,128)(2,1)S(1)}, bf16[128,1024]{1,0:T(8,128)(2,1)S(1)}, u32[]{:S(2)}, u32[]{:S(2)}) collective-permute-start(bf16[128,1024]{1,0:T(8,128)(2,1)S(1)} %pad_maximum_fusion), channel_id=1, source_target_pairs={{0,16},{4,20},{8,24},{12,28},{16,0},{20,4},{24,8},{28,12},{1,17},{... | collective-permute-start | bytes 786440 | tf_op jit(solution)/shard_map/ppermute | solution.py:21
  30.2 2.0 %collective-permute-start.8 = (bf16[128,2048]{1,0:T(8,128)(2,1)S(1)}, bf16[128,2048]{1,0:T(8,128)(2,1)S(1)}, u32[]{:S(2)}, u32[]{:S(2)}) collective-permute-start(bf16[128,2048]{1,0:T(8,128)(2,1)S(1)} %constant_dynamic-update-slice_fusion.refs_2_), channel_id=1, source_target_pairs={{0,4},{4,0},{8,12},{12,8},{16,20},{20,16},{24,28},{28,24},{1,5},{5... | collective-permute-start | bytes 1572872 | tf_op jit(solution)/shard_map/ppermute | solution.py:21
  33.6 1.2 %collective-permute-start.9 = (bf16[32,128]{1,0:T(8,128)(2,1)S(1)}, bf16[32,128]{1,0:T(8,128)(2,1)S(1)}, u32[]{:S(2)}, u32[]{:S(2)}) collective-permute-start(bf16[32,128]{1,0:T(8,128)(2,1)S(1)} %get-tuple-element.26), channel_id=1, source_target_pairs={{0,4},{4,0},{8,12},{12,8},{16,20},{20,16},{24,28},{28,24},{1,5},{5... | collective-permute-start | bytes 24584 | tf_op jit(solution)/shard_map/ppermute | solution.py:21
  34.8 6.7 %collective-permute-start.12 = (bf16[16,128]{1,0:T(8,128)(2,1)S(1)}, bf16[16,128]{1,0:T(8,128)(2,1)S(1)}, u32[]{:S(2)}, u32[]{:S(2)}) collective-permute-start(bf16[16,128]{1,0:T(8,128)(2,1)S(1)} %pad_maximum_fusion.3), channel_id=1, source_target_pairs={{0,24},{4,28},{8,16},{12,20},{16,8},{20,12},{24,0},{28,4},{1,25},{... | collective-permute-start | bytes 12296 | tf_op jit(solution)/shard_map/ppermute | solution.py:21
  37.4 3.6 %collective-permute-start.10 = (bf16[16,128]{1,0:T(8,128)(2,1)S(1)}, bf16[16,128]{1,0:T(8,128)(2,1)S(1)}, u32[]{:S(2)}, u32[]{:S(2)}) collective-permute-start(bf16[16,128]{1,0:T(8,128)(2,1)S(1)} %pad_maximum_fusion.1), channel_id=1, source_target_pairs={{0,8},{4,12},{8,0},{12,4},{16,24},{20,28},{24,16},{28,20},{1,9},{5... | collective-permute-start | bytes 12296 | tf_op jit(solution)/shard_map/ppermute | solution.py:21
  37.9 3.6 %collective-permute-start.11 = (bf16[16,128]{1,0:T(8,128)(2,1)S(1)}, bf16[16,128]{1,0:T(8,128)(2,1)S(1)}, u32[]{:S(2)}, u32[]{:S(2)}) collective-permute-start(bf16[16,128]{1,0:T(8,128)(2,1)S(1)} %pad_maximum_fusion.2), channel_id=1, source_target_pairs={{0,16},{4,20},{8,24},{12,28},{16,0},{20,4},{24,8},{28,12},{1,17},{... | collective-permute-start | bytes 12296 | tf_op jit(solution)/shard_map/ppermute | solution.py:21
